TPU v7x, 32 devices: a whole 2x2x4 slice. The times are simulated.
32 devices in a mesh: dp: 8 (over y, x, core), mp: 4 (over z).
Axes of the slice: x: 2, y: 2, z: 4, core: 2. Of those that a mesh axis runs over, the one named last changes fastest.
Arguments:
- tokens: bfloat16 [32768, 1024], P('dp', 'mp'), may hold values from -6 to 6
- cotangent: bfloat16 [32768, 1024], P('dp', 'mp'), may hold values from -6 to 6
- norm_gain: float32 [1024], P('mp'), may hold values from 0.5 to 1.5
- ema_delta: float32 [1024, 16], P('mp'), may hold values from -4 to 2
- ema_alpha: float32 [1024, 16], P('mp'), may hold values from -1.5 to 2
- ema_beta: float32 [1024, 16], P('mp'), may hold values from -4 to 4
- ema_eta: float32 [1024, 16], P('mp'), may hold values from -1.5 to 1.5
- ema_omega: float32 [1024], P('mp'), may hold values from -4 to 4
- shared_proj: bfloat16 [1024, 128], replicated, may hold values from -0.1875 to 0.1875
- query_gain: float32 [128], replicated, may hold values from -8 to 8
- query_bias: float32 [128], replicated, may hold values from -4 to 4
- key_gain: float32 [128], replicated, may hold values from -8 to 8
- value_proj: bfloat16 [1024, 2048], P(None, 'mp'), may hold values from -0.1875 to 0.1875
- gate_proj: bfloat16 [1024, 2048], P(None, 'mp'), may hold values from -0.1875 to 0.1875
- mixer_proj: bfloat16 [1024, 1024], P(None, 'mp'), may hold values from -0.1875 to 0.1875
- update_proj: bfloat16 [1024, 1024], P(None, 'mp'), may hold values from -0.1875 to 0.1875
- output_proj: bfloat16 [2048, 1024], P('mp'), may hold values from -0.5 to 0.5
- ffn_gain: float32 [1024], P('mp'), may hold values from 0.5 to 1.5
- up_proj: bfloat16 [1024, 4096], P(None, 'mp'), may hold values from -0.1875 to 0.1875
- down_proj: bfloat16 [4096, 1024], P('mp'), may hold values from -0.09375 to 0.09375
Outputs:
- layer_out: bfloat16 [32768, 1024], P('dp', 'mp')
- token_grad: bfloat16 [32768, 1024], P('dp', 'mp')
- gain_grad: float32 [1024], P('mp')
- delta_grad: float32 [1024, 16], P('mp')
- alpha_grad: float32 [1024, 16], P('mp')
- beta_grad: float32 [1024, 16], P('mp')
- eta_grad: float32 [1024, 16], P('mp')
- omega_grad: float32 [1024], P('mp')
- shared_grad: float32 [1024, 128], replicated
- query_grad: float32 [128], replicated
- bias_grad: float32 [128], replicated
- key_grad: float32 [128], replicated
- value_grad: float32 [1024, 2048], P(None, 'mp')
- gate_grad: float32 [1024, 2048], P(None, 'mp')
- mixer_grad: float32 [1024, 1024], P(None, 'mp')
- update_grad: float32 [1024, 1024], P(None, 'mp')
- output_grad: float32 [2048, 1024], P('mp')
- ffn_grad: float32 [1024], P('mp')
- up_grad: float32 [1024, 4096], P(None, 'mp')
- down_grad: float32 [4096, 1024], P('mp')
All inputs are finite; a program needn't handle non-finite values.
Results may differ from a plain program's by a relative error of at most 0.0307.
Values may be sent and summed in bfloat16 or wider, within the bound.
A program may use at most 384 MiB of HBM per device.

v0:
```python
import jax
import jax.numpy as jnp
from jax import lax
from jax.sharding import PartitionSpec as P

D = 1024
GROUP = 128
LEN = 2048
MICRO = 2


EPS = 1e-05


def matmul(left, right):
    return jnp.dot(left, right, preferred_element_type=jnp.float32)


def matmul_tn(left, right):
    return lax.dot_general(
        left, right, (((0,), (0,)), ((), ())), preferred_element_type=jnp.float32
    )


def matmul_nt(left, right):
    return lax.dot_general(
        left, right, (((1,), (1,)), ((), ())), preferred_element_type=jnp.float32
    )


def silu_slope(values):
    logistic = jax.nn.sigmoid(values)
    return logistic * (1.0 + values * (1.0 - logistic))


def norm_forward(shard, gain):
    total, power = lax.psum((jnp.sum(shard, axis=1), jnp.sum(shard * shard, axis=1)), "mp")
    mean_row = total / D
    scale = lax.rsqrt(power / D - mean_row * mean_row + EPS)
    normed = (shard - mean_row[:, None]) * scale[:, None]
    return (normed, scale, (normed * gain).astype(jnp.bfloat16))


def norm_backward(grad, normed, scale, gain):
    gain_part = jnp.sum(grad * normed, axis=0)
    scaled = grad * gain
    first, second = lax.psum((jnp.sum(scaled, axis=1), jnp.sum(scaled * normed, axis=1)), "mp")
    back = scale[:, None] * (scaled - (first / D)[:, None] - normed * (second / D)[:, None])
    return (back, gain_part)


def ema_local(signal, delta, alpha, beta, eta):
    rate = jax.nn.sigmoid(delta)
    keep_log = jnp.log(1.0 - rate * jax.nn.sigmoid(alpha))
    push = rate * beta
    width = signal.shape[1]
    blocks = signal.reshape(-1, LEN // GROUP, GROUP, width)
    offsets = jnp.arange(GROUP, dtype=jnp.float32)
    powers = jnp.exp(offsets[:, None, None] * keep_log[None])
    kernel = jnp.sum(powers * (push * eta)[None], axis=2)
    lag = jnp.arange(GROUP)[:, None] - jnp.arange(GROUP)[None, :]
    toeplitz = jnp.where((lag >= 0)[:, :, None], jnp.take(kernel, jnp.maximum(lag, 0), axis=0), 0.0)
    inner = jnp.einsum("tsc,gbsc->gbtc", toeplitz, blocks, precision=lax.Precision.HIGHEST)
    tail = jnp.exp((GROUP - 1.0 - offsets)[:, None, None] * keep_log[None]) * push[None]
    ends = jnp.einsum("gbsc,scj->bgcj", blocks, tail, precision=lax.Precision.HIGHEST)
    carry_keep = jnp.exp(GROUP * keep_log)

    def advance(state, end_now):
        return (carry_keep * state + end_now, state)

    _, starts = lax.scan(advance, jnp.zeros(ends.shape[1:], jnp.float32), ends)
    lead = jnp.exp((offsets + 1.0)[:, None, None] * keep_log[None]) * eta[None]
    outer = jnp.einsum("tcj,bgcj->gbtc", lead, starts, precision=lax.Precision.HIGHEST)
    return (inner + outer).reshape(signal.shape)


def group_scores(query, keys):
    blocks = query.shape[0] // GROUP
    query_blocks = query.reshape(blocks, GROUP, query.shape[1])
    key_blocks = keys.reshape(blocks, GROUP, keys.shape[1])
    raw = jnp.einsum("nqz,nkz->nqk", query_blocks, key_blocks, preferred_element_type=jnp.float32)
    raw = raw * query.shape[1] ** (-0.5)
    place = jnp.arange(GROUP)
    return jnp.where((place[:, None] >= place[None, :])[None], raw, -1e30)


def local(
    tokens,
    cotangent,
    norm_gain,
    ema_delta,
    ema_alpha,
    ema_beta,
    ema_eta,
    ema_omega,
    shared_proj,
    query_gain,
    query_bias,
    key_gain,
    value_proj,
    gate_proj,
    mixer_proj,
    update_proj,
    output_proj,
    ffn_gain,
    up_proj,
    down_proj,
):
    width = tokens.shape[1]
    rows_micro = tokens.shape[0] // MICRO
    shared_rows = lax.dynamic_slice_in_dim(shared_proj, lax.axis_index("mp") * width, width, 0)
    head_scale = query_gain.shape[0] ** (-0.5)
    mixer_totals_list = tuple(
        (
            jnp.zeros(item.shape, jnp.float32)
            for item in (
                norm_gain,
                ema_delta,
                ema_alpha,
                ema_beta,
                ema_eta,
                ema_omega,
                shared_proj,
                query_gain,
                query_bias,
                key_gain,
                value_proj,
                gate_proj,
                mixer_proj,
                update_proj,
                output_proj,
            )
        )
    )
    ffn_sums = tuple(
        (jnp.zeros(item.shape, jnp.float32) for item in (ffn_gain, up_proj, down_proj))
    )
    layer_rows = []
    token_rows = []
    for batch_index in range(MICRO):
        first_row = batch_index * rows_micro
        inputs = lax.slice_in_dim(tokens, first_row, first_row + rows_micro, axis=0).astype(
            jnp.float32
        )
        grad_out = lax.slice_in_dim(cotangent, first_row, first_row + rows_micro, axis=0)
        normed_one, scale_one, normed_low = norm_forward(inputs, norm_gain)
        signal = normed_low.astype(jnp.float32)
        ema_value, ema_pull = jax.vjp(ema_local, signal, ema_delta, ema_alpha, ema_beta, ema_eta)
        mix_pre = ema_value + ema_omega * signal
        mixed_low = jax.nn.silu(mix_pre).astype(jnp.bfloat16)
        normed_all, mixed_all = (
            lax.all_gather(normed_low, "mp", axis=1, tiled=True),
            lax.all_gather(mixed_low, "mp", axis=1, tiled=True),
        )
        shared_pre = matmul(mixed_all, shared_proj)
        shared = jax.nn.silu(shared_pre)
        query = (shared * query_gain + query_bias).astype(jnp.bfloat16)
        keys = (shared * key_gain).astype(jnp.bfloat16)
        value_pre = matmul(normed_all, value_proj)
        values = jax.nn.silu(value_pre).astype(jnp.bfloat16)
        gate_pre = matmul(mixed_all, gate_proj)
        gate = jax.nn.silu(gate_pre)
        scores = group_scores(query, keys)
        peak = jnp.max(scores, axis=-1, keepdims=True)
        weights = jnp.exp(scores - peak)
        weight_sum = jnp.sum(weights, axis=-1, keepdims=True)
        log_total = peak + jnp.log(weight_sum)
        probabilities = weights / weight_sum
        blocks = probabilities.shape[0]
        value_block_rows = values.reshape(blocks, GROUP, values.shape[1])
        attention_result = jnp.einsum(
            "dzc,dcs->dzs",
            probabilities.astype(jnp.bfloat16),
            value_block_rows,
            preferred_element_type=jnp.float32,
        ).reshape(rows_micro, values.shape[1])
        hidden = (gate * attention_result).astype(jnp.bfloat16)
        attn_out = lax.psum_scatter(
            matmul(hidden, output_proj).astype(jnp.bfloat16), "mp", scatter_dimension=1, tiled=True
        ).astype(jnp.float32)
        update = jax.nn.sigmoid(matmul(mixed_all, update_proj))
        act_pre = matmul(mixed_all, mixer_proj) + attn_out
        act_value = jax.nn.silu(act_pre)
        middle = update * act_value + (1.0 - update) * inputs
        normed_two, scale_two, ffn_low = norm_forward(middle, ffn_gain)
        ffn_all = lax.all_gather(ffn_low, "mp", axis=1, tiled=True)
        up_pre = matmul(ffn_all, up_proj)
        upper = jax.nn.silu(up_pre).astype(jnp.bfloat16)
        down_out = lax.psum_scatter(
            matmul(upper, down_proj).astype(jnp.bfloat16), "mp", scatter_dimension=1, tiled=True
        ).astype(jnp.float32)
        layer_rows.append((middle + down_out).astype(jnp.bfloat16))
        grad_all = lax.all_gather(grad_out, "mp", axis=1, tiled=True)
        down_part = matmul_tn(upper, grad_all)
        d_up_pre = (matmul_nt(grad_all, down_proj) * silu_slope(up_pre)).astype(jnp.bfloat16)
        up_part = matmul_tn(ffn_all, d_up_pre)
        d_ffn_in = lax.psum_scatter(
            matmul_nt(d_up_pre, up_proj).astype(jnp.bfloat16), "mp", scatter_dimension=1, tiled=True
        ).astype(jnp.float32)
        d_middle, ffn_gain_part = norm_backward(d_ffn_in, normed_two, scale_two, ffn_gain)
        d_middle = d_middle + grad_out.astype(jnp.float32)
        ffn_sums = (ffn_sums[0] + ffn_gain_part, ffn_sums[1] + up_part, ffn_sums[2] + down_part)
        if batch_index == MICRO - 1:
            ffn_reduced = ffn_sums
        d_update_pre = (d_middle * (act_value - inputs) * update * (1.0 - update)).astype(
            jnp.bfloat16
        )
        d_act_pre = (d_middle * update * silu_slope(act_pre)).astype(jnp.bfloat16)
        d_inputs = d_middle * (1.0 - update)
        mixer_part = matmul_tn(mixed_all, d_act_pre)
        update_part = matmul_tn(mixed_all, d_update_pre)
        d_act_all = lax.all_gather(d_act_pre, "mp", axis=1, tiled=True)
        output_part = matmul_tn(hidden, d_act_all)
        d_hidden = matmul_nt(d_act_all, output_proj)
        d_gate_pre = (d_hidden * attention_result * silu_slope(gate_pre)).astype(jnp.bfloat16)
        d_attended = (d_hidden * gate).astype(jnp.bfloat16)
        attention_result_blocks = d_attended.reshape(blocks, GROUP, d_attended.shape[1])
        probs_again = jnp.exp(group_scores(query, keys) - log_total)
        d_probs = lax.psum(
            jnp.einsum(
                "gas,gcs->gac",
                attention_result_blocks,
                value_block_rows,
                preferred_element_type=jnp.float32,
            ).astype(jnp.bfloat16),
            "mp",
        ).astype(jnp.float32)
        d_value = jnp.einsum(
            "uhi,uhs->uis",
            probs_again.astype(jnp.bfloat16),
            attention_result_blocks,
            preferred_element_type=jnp.float32,
        ).reshape(rows_micro, values.shape[1])
        d_value_pre = (d_value * silu_slope(value_pre)).astype(jnp.bfloat16)
        d_scores = probs_again * (d_probs - jnp.sum(probs_again * d_probs, axis=-1, keepdims=True))
        d_scores_low = d_scores.astype(jnp.bfloat16)
        query_blocks = query.reshape(blocks, GROUP, query.shape[1])
        key_blocks = keys.reshape(blocks, GROUP, keys.shape[1])
        d_query = (
            jnp.einsum(
                "nqk,nkz->nqz", d_scores_low, key_blocks, preferred_element_type=jnp.float32
            ).reshape(rows_micro, -1)
            * head_scale
        )
        d_keys = (
            jnp.einsum(
                "nqk,nqz->nkz", d_scores_low, query_blocks, preferred_element_type=jnp.float32
            ).reshape(rows_micro, -1)
            * head_scale
        )
        query_part = jnp.sum(d_query * shared, axis=0)
        bias_part = jnp.sum(d_query, axis=0)
        key_part = jnp.sum(d_keys * shared, axis=0)
        d_shared_pre = ((d_query * query_gain + d_keys * key_gain) * silu_slope(shared_pre)).astype(
            jnp.bfloat16
        )
        shared_part = matmul_tn(mixed_all, d_shared_pre)
        value_part = matmul_tn(normed_all, d_value_pre)
        gate_part = matmul_tn(mixed_all, d_gate_pre)
        mixed_terms = matmul_nt(d_gate_pre, gate_proj) + matmul_nt(d_update_pre, update_proj)
        mixed_terms = mixed_terms + matmul_nt(d_act_pre, mixer_proj)
        normed_terms = matmul_nt(d_value_pre, value_proj)
        d_mixed, d_normed = (
            lax.psum_scatter(
                mixed_terms.astype(jnp.bfloat16), "mp", scatter_dimension=1, tiled=True
            ).astype(jnp.float32),
            lax.psum_scatter(
                normed_terms.astype(jnp.bfloat16), "mp", scatter_dimension=1, tiled=True
            ).astype(jnp.float32),
        )
        d_mixed = d_mixed + matmul_nt(d_shared_pre, shared_rows)
        d_mix_pre = d_mixed * silu_slope(mix_pre)
        omega_part = jnp.sum(d_mix_pre * signal, axis=0)
        d_signal, delta_part, alpha_part, beta_part, eta_part = ema_pull(d_mix_pre)
        d_normed = d_normed + d_signal + d_mix_pre * ema_omega
        d_tokens, gain_part = norm_backward(d_normed, normed_one, scale_one, norm_gain)
        token_rows.append((d_inputs + d_tokens).astype(jnp.bfloat16))
        summand_terms = (
            gain_part,
            delta_part,
            alpha_part,
            beta_part,
            eta_part,
            omega_part,
            shared_part,
            query_part,
            bias_part,
            key_part,
            value_part,
            gate_part,
            mixer_part,
            update_part,
            output_part,
        )
        mixer_totals_list = tuple(
            (
                running_total + summand_term
                for running_total, summand_term in zip(mixer_totals_list, summand_terms)
            )
        )
    reduced = lax.psum(
        (
            mixer_totals_list[0],
            mixer_totals_list[1],
            mixer_totals_list[2],
            mixer_totals_list[3],
            mixer_totals_list[4],
            mixer_totals_list[5],
            mixer_totals_list[6],
            mixer_totals_list[7],
            mixer_totals_list[8],
            mixer_totals_list[9],
            mixer_totals_list[10],
            mixer_totals_list[11],
            mixer_totals_list[12],
            mixer_totals_list[13],
            mixer_totals_list[14],
            ffn_sums[0],
            ffn_sums[1],
            ffn_sums[2],
        ),
        "dp",
    )
    mixer_reduced = reduced[:15]
    ffn_reduced = reduced[15:]
    layer_out = jnp.concatenate(layer_rows, axis=0)
    token_grad = jnp.concatenate(token_rows, axis=0)
    return (
        layer_out,
        token_grad,
        mixer_reduced[0],
        mixer_reduced[1],
        mixer_reduced[2],
        mixer_reduced[3],
        mixer_reduced[4],
        mixer_reduced[5],
        mixer_reduced[6],
        mixer_reduced[7],
        mixer_reduced[8],
        mixer_reduced[9],
        mixer_reduced[10],
        mixer_reduced[11],
        mixer_reduced[12],
        mixer_reduced[13],
        mixer_reduced[14],
        ffn_reduced[0],
        ffn_reduced[1],
        ffn_reduced[2],
    )


def solution(mesh):
    in_specs = (
        P("dp", "mp"),
        P("dp", "mp"),
        P("mp"),
        P("mp", None),
        P("mp", None),
        P("mp", None),
        P("mp", None),
        P("mp"),
        P(),
        P(),
        P(),
        P(),
        P(None, "mp"),
        P(None, "mp"),
        P(None, "mp"),
        P(None, "mp"),
        P("mp", None),
        P("mp"),
        P(None, "mp"),
        P("mp", None),
    )
    out_specs = (
        P("dp", "mp"),
        P("dp", "mp"),
        P("mp"),
        P("mp", None),
        P("mp", None),
        P("mp", None),
        P("mp", None),
        P("mp"),
        P(),
        P(),
        P(),
        P(),
        P(None, "mp"),
        P(None, "mp"),
        P(None, "mp"),
        P(None, "mp"),
        P("mp", None),
        P("mp"),
        P(None, "mp"),
        P("mp", None),
    )
    return jax.shard_map(local, mesh=mesh, in_specs=in_specs, out_specs=out_specs, check_vma=False)
```

profile of v0, /device:TPU:0, one launch (start us, length us, event | category | flops | bytes accessed | tf_op | source)
XLA Modules:
  0.0 2425.8 jit_solution(17531408031681746158)
XLA Ops:
  15.4 21.4 all-reduce.5
  45.8 6.0 fusion.142
  55.5 66.9 %gather_fusion = f32[16384,256]{1,0:T(8,128)} fusion(f32[128,256]{1,0:T(8,128)S(1)} %copy.189, s32[16384]{0:T(1024)} %broadcast_clamp_fusion), kind=kCustom, calls=%fused_computation.clone | custom fusion | bytes 33619968 | tf_op jit(solution)/shard_map/jvp(jit(_take))/gather | solution.py:62
  122.4 18.1 copy.190
  140.5 20.4 fusion.2
  160.9 14.5 fusion.3
  179.7 21.2 while.64
  208.4 21.2 while.65
  233.1 7.3 bitcast_add_fusion.6
  243.3 7.3 bitcast_add_fusion.7
  261.9 76.3 %all-gather.11.cloned.1.call-done = bf16[2048,1024]{1,0:T(8,128)(2,1)} async-done(((bf16[2048,256]{1,0:T(8,128)(2,1)}), bf16[2048,1024]{1,0:T(8,128)(2,1)}) %all-gather.11.cloned.1.call-update) | async-done | bytes 4194320 | tf_op jit(solution)/shard_map/all_gather | solution.py:153
  341.7 77.5 %all-gather.17.cloned.1.call-done = bf16[2048,1024]{1,0:T(8,128)(2,1)} async-done(((bf16[2048,256]{1,0:T(8,128)(2,1)}), bf16[2048,1024]{1,0:T(8,128)(2,1)}) %all-gather.17.cloned.1.call-update) | async-done | bytes 4194320 | tf_op jit(solution)/shard_map/all_gather | solution.py:153
  425.5 74.6 %all-gather.19.cloned.1.call-done = bf16[2048,1024]{1,0:T(8,128)(2,1)} async-done(((bf16[2048,256]{1,0:T(8,128)(2,1)}), bf16[2048,1024]{1,0:T(8,128)(2,1)}) %all-gather.19.cloned.1.call-update) | async-done | bytes 4194320 | tf_op jit(solution)/shard_map/all_gather | solution.py:152
  500.1 7.3 multiply_convert_fusion.6
  524.0 56.2 %all-gather.13.cloned.1.call-done = bf16[2048,1024]{1,0:T(8,128)(2,1)} async-done(((bf16[2048,256]{1,0:T(8,128)(2,1)}), bf16[2048,1024]{1,0:T(8,128)(2,1)}) %all-gather.13.cloned.1.call-update) | async-done | bytes 4194320 | tf_op jit(solution)/shard_map/all_gather | solution.py:152
  580.3 7.5 multiply_convert_fusion.7
  607.9 49.4 %reduce-scatter.15.cloned.1.call-done = bf16[2048,256]{1,0:T(8,128)(2,1)} async-done(((bf16[2048,1024]{1,0:T(8,128)(2,1)}), bf16[2048,256]{1,0:T(8,128)(2,1)}) %reduce-scatter.15.cloned.1.call-update) | async-done | bytes 1048592 | tf_op jit(solution)/shard_map/reduce_scatter | solution.py:178
  662.5 74.5 %reduce-scatter.11.cloned.1.call-done = bf16[2048,256]{1,0:T(8,128)(2,1)} async-done(((bf16[2048,1024]{1,0:T(8,128)(2,1)}), bf16[2048,256]{1,0:T(8,128)(2,1)}) %reduce-scatter.11.cloned.1.call-update) | async-done | bytes 1048592 | tf_op jit(solution)/shard_map/reduce_scatter | solution.py:178
  742.0 6.6 fusion.254
  748.6 18.2 all-reduce.4
  773.1 75.6 %all-gather.15.cloned.1.call-done = bf16[2048,1024]{1,0:T(8,128)(2,1)} async-done(((bf16[2048,256]{1,0:T(8,128)(2,1)}), bf16[2048,1024]{1,0:T(8,128)(2,1)}) %all-gather.15.cloned.1.call-update) | async-done | bytes 4194320 | tf_op jit(solution)/shard_map/all_gather | solution.py:186
  848.7 10.7 multiply_convert_fusion.3
  859.5 69.6 %all-gather.23.cloned.1.call-done = bf16[2048,1024]{1,0:T(8,128)(2,1)} async-done(((bf16[2048,256]{1,0:T(8,128)(2,1)}), bf16[2048,1024]{1,0:T(8,128)(2,1)}) %all-gather.23.cloned.1.call-update) | async-done | bytes 4194320 | tf_op jit(solution)/shard_map/all_gather | solution.py:193
  929.1 11.8 multiply_convert_fusion.1
  942.9 6.3 convolution_convert_fusion.5
  949.5 74.9 %reduce-scatter.19.cloned.1.call-done = bf16[2048,256]{1,0:T(8,128)(2,1)} async-done(((bf16[2048,1024]{1,0:T(8,128)(2,1)}), bf16[2048,256]{1,0:T(8,128)(2,1)}) %reduce-scatter.19.cloned.1.call-update) | async-done | bytes 1048592 | tf_op jit(solution)/shard_map/reduce_scatter | solution.py:197
  1029.9 80.4 %all-gather.21.cloned.1.call-done = bf16[2048,1024]{1,0:T(8,128)(2,1)} async-done(((bf16[2048,256]{1,0:T(8,128)(2,1)}), bf16[2048,1024]{1,0:T(8,128)(2,1)}) %all-gather.21.cloned.1.call-update) | async-done | bytes 4194320 | tf_op jit(solution)/shard_map/all_gather | solution.py:186
  1110.4 9.0 fusion.268
  1119.4 71.4 %all-gather.27.cloned.1.call-done = bf16[2048,1024]{1,0:T(8,128)(2,1)} async-done(((bf16[2048,256]{1,0:T(8,128)(2,1)}), bf16[2048,1024]{1,0:T(8,128)(2,1)}) %all-gather.27.cloned.1.call-update) | async-done | bytes 4194320 | tf_op jit(solution)/shard_map/all_gather | solution.py:193
  1190.8 11.8 multiply_convert_fusion
  1204.7 6.3 convolution_convert_fusion.4
  1211.4 74.8 %reduce-scatter.25.cloned.1.call-done = bf16[2048,256]{1,0:T(8,128)(2,1)} async-done(((bf16[2048,1024]{1,0:T(8,128)(2,1)}), bf16[2048,256]{1,0:T(8,128)(2,1)}) %reduce-scatter.25.cloned.1.call-update) | async-done | bytes 1048592 | tf_op jit(solution)/shard_map/reduce_scatter | solution.py:197
  1289.4 18.2 all-reduce.3
  1307.7 6.4 fusion.93
  1314.3 6.1 fusion.75
  1320.5 6.1 fusion.274
  1326.6 66.7 %all-gather.29.cloned.1.call-done = bf16[2048,1024]{1,0:T(8,128)(2,1)} async-done(((bf16[2048,256]{1,0:T(8,128)(2,1)}), bf16[2048,1024]{1,0:T(8,128)(2,1)}) %all-gather.29.cloned.1.call-update) | async-done | bytes 4194320 | tf_op jit(solution)/shard_map/all_gather | solution.py:212
  1393.3 8.3 fusion.24
  1404.4 69.1 %all-gather.25.cloned.1.call-done = bf16[2048,1024]{1,0:T(8,128)(2,1)} async-done(((bf16[2048,256]{1,0:T(8,128)(2,1)}), bf16[2048,1024]{1,0:T(8,128)(2,1)}) %all-gather.25.cloned.1.call-update) | async-done | bytes 4194320 | tf_op jit(solution)/shard_map/all_gather | solution.py:212
  1473.5 8.3 fusion.27
  1489.7 7.0 add_convert_fusion
  1528.7 10.6 convolution_convert_fusion.6
  1540.1 9.5 convolution_convert_fusion.7
  1550.1 10.3 fusion.286
  1565.0 10.5 convolution_add_fusion.4
  1575.6 6.3 convolution_add_fusion.5
  1645.5 23.4 while.67
  1668.9 24.7 %reduce-scatter.23.cloned.1.call-done = bf16[2048,256]{1,0:T(8,128)(2,1)} async-done(((bf16[2048,1024]{1,0:T(8,128)(2,1)}), bf16[2048,256]{1,0:T(8,128)(2,1)}) %reduce-scatter.23.cloned.1.call-update) | async-done | bytes 1048592 | tf_op jit(solution)/shard_map/reduce_scatter | solution.py:264
  1708.5 23.4 while.66
  1734.4 17.7 fusion
  1763.5 17.5 fusion.1
  1790.0 16.1 select_bitcast_fusion.1
  1806.0 17.9 copy.254
  1823.9 99.6 %scatter_custom_fusion = f32[128,256]{1,0:T(8,128)} fusion(s32[16384]{0:T(1024)S(1)} %fusion.236, f32[16384,256]{1,0:T(8,128)} %bitcast.424, f32[]{:T(128)} %constant.164.clone.1), kind=kCustom, calls=%fused_computation.354 | custom fusion | flops 4194304 | bytes 131584 | tf_op jit(solution)/shard_map/transpose(jvp(jit(_take)))/scatter-add | solution.py:62
  1925.2 16.9 select_bitcast_fusion
  1942.0 17.9 copy.255
  1960.0 99.4 %scatter_custom_fusion.1 = f32[128,256]{1,0:T(8,128)} fusion(s32[16384]{0:T(1024)S(1)} %fusion.236, f32[16384,256]{1,0:T(8,128)} %bitcast.423, f32[]{:T(128)} %constant.164.clone.1), kind=kCustom, calls=%fused_computation.352 | custom fusion | flops 4194304 | bytes 131584 | tf_op jit(solution)/shard_map/transpose(jvp(jit(_take)))/scatter-add | solution.py:62
  2067.8 11.6 fusion.97
  2091.3 8.3 fusion.69
  2107.4 18.5 all-reduce.2
  2126.1 7.5 fusion.86
  2133.6 6.3 fusion.68
  2143.0 12.7 all-reduce.11.cloned.1.call-done
  2155.7 233.3 %all-reduce.13.cloned.1.call-done = (f32[1024,128]{1,0:T(8,128)}, f32[1024,512]{1,0:T(8,128)}, f32[1024,512]{1,0:T(8,128)}, f32[1024,256]{1,0:T(8,128)}, f32[102...) async-done(((f32[1024,128]{1,0:T(8,128)}, f32[1024,512]{1,0:T(8,128)}, f32[1024,512]{1,0:T(8,128)}, f32[1024,256]{1,0:T(8,128)}, ...) | async-done | bytes 17301520 | tf_op jit(solution)/shard_map/psum | solution.py:301
  (757 shorter events, 427.5 us)
Async XLA Ops:
  7.2 841.5 %copy-start = (bf16[1024,1024]{1,0:T(8,128)(2,1)S(1)}, bf16[1024,1024]{1,0:T(8,128)(2,1)}, u32[]{:S(2)}) copy-start(bf16[1024,1024]{1,0:T(8,128)(2,1)} %param.48) | copy-start | bytes 6291460
  7.3 331.0 %all-gather.11.cloned.1.call-start = ((), (), s32[]{:S(2)}) async-start(), calls=%async_computation.10 | async-start | bytes 5242880 | tf_op jit(solution)/shard_map/all_gather | solution.py:153
  12.0 231.3 %copy-start.69 = (f32[256,16]{1,0:T(8,128)}, f32[256,16]{1,0:T(8,128)S(1)}, u32[]{:S(2)}) copy-start(f32[256,16]{1,0:T(8,128)S(1)} %copy.195) | copy-start | bytes 49156
  12.7 230.5 %copy-start.47 = (f32[256,16]{1,0:T(8,128)}, f32[256,16]{1,0:T(8,128)S(1)}, u32[]{:S(2)}) copy-start(f32[256,16]{1,0:T(8,128)S(1)} %copy.187) | copy-start | bytes 49156
  40.9 212.5 %copy-start.16 = (bf16[2048,256]{1,0:T(8,128)(2,1)}, bf16[2048,256]{1,0:T(8,128)(2,1)S(1)}, u32[]{:S(2)}) copy-start(bf16[2048,256]{1,0:T(8,128)(2,1)S(1)} %get-tuple-element.727) | copy-start | bytes 3145732
  140.5 20.4 copy-start.2
  140.5 20.4 copy-start.24
  207.7 25.4 %copy-start.159 = (f32[128]{0:T(128)S(1)}, f32[128]{0:T(128)}, u32[]{:S(2)}) copy-start(f32[128]{0:T(128)} %get-tuple-element.782) | copy-start | bytes 1540
  259.3 79.0 %copy-start.105 = (bf16[1024,128]{1,0:T(8,128)(2,1)S(1)}, bf16[1024,128]{1,0:T(8,128)(2,1)}, u32[]{:S(2)}) copy-start(bf16[1024,128]{1,0:T(8,128)(2,1)} %param.38) | copy-start | bytes 786436
  259.3 159.9 %all-gather.17.cloned.1.call-start = ((), (), s32[]{:S(2)}) async-start(), calls=%async_computation.15 | async-start | bytes 5242880 | tf_op jit(solution)/shard_map/all_gather | solution.py:153
  260.0 240.0 %all-gather.19.cloned.1.call-start = ((), (), s32[]{:S(2)}) async-start(), calls=%async_computation.16 | async-start | bytes 5242880 | tf_op jit(solution)/shard_map/all_gather | solution.py:152
  260.8 319.5 %all-gather.13.cloned.1.call-start = ((), (), s32[]{:S(2)}) async-start(), calls=%async_computation.11 | async-start | bytes 5242880 | tf_op jit(solution)/shard_map/all_gather | solution.py:152
  261.3 396.0 %reduce-scatter.15.cloned.1.call-start = ((), (), s32[]{:S(2)}) async-start(), calls=%async_computation.17 | async-start | bytes 5242880 | tf_op jit(solution)/shard_map/reduce_scatter | solution.py:178
  261.9 157.3 %copy-start.167 = (f32[128]{0:T(128)S(1)}, f32[128]{0:T(128)}, u32[]{:S(2)}) copy-start(f32[128]{0:T(128)} %param.41) | copy-start | bytes 1540
  261.9 157.3 %copy-start.169 = (f32[128]{0:T(128)S(1)}, f32[128]{0:T(128)}, u32[]{:S(2)}) copy-start(f32[128]{0:T(128)} %param.39) | copy-start | bytes 1540
  261.9 157.3 %copy-start.183 = (f32[128]{0:T(128)S(1)}, f32[128]{0:T(128)}, u32[]{:S(2)}) copy-start(f32[128]{0:T(128)} %param.40) | copy-start | bytes 1540
  341.7 82.4 %copy-start.54 = (f32[2048,128]{1,0:T(8,128)}, f32[2048,128]{1,0:T(8,128)S(1)}, u32[]{:S(2)}) copy-start(f32[2048,128]{1,0:T(8,128)S(1)} %fusion.267) | copy-start | bytes 3145732
  425.3 82.1 %copy-start.12 = (f32[16,128,128]{1,2,0:T(8,128)}, f32[16,128,128]{1,2,0:T(8,128)S(1)}, u32[]{:S(2)}) copy-start(f32[16,128,128]{1,2,0:T(8,128)S(1)} %get-tuple-element.772) | copy-start | bytes 3145732
  425.3 82.1 %copy-start.124 = (f32[16,128]{1,0:T(8,128)}, f32[16,128]{1,0:T(8,128)S(1)}, u32[]{:S(2)}) copy-start(f32[16,128]{1,0:T(8,128)S(1)} %get-tuple-element.771) | copy-start | bytes 24580
  425.5 81.9 %copy-start.140 = (f32[16,128]{1,0:T(8,128)}, f32[16,128]{1,0:T(8,128)S(1)}, u32[]{:S(2)}) copy-start(f32[16,128]{1,0:T(8,128)S(1)} %fusion.215) | copy-start | bytes 24580
  521.9 215.0 %reduce-scatter.11.cloned.1.call-start = ((), (), s32[]{:S(2)}) async-start(), calls=%async_computation.12 | async-start | bytes 5242880 | tf_op jit(solution)/shard_map/reduce_scatter | solution.py:178
  523.8 63.9 %copy-start.14 = (f32[16,128,128]{1,2,0:T(8,128)}, f32[16,128,128]{1,2,0:T(8,128)S(1)}, u32[]{:S(2)}) copy-start(f32[16,128,128]{1,2,0:T(8,128)S(1)} %get-tuple-element.766) | copy-start | bytes 3145732
  523.8 63.9 %copy-start.126 = (f32[16,128]{1,0:T(8,128)}, f32[16,128]{1,0:T(8,128)S(1)}, u32[]{:S(2)}) copy-start(f32[16,128]{1,0:T(8,128)S(1)} %get-tuple-element.765) | copy-start | bytes 24580
  524.0 63.7 %copy-start.142 = (f32[16,128]{1,0:T(8,128)}, f32[16,128]{1,0:T(8,128)S(1)}, u32[]{:S(2)}) copy-start(f32[16,128]{1,0:T(8,128)S(1)} %fusion.214) | copy-start | bytes 24580
  602.2 55.2 %copy-start.76 = (bf16[1024,256]{1,0:T(8,128)(2,1)S(1)}, bf16[1024,256]{1,0:T(8,128)(2,1)}, u32[]{:S(2)}) copy-start(bf16[1024,256]{1,0:T(8,128)(2,1)} %param.44) | copy-start | bytes 1572868
  602.2 246.6 %all-gather.15.cloned.1.call-start = ((), (), s32[]{:S(2)}) async-start(), calls=%async_computation.13 | async-start | bytes 5242880 | tf_op jit(solution)/shard_map/all_gather | solution.py:186
  742.0 24.9 %copy-start.154 = (f32[256]{0:T(256)S(1)}, f32[256]{0:T(256)}, u32[]{:S(2)}) copy-start(f32[256]{0:T(256)} %param.47) | copy-start | bytes 3076
  766.8 547.4 %copy-start.106 = (f32[2048]{0:T(1024)}, f32[2048]{0:T(1024)S(1)}, u32[]{:S(2)}) copy-start(f32[2048]{0:T(1024)S(1)} %get-tuple-element.749) | copy-start | bytes 24580
  766.8 547.4 %copy-start.108 = (f32[2048]{0:T(1024)}, f32[2048]{0:T(1024)S(1)}, u32[]{:S(2)}) copy-start(f32[2048]{0:T(1024)S(1)} %get-tuple-element.750) | copy-start | bytes 24580
  769.6 159.5 %all-gather.23.cloned.1.call-start = ((), (), s32[]{:S(2)}) async-start(), calls=%async_computation.20 | async-start | bytes 5242880 | tf_op jit(solution)/shard_map/all_gather | solution.py:193
  772.7 251.6 %reduce-scatter.19.cloned.1.call-start = ((), (), s32[]{:S(2)}) async-start(), calls=%async_computation.21 | async-start | bytes 5242880 | tf_op jit(solution)/shard_map/reduce_scatter | solution.py:197
  949.2 161.2 %all-gather.21.cloned.1.call-start = ((), (), s32[]{:S(2)}) async-start(), calls=%async_computation.18 | async-start | bytes 5242880 | tf_op jit(solution)/shard_map/all_gather | solution.py:186
  949.4 358.2 %copy-start.110 = (f32[2048]{0:T(1024)}, f32[2048]{0:T(1024)S(1)}, u32[]{:S(2)}) copy-start(f32[2048]{0:T(1024)S(1)} %get-tuple-element.751) | copy-start | bytes 24580
  949.4 358.2 %copy-start.112 = (f32[2048]{0:T(1024)}, f32[2048]{0:T(1024)S(1)}, u32[]{:S(2)}) copy-start(f32[2048]{0:T(1024)S(1)} %get-tuple-element.752) | copy-start | bytes 24580
  1029.1 161.7 %all-gather.27.cloned.1.call-start = ((), (), s32[]{:S(2)}) async-start(), calls=%async_computation.25 | async-start | bytes 5242880 | tf_op jit(solution)/shard_map/all_gather | solution.py:193
  1029.9 256.3 %reduce-scatter.25.cloned.1.call-start = ((), (), s32[]{:S(2)}) async-start(), calls=%async_computation.26 | async-start | bytes 5242880 | tf_op jit(solution)/shard_map/reduce_scatter | solution.py:197
  1211.1 96.6 %copy-start.4 = (bf16[4096,256]{1,0:T(8,128)(2,1)S(1)}, bf16[4096,256]{1,0:T(8,128)(2,1)}, u32[]{:S(2)}) copy-start(bf16[4096,256]{1,0:T(8,128)(2,1)} %param.30) | copy-start | bytes 6291460
  1211.1 182.2 %all-gather.29.cloned.1.call-start = ((), (), s32[]{:S(2)}) async-start(), calls=%async_computation.27 | async-start | bytes 5242880 | tf_op jit(solution)/shard_map/all_gather | solution.py:212
  1314.2 159.3 %all-gather.25.cloned.1.call-start = ((), (), s32[]{:S(2)}) async-start(), calls=%async_computation.22 | async-start | bytes 5242880 | tf_op jit(solution)/shard_map/all_gather | solution.py:212
  1320.4 290.7 %all-reduce.15.cloned.1.call-start = ((), (), s32[]{:S(2)}) async-start(), calls=%async_computation.32 | async-start | bytes 2097152 | tf_op jit(solution)/shard_map/psum | solution.py:219
  1320.5 72.8 %copy-start.177 = (bf16[512,1024]{1,0:T(8,128)(2,1)S(1)}, bf16[512,1024]{1,0:T(8,128)(2,1)}, u32[]{:S(2)}) copy-start(bf16[512,1024]{1,0:T(8,128)(2,1)} %param.46) | copy-start | bytes 3145732
  1484.7 146.0 %reduce-scatter.29.cloned.1.call-start = ((), (), s32[]{:S(2)}) async-start(), calls=%async_computation.29 | async-start | bytes 5242880 | tf_op jit(solution)/shard_map/reduce_scatter | solution.py:264
  1496.7 197.0 %reduce-scatter.23.cloned.1.call-start = ((), (), s32[]{:S(2)}) async-start(), calls=%async_computation.24 | async-start | bytes 5242880 | tf_op jit(solution)/shard_map/reduce_scatter | solution.py:264
  1505.7 585.5 %reduce-scatter.27.cloned.1.call-start = ((), (), s32[]{:S(2)}) async-start(), calls=%async_computation.28 | async-start | bytes 5242880 | tf_op jit(solution)/shard_map/reduce_scatter | solution.py:267
  1517.1 574.2 %reduce-scatter.21.cloned.1.call-start = ((), (), s32[]{:S(2)}) async-start(), calls=%async_computation.23 | async-start | bytes 5242880 | tf_op jit(solution)/shard_map/reduce_scatter | solution.py:267
  1528.5 597.5 %reduce-scatter.17.cloned.1.call-start = ((), (), s32[]{:S(2)}) async-start(), calls=%async_computation.19 | async-start | bytes 5242880 | tf_op jit(solution)/shard_map/reduce_scatter | solution.py:189
  1539.4 594.2 %reduce-scatter.13.cloned.1.call-start = ((), (), s32[]{:S(2)}) async-start(), calls=%async_computation.14 | async-start | bytes 5242880 | tf_op jit(solution)/shard_map/reduce_scatter | solution.py:189
  1549.6 606.1 %all-reduce.11.cloned.1.call-start = ((), (), s32[]{:S(2)}) async-start(), calls=%async_computation.30 | async-start | bytes 140288 | tf_op jit(solution)/shard_map/psum | solution.py:301
  1642.2 51.5 %copy-start.80 = (bf16[2048,128]{1,0:T(8,128)(2,1)S(1)}, bf16[2048,128]{1,0:T(8,128)(2,1)}, u32[]{:S(2)}) copy-start(bf16[2048,128]{1,0:T(8,128)(2,1)} %copy-done.79) | copy-start | bytes 1572868
  1708.5 25.9 %copy-start.96 = (pred[128,128]{1,0:T(8,128)(4,1)S(1)}, pred[128,128]{1,0:T(8,128)(4,1)}, u32[]{:S(2)}) copy-start(pred[128,128]{1,0:T(8,128)(4,1)} %get-tuple-element.778) | copy-start | bytes 49156
  1708.5 25.9 %copy-start.104 = (pred[128,128]{1,0:T(8,128)(4,1)S(1)}, pred[128,128]{1,0:T(8,128)(4,1)}, u32[]{:S(2)}) copy-start(pred[128,128]{1,0:T(8,128)(4,1)} %get-tuple-element.779) | copy-start | bytes 49156
  1806.0 119.1 %copy-start.23 = (bf16[16,128,256]{1,0,2:T(8,128)(2,1)S(1)}, bf16[16,128,256]{1,0,2:T(8,128)(2,1)}, u32[]{:S(2)}) copy-start(bf16[16,128,256]{1,0,2:T(8,128)(2,1)} %copy.199) | copy-start | bytes 3145732
  2067.8 23.5 copy-start.5
  2067.8 23.5 copy-start.133
  2067.8 23.5 copy-start.135
  2067.8 23.5 copy-start.137
  2067.8 23.5 copy-start.139
  2102.0 286.9 %all-reduce.13.cloned.1.call-start = ((), (), s32[]{:S(2)}) async-start(), calls=%async_computation.31 | async-start | bytes 34603008 | tf_op jit(solution)/shard_map/psum | solution.py:301
  2106.6 19.3 copy-start.111
  2106.6 19.3 copy-start.113
  2106.7 19.3 copy-start.149
  2106.7 19.3 copy-start.151
  2106.7 19.3 copy-start.155
  2106.7 19.3 copy-start.158
  (148 other events, 662.6 us)
Sparse Core Ops, SparseCore 0:
  259.4 78.7 all-gather.10
  340.4 78.7 all-gather.16
  421.3 78.7 all-gather.18
  501.5 78.7 all-gather.12
  582.4 74.9 reduce-scatter.14
  659.6 77.2 reduce-scatter.10
  769.7 78.9 all-gather.14
  850.3 78.7 all-gather.22
  949.3 74.9 reduce-scatter.18
  1029.3 81.0 all-gather.20
  1112.0 78.7 all-gather.26
  1211.2 74.9 reduce-scatter.24
  1314.3 78.9 all-gather.28
  1394.7 78.7 all-gather.24
  1484.8 50.3 all-reduce.14
  1537.5 76.1 reduce-scatter.28
  1616.4 77.2 reduce-scatter.22
  1695.9 77.2 reduce-scatter.26
  1776.1 77.2 reduce-scatter.20
  1855.6 77.2 reduce-scatter.16
  1935.2 77.2 reduce-scatter.12
  2102.2 53.4 all-reduce.10
  2161.4 227.5 all-reduce.12
where the time goes:
time: 2440 us; the launch traced here: 2430 us
  waiting for transfers between devices  1260 us (52%)
  matrix products  442 us (18%)
  other arithmetic  370 us (15%)
  local copies, waits for them, and re-layouts  253 us (10%)
  blocking collectives  76.4 us (3%)
    psum x2, waiting for transfers between devices, local(): lax.psum((mixer_totals_list[0], mixer_totals_list[1], mixer_totals_list[2...  246 us
    scatter-add x2, other arithmetic, ema_local(): jnp.take(kernel, jnp.maximum(lag, 0), axis=0)  199 us
    all_gather x2, waiting for transfers between devices, local(): ffn_all = lax.all_gather(ffn_low, 'mp', axis=1, tiled=True)  156 us
    all_gather x2, waiting for transfers between devices, local(): lax.all_gather(mixed_low, 'mp', axis=1, tiled=True)  154 us
    reduce_scatter x2, waiting for transfers between devices, local(): lax.psum_scatter(matmul_nt(d_up_pre, up_proj).astype(jnp.bfloat16), 'mp',...  150 us
    all_gather x2, waiting for transfers between devices, local(): grad_all = lax.all_gather(grad_out, 'mp', axis=1, tiled=True)  141 us
    all_gather x2, waiting for transfers between devices, local(): d_act_all = lax.all_gather(d_act_pre, 'mp', axis=1, tiled=True)  136 us
    all_gather x2, waiting for transfers between devices, local(): lax.all_gather(normed_low, 'mp', axis=1, tiled=True)  131 us
  transfers between devices with their start and end apart: 23, of which 17 were waited for; matrix products, arithmetic and copies ran while one was open for 29% of the time, Pallas kernels for 0%

commit v1 on v0

v1 whole, which is shorter than its diff:
```python
import functools

import jax
import jax.numpy as jnp
from jax import lax
from jax.experimental import pallas as pl
from jax.experimental.pallas import tpu as pltpu
from jax.sharding import PartitionSpec as P

D = 1024
GROUP = 128
LEN = 2048
NDIM = 16
LANES = 128
SUB = D // LANES
EPS = 1e-05
TB = 128


def matmul(left, right):
    return jnp.dot(left, right, preferred_element_type=jnp.float32)


def matmul_tn(left, right):
    return lax.dot_general(
        left, right, (((0,), (0,)), ((), ())), preferred_element_type=jnp.float32
    )


def matmul_nt(left, right):
    return lax.dot_general(
        left, right, (((1,), (1,)), ((), ())), preferred_element_type=jnp.float32
    )


def silu_slope(values):
    logistic = jax.nn.sigmoid(values)
    return logistic * (1.0 + values * (1.0 - logistic))


def to_rows(scratch, value):
    for part in range(SUB):
        scratch[pl.ds(part, TB, stride=SUB), :] = value[:, part * LANES : (part + 1) * LANES]


def from_rows(scratch):
    return jnp.concatenate(
        [scratch[pl.ds(part, TB, stride=SUB), :] for part in range(SUB)], axis=1
    )


def row(scratch, index):
    return scratch[pl.ds(pl.multiple_of(index * SUB, SUB), SUB), :]


def norm_ends_kernel(x_ref, gain_ref, keep_ref, xn_ref, ends_ref, rows):
    x = x_ref[...].astype(jnp.float32)
    mean = jnp.mean(x, axis=1, keepdims=True)
    power = jnp.mean(x * x, axis=1, keepdims=True)
    scale = lax.rsqrt(power - mean * mean + EPS)
    xn = ((x - mean) * scale * gain_ref[...]).astype(jnp.bfloat16)
    xn_ref[...] = xn
    to_rows(rows, xn.astype(jnp.float32))

    @pl.when(pl.program_id(0) == 0)
    def _():
        ends_ref[...] = jnp.zeros_like(ends_ref)

    keep = [keep_ref[j] for j in range(NDIM)]

    def step(t, carry):
        state, slope = carry
        now = row(rows, t)
        slope = tuple(keep[j] * slope[j] + state[j] for j in range(NDIM))
        state = tuple(keep[j] * state[j] + now for j in range(NDIM))
        return (state, slope)

    state = tuple(ends_ref[j] for j in range(NDIM))
    slope = tuple(ends_ref[NDIM + j] for j in range(NDIM))
    state, slope = lax.fori_loop(0, TB, step, (state, slope), unroll=4)
    for j in range(NDIM):
        ends_ref[j] = state[j]
        ends_ref[NDIM + j] = slope[j]


def ema_kernel(xn_ref, keep_ref, weight_ref, omega_ref, start_ref, mix_ref, xp_ref, rows, outs, state_ref):
    xn = xn_ref[...].astype(jnp.float32)
    to_rows(rows, xn)

    @pl.when(pl.program_id(0) == 0)
    def _():
        for j in range(NDIM):
            state_ref[j] = start_ref[j]

    keep = [keep_ref[j] for j in range(NDIM)]

    def step(t, state):
        now = row(rows, t)
        state = tuple(keep[j] * state[j] + now for j in range(NDIM))
        terms = [weight_ref[j] * state[j] for j in range(NDIM)]
        while len(terms) > 1:
            terms = [a + b for a, b in zip(terms[::2], terms[1::2])]
        outs[pl.ds(pl.multiple_of(t * SUB, SUB), SUB), :] = terms[0]
        return state

    state = lax.fori_loop(0, TB, step, tuple(state_ref[j] for j in range(NDIM)), unroll=4)
    for j in range(NDIM):
        state_ref[j] = state[j]
    mix = from_rows(outs) + omega_ref[...] * xn
    mix_ref[...] = mix
    xp_ref[...] = (mix * jax.nn.sigmoid(mix)).astype(jnp.bfloat16)


def adjoint_start_kernel(grad_ref, keep_ref, start_ref, rows):
    to_rows(rows, grad_ref[...])

    @pl.when(pl.program_id(0) == 0)
    def _():
        start_ref[...] = jnp.zeros_like(start_ref)

    keep = [keep_ref[j] for j in range(NDIM)]

    def step(t, state):
        now = row(rows, TB - 1 - t)
        return tuple(keep[j] * state[j] + now for j in range(NDIM))

    state = lax.fori_loop(0, TB, step, tuple(start_ref[j] for j in range(NDIM)), unroll=4)
    for j in range(NDIM):
        start_ref[j] = state[j]


def ema_params_kernel(grad_ref, xn_ref, keep_ref, start_ref, sums_ref, omega_ref, grads, rows, state_ref):
    xn = xn_ref[...].astype(jnp.float32)
    to_rows(rows, xn)
    grad = grad_ref[...]
    to_rows(grads, grad)

    @pl.when(pl.program_id(0) == 0)
    def _():
        sums_ref[...] = jnp.zeros_like(sums_ref)
        omega_ref[...] = jnp.zeros_like(omega_ref)
        state_ref[...] = start_ref[...]

    omega_ref[...] += jnp.sum(grad * xn, axis=0, keepdims=True)
    half = NDIM // 2
    for first in (0, half):
        dims = range(first, first + half)
        keep = [keep_ref[j] for j in dims]

        def step(t, carry):
            state, slope, weight_sum, keep_sum = carry
            now = row(rows, t)
            grad_now = row(grads, t)
            slope = tuple(keep[j] * slope[j] + state[j] for j in range(half))
            state = tuple(keep[j] * state[j] + now for j in range(half))
            weight_sum = tuple(weight_sum[j] + grad_now * state[j] for j in range(half))
            keep_sum = tuple(keep_sum[j] + grad_now * slope[j] for j in range(half))
            return (state, slope, weight_sum, keep_sum)

        carry = (
            tuple(state_ref[j] for j in dims),
            tuple(state_ref[NDIM + j] for j in dims),
            tuple(sums_ref[j] for j in dims),
            tuple(sums_ref[NDIM + j] for j in dims),
        )
        state, slope, weight_sum, keep_sum = lax.fori_loop(0, TB, step, carry, unroll=4)
        for place, j in enumerate(dims):
            state_ref[j] = state[place]
            state_ref[NDIM + j] = slope[place]
            sums_ref[j] = weight_sum[place]
            sums_ref[NDIM + j] = keep_sum[place]


def token_grad_kernel(
    grad_ref, x_ref, normed_ref, direct_ref, gain_ref, omega_ref, keep_ref, weight_ref, start_ref,
    out_ref, gain_sum_ref, rows, outs, state_ref,
):
    grad = grad_ref[...]
    to_rows(rows, grad)

    @pl.when(pl.program_id(0) == 0)
    def _():
        gain_sum_ref[...] = jnp.zeros_like(gain_sum_ref)
        for j in range(NDIM):
            state_ref[j] = start_ref[j]

    keep = [keep_ref[j] for j in range(NDIM)]

    def step(t, state):
        place = TB - 1 - t
        now = row(rows, place)
        state = tuple(keep[j] * state[j] + now for j in range(NDIM))
        terms = [weight_ref[j] * state[j] for j in range(NDIM)]
        while len(terms) > 1:
            terms = [a + b for a, b in zip(terms[::2], terms[1::2])]
        outs[pl.ds(pl.multiple_of(place * SUB, SUB), SUB), :] = terms[0]
        return state

    state = lax.fori_loop(0, TB, step, tuple(state_ref[j] for j in range(NDIM)), unroll=4)
    for j in range(NDIM):
        state_ref[j] = state[j]
    d_xn = from_rows(outs) + grad * omega_ref[...] + normed_ref[...].astype(jnp.float32)
    x = x_ref[...].astype(jnp.float32)
    mean = jnp.mean(x, axis=1, keepdims=True)
    power = jnp.mean(x * x, axis=1, keepdims=True)
    scale = lax.rsqrt(power - mean * mean + EPS)
    normed = (x - mean) * scale
    gain_sum_ref[...] += jnp.sum(d_xn * normed, axis=0, keepdims=True)
    scaled = d_xn * gain_ref[...]
    first = jnp.mean(scaled, axis=1, keepdims=True)
    second = jnp.mean(scaled * normed, axis=1, keepdims=True)
    back = scale * (scaled - first - normed * second)
    out_ref[...] = (direct_ref[...].astype(jnp.float32) + back).astype(jnp.bfloat16)


def sds(shape, dtype=jnp.float32):
    return jax.ShapeDtypeStruct(shape, dtype)


def block(reverse=None):
    if reverse is None:
        return pl.BlockSpec((TB, D), lambda i: (i, 0))
    return pl.BlockSpec((TB, D), lambda i: (reverse - 1 - i, 0))


def whole(*shape):
    return pl.BlockSpec(shape, lambda i: (0,) * len(shape))


STATE = (NDIM, SUB, LANES)
STATES = (2 * NDIM, SUB, LANES)
ROWS = pltpu.VMEM((TB * SUB, LANES), jnp.float32)
PARAMS = pltpu.CompilerParams(vmem_limit_bytes=32 << 20)


def norm_ends(x, gain, keep):
    count = x.shape[0]
    return pl.pallas_call(
        norm_ends_kernel,
        grid=(count // TB,),
        in_specs=[block(), whole(1, D), whole(*STATE)],
        out_specs=[block(), whole(*STATES)],
        out_shape=[sds((count, D), jnp.bfloat16), sds(STATES)],
        scratch_shapes=[ROWS],
        compiler_params=PARAMS,
        cost_estimate=pl.CostEstimate(flops=count * D * 64, transcendentals=0, bytes_accessed=count * D * 4),
        name="norm_ends",
    )(x, gain, keep)


def ema(xn, keep, weight, omega, start):
    count = xn.shape[0]
    return pl.pallas_call(
        ema_kernel,
        grid=(count // TB,),
        in_specs=[block(), whole(*STATE), whole(*STATE), whole(1, D), whole(*STATES)],
        out_specs=[block(), block()],
        out_shape=[sds((count, D)), sds((count, D), jnp.bfloat16)],
        scratch_shapes=[ROWS, ROWS, pltpu.VMEM(STATE, jnp.float32)],
        compiler_params=PARAMS,
        cost_estimate=pl.CostEstimate(flops=count * D * 64, transcendentals=0, bytes_accessed=count * D * 8),
        name="ema",
    )(xn, keep, weight, omega, start)


def adjoint_start(grad, keep):
    count = grad.shape[0]
    return pl.pallas_call(
        adjoint_start_kernel,
        grid=(count // TB,),
        in_specs=[block(count // TB), whole(*STATE)],
        out_specs=whole(*STATE),
        out_shape=sds(STATE),
        scratch_shapes=[ROWS],
        compiler_params=PARAMS,
        cost_estimate=pl.CostEstimate(flops=count * D * 32, transcendentals=0, bytes_accessed=count * D * 4),
        name="adjoint_start",
    )(grad, keep)


def ema_params(grad, xn, keep, start):
    count = grad.shape[0]
    return pl.pallas_call(
        ema_params_kernel,
        grid=(count // TB,),
        in_specs=[block(), block(), whole(*STATE), whole(*STATES)],
        out_specs=[whole(*STATES), whole(1, D)],
        out_shape=[sds(STATES), sds((1, D))],
        scratch_shapes=[ROWS, ROWS, pltpu.VMEM(STATES, jnp.float32)],
        compiler_params=PARAMS,
        cost_estimate=pl.CostEstimate(flops=count * D * 128, transcendentals=0, bytes_accessed=count * D * 6),
        name="ema_params",
    )(grad, xn, keep, start)


def token_grads(grad, x, normed_part, direct, gain, omega, keep, weight, start):
    count = grad.shape[0]
    back = count // TB
    return pl.pallas_call(
        token_grad_kernel,
        grid=(back,),
        in_specs=[
            block(back), block(back), block(back), block(back),
            whole(1, D), whole(1, D), whole(*STATE), whole(*STATE), whole(*STATE),
        ],
        out_specs=[block(back), whole(1, D)],
        out_shape=[sds((count, D), jnp.bfloat16), sds((1, D))],
        scratch_shapes=[ROWS, ROWS, pltpu.VMEM(STATE, jnp.float32)],
        compiler_params=PARAMS,
        cost_estimate=pl.CostEstimate(flops=count * D * 64, transcendentals=0, bytes_accessed=count * D * 14),
        name="token_grads",
    )(grad, x, normed_part, direct, gain, omega, keep, weight, start)


def group_scores(query, keys):
    blocks = query.shape[0] // GROUP
    query_blocks = query.reshape(blocks, GROUP, query.shape[1])
    key_blocks = keys.reshape(blocks, GROUP, keys.shape[1])
    raw = jnp.einsum("nqz,nkz->nqk", query_blocks, key_blocks, preferred_element_type=jnp.float32)
    raw = raw * query.shape[1] ** (-0.5)
    place = jnp.arange(GROUP)
    return jnp.where((place[:, None] >= place[None, :])[None], raw, -1e30)


def gather_columns(shard, dp, index):
    share = shard.shape[0] // dp
    part = lax.dynamic_slice_in_dim(shard, index * share, share, 0)
    part = lax.all_gather(part, "mp", axis=1, tiled=True)
    return lax.all_gather(part, "dp", axis=0, tiled=True)


def gather_rows(shard, dp, index):
    share = shard.shape[0] // dp
    part = lax.dynamic_slice_in_dim(shard, index * share, share, 0)
    return lax.all_gather(part, ("mp", "dp"), axis=0, tiled=True)


def reduce_columns(grad):
    part = lax.psum_scatter(grad.astype(jnp.bfloat16), "dp", scatter_dimension=0, tiled=True)
    part = lax.psum_scatter(part, "mp", scatter_dimension=1, tiled=True)
    return lax.all_gather(part, "dp", axis=0, tiled=True).astype(jnp.float32)


def reduce_rows(grad, dp, mp):
    share = grad.shape[0] // (dp * mp)
    blocks = grad.astype(jnp.bfloat16).reshape(mp, dp, share, grad.shape[1])
    part = lax.psum_scatter(blocks, "dp", scatter_dimension=1, tiled=False)
    part = lax.psum_scatter(part, "mp", scatter_dimension=0, tiled=False)
    return lax.all_gather(part, "dp", axis=0, tiled=True).astype(jnp.float32)


def local(
    dp,
    mp,
    tokens,
    cotangent,
    norm_gain,
    ema_delta,
    ema_alpha,
    ema_beta,
    ema_eta,
    ema_omega,
    shared_proj,
    query_gain,
    query_bias,
    key_gain,
    value_proj,
    gate_proj,
    mixer_proj,
    update_proj,
    output_proj,
    ffn_gain,
    up_proj,
    down_proj,
):
    width = tokens.shape[1]
    index = lax.axis_index("dp")
    part = lax.axis_index("mp")
    count = tokens.shape[0] // mp
    span = LEN // count
    head_scale = query_gain.shape[0] ** (-0.5)

    x_low = lax.all_to_all(tokens, "mp", 0, 1, tiled=True)
    small = jnp.concatenate(
        [
            ema_delta, ema_alpha, ema_beta, ema_eta,
            norm_gain[:, None], ema_omega[:, None], ffn_gain[:, None],
        ],
        axis=1,
    )
    small = lax.all_gather(small, "mp", axis=0, tiled=True)
    small = small.T
    delta, alpha, beta, eta = (small[NDIM * i : NDIM * (i + 1)] for i in range(4))
    gain = small[4 * NDIM : 4 * NDIM + 1]
    omega = small[4 * NDIM + 1 : 4 * NDIM + 2]
    gain_two = small[4 * NDIM + 2 : 4 * NDIM + 3]
    rate = jax.nn.sigmoid(delta)
    damp = jax.nn.sigmoid(alpha)
    keep = (1.0 - rate * damp).reshape(STATE)
    weight = (rate * beta * eta).reshape(STATE)

    value_all = gather_columns(value_proj, dp, index)
    gate_all = gather_columns(gate_proj, dp, index)
    update_all = gather_columns(update_proj, dp, index)
    mixer_all = gather_columns(mixer_proj, dp, index)
    output_all = gather_rows(output_proj, dp, index)
    up_all = gather_columns(up_proj, dp, index)
    down_all = gather_rows(down_proj, dp, index)
    grad_out = lax.all_to_all(cotangent, "mp", 0, 1, tiled=True)

    xn, ends = norm_ends(x_low, gain, keep)
    forward = [(i, i + 1) for i in range(mp - 1) if (i + 1) % span]
    backward = [(j, i) for i, j in forward]
    starts = lax.ppermute(ends, "mp", forward)
    value_pre = matmul(xn, value_all)
    values = jax.nn.silu(value_pre).astype(jnp.bfloat16)
    mix_pre, xp = ema(xn, keep, weight, omega, starts)

    shared_pre = matmul(xp, shared_proj)
    shared = jax.nn.silu(shared_pre)
    query = (shared * query_gain + query_bias).astype(jnp.bfloat16)
    keys = (shared * key_gain).astype(jnp.bfloat16)
    gate_pre = matmul(xp, gate_all)
    gate = jax.nn.silu(gate_pre)
    scores = group_scores(query, keys)
    peak = jnp.max(scores, axis=-1, keepdims=True)
    weights = jnp.exp(scores - peak)
    probs = weights / jnp.sum(weights, axis=-1, keepdims=True)
    probs_low = probs.astype(jnp.bfloat16)
    blocks = probs.shape[0]
    value_blocks = values.reshape(blocks, GROUP, values.shape[1])
    attended = jnp.einsum(
        "dzc,dcs->dzs", probs_low, value_blocks, preferred_element_type=jnp.float32
    ).reshape(count, values.shape[1])
    hidden = (gate * attended).astype(jnp.bfloat16)
    inputs = x_low.astype(jnp.float32)
    update = jax.nn.sigmoid(matmul(xp, update_all))
    act_pre = matmul(xp, mixer_all) + matmul(hidden, output_all)
    act_value = jax.nn.silu(act_pre)
    middle = update * act_value + (1.0 - update) * inputs
    mean = jnp.mean(middle, axis=1, keepdims=True)
    power = jnp.mean(middle * middle, axis=1, keepdims=True)
    scale_two = lax.rsqrt(power - mean * mean + EPS)
    normed_two = (middle - mean) * scale_two
    ffn_in = (normed_two * gain_two).astype(jnp.bfloat16)
    up_pre = matmul(ffn_in, up_all)
    upper = jax.nn.silu(up_pre).astype(jnp.bfloat16)
    layer_rows = (middle + matmul(upper, down_all)).astype(jnp.bfloat16)
    layer_out = lax.all_to_all(layer_rows, "mp", 1, 0, tiled=True)

    down_grad = reduce_rows(matmul_tn(upper, grad_out), dp, mp)
    d_up_pre = (matmul_nt(grad_out, down_all) * silu_slope(up_pre)).astype(jnp.bfloat16)
    up_grad = reduce_columns(matmul_tn(ffn_in, d_up_pre))
    d_ffn_in = matmul_nt(d_up_pre, up_all)
    ffn_part = jnp.sum(d_ffn_in * normed_two, axis=0)
    scaled = d_ffn_in * gain_two
    first = jnp.mean(scaled, axis=1, keepdims=True)
    second = jnp.mean(scaled * normed_two, axis=1, keepdims=True)
    d_middle = grad_out.astype(jnp.float32) + scale_two * (scaled - first - normed_two * second)

    d_update_pre = (d_middle * (act_value - inputs) * update * (1.0 - update)).astype(jnp.bfloat16)
    d_act_pre = (d_middle * update * silu_slope(act_pre)).astype(jnp.bfloat16)
    d_inputs = d_middle * (1.0 - update)
    output_grad = reduce_rows(matmul_tn(hidden, d_act_pre), dp, mp)
    mixer_grad = reduce_columns(matmul_tn(xp, d_act_pre))
    update_grad = reduce_columns(matmul_tn(xp, d_update_pre))
    d_hidden = matmul_nt(d_act_pre, output_all)
    d_gate_pre = (d_hidden * attended * silu_slope(gate_pre)).astype(jnp.bfloat16)
    d_attended = (d_hidden * gate).astype(jnp.bfloat16).reshape(blocks, GROUP, -1)
    gate_grad = reduce_columns(matmul_tn(xp, d_gate_pre))
    d_probs = jnp.einsum(
        "gas,gcs->gac", d_attended, value_blocks, preferred_element_type=jnp.float32
    )
    d_value = jnp.einsum(
        "uhi,uhs->uis", probs_low, d_attended, preferred_element_type=jnp.float32
    ).reshape(count, values.shape[1])
    d_value_pre = (d_value * silu_slope(value_pre)).astype(jnp.bfloat16)
    value_grad = reduce_columns(matmul_tn(xn, d_value_pre))
    d_scores = probs * (d_probs - jnp.sum(probs * d_probs, axis=-1, keepdims=True))
    d_scores_low = d_scores.astype(jnp.bfloat16)
    query_blocks = query.reshape(blocks, GROUP, -1)
    key_blocks = keys.reshape(blocks, GROUP, -1)
    d_query = (
        jnp.einsum(
            "nqk,nkz->nqz", d_scores_low, key_blocks, preferred_element_type=jnp.float32
        ).reshape(count, -1)
        * head_scale
    )
    d_keys = (
        jnp.einsum(
            "nqk,nqz->nkz", d_scores_low, query_blocks, preferred_element_type=jnp.float32
        ).reshape(count, -1)
        * head_scale
    )
    query_part = jnp.sum(d_query * shared, axis=0)
    bias_part = jnp.sum(d_query, axis=0)
    key_part = jnp.sum(d_keys * shared, axis=0)
    d_shared_pre = ((d_query * query_gain + d_keys * key_gain) * silu_slope(shared_pre)).astype(
        jnp.bfloat16
    )
    shared_part = matmul_tn(xp, d_shared_pre)
    d_mixed = matmul_nt(d_gate_pre, gate_all) + matmul_nt(d_update_pre, update_all)
    d_mixed = d_mixed + matmul_nt(d_act_pre, mixer_all) + matmul_nt(d_shared_pre, shared_proj)
    d_mix_pre = d_mixed * silu_slope(mix_pre)
    normed_part = matmul_nt(d_value_pre, value_all)

    ahead = lax.ppermute(adjoint_start(d_mix_pre, keep), "mp", backward)
    sums, omega_part = ema_params(d_mix_pre, xn, keep, starts)
    token_rows, gain_part = token_grads(
        d_mix_pre, x_low, normed_part, d_inputs, gain, omega, keep, weight, ahead
    )
    token_grad = lax.all_to_all(token_rows, "mp", 1, 0, tiled=True)

    feature = jnp.concatenate(
        [sums.reshape(2 * NDIM, D), omega_part, gain_part, ffn_part[None]], axis=0
    )
    feature, shared_grad, query_grad, bias_grad, key_grad = lax.psum(
        (feature, shared_part, query_part, bias_part, key_part), ("dp", "mp")
    )
    weight_sum = feature[:NDIM]
    keep_sum = feature[NDIM : 2 * NDIM] * weight.reshape(NDIM, D)
    d_rate = weight_sum * beta * eta - keep_sum * damp
    packed = jnp.concatenate(
        [
            d_rate * rate * (1.0 - rate),
            -keep_sum * rate * damp * (1.0 - damp),
            weight_sum * rate * eta,
            weight_sum * rate * beta,
            feature[2 * NDIM :],
        ],
        axis=0,
    )
    mine = lax.dynamic_slice_in_dim(packed, part * width, width, 1).T
    delta_grad, alpha_grad, beta_grad, eta_grad = (
        mine[:, NDIM * i : NDIM * (i + 1)] for i in range(4)
    )
    omega_grad = mine[:, 4 * NDIM]
    gain_grad = mine[:, 4 * NDIM + 1]
    ffn_grad = mine[:, 4 * NDIM + 2]
    return (
        layer_out, token_grad, gain_grad, delta_grad, alpha_grad, beta_grad, eta_grad, omega_grad,
        shared_grad, query_grad, bias_grad, key_grad, value_grad, gate_grad, mixer_grad,
        update_grad, output_grad, ffn_grad, up_grad, down_grad,
    )


def solution(mesh):
    dp, mp = mesh.shape["dp"], mesh.shape["mp"]
    params = (
        P("mp"), P("mp", None), P("mp", None), P("mp", None), P("mp", None), P("mp"),
        P(), P(), P(), P(),
        P(None, "mp"), P(None, "mp"), P(None, "mp"), P(None, "mp"), P("mp", None),
        P("mp"), P(None, "mp"), P("mp", None),
    )
    specs = (P("dp", "mp"), P("dp", "mp")) + params
    return jax.shard_map(
        functools.partial(local, dp, mp), mesh=mesh, in_specs=specs, out_specs=specs, check_vma=False
    )
```

time: 2440 us -> 1380 us (0.57)
  waiting for transfers between devices: 1260 us -> 682 us
  other arithmetic: 370 us -> 51.4 us
  local copies, waits for them, and re-layouts: 253 us -> 43.2 us
  matrix products: 442 us -> 256 us
  blocking collectives: 76.4 us -> 229 us
  Pallas kernels: 0 us -> 75.4 us
    all_gather x10 -> x13, waiting for transfers between devices: 717 us -> 185 us  [the longest x3 61.8 us: reduce_columns(): return lax.all_gather(part, 'dp', axis=0, tiled=True).astype(jnp.float32)]
    scatter-add x2 -> x0, other arithmetic: 199 us -> none  [ema_local(): jnp.take(kernel, jnp.maximum(lag, 0), axis=0)]
    psum x3 -> x1, waiting for transfers between devices: 246 us -> 52.7 us  [local(): lax.psum((feature, shared_part, query_part, bias_part, key_part), ('dp',...]
    all_gather x0 -> x7, blocking collectives: none -> 160 us  [the longest x4 73.2 us: gather_columns(): part = lax.all_gather(part, 'mp', axis=1, tiled=True)]
    dot_general x24 -> x3, matrix products: 177 us -> 18.8 us  [the longest x1 7.16 us: local(): jnp.einsum('uhi,uhs->uis', probs_low, d_attended, preferred_element_type=...]
    all_to_all x0 -> x4, waiting for transfers between devices: none -> 89.5 us  [the longest x1 52.7 us: local(): layer_out = lax.all_to_all(layer_rows, 'mp', 1, 0, tiled=True)]
    gather x2 -> x0, local copies, waits for them, and re-layouts: 85 us -> none  [ema_local(): jnp.take(kernel, jnp.maximum(lag, 0), axis=0)]
    pallas_call x0 -> x5, Pallas kernels: none -> 75.4 us  [the longest x1 25.6 us: ema_params(): pl.pallas_call(ema_params_kernel, grid=(count // TB,), in_specs=[block(),...]
  transfers between devices with their start and end apart: 23 -> 34, of which waited for: 17 -> 21; matrix products, arithmetic and copies ran while one was open for 29% -> 18% of each run, Pallas kernels for 0% -> 5%
where the time goes in v1:
time: 1380 us; the launch traced here: 1370 us
  waiting for transfers between devices  682 us (49%)
  matrix products  256 us (19%)
  blocking collectives  229 us (17%)
  Pallas kernels  75.4 us (5%)
  other arithmetic  51.4 us (4%)
  local copies, waits for them, and re-layouts  43.2 us (3%)
  starting transfers between devices  21.5 us (2%)
  between operations  15.5 us (1%)
    reduce_scatter x5, waiting for transfers between devices, reduce_columns(): lax.psum_scatter(grad.astype(jnp.bfloat16), 'dp', scatter_dimension=0, ti...  120 us
    reduce_scatter x2, waiting for transfers between devices, reduce_rows(): part = lax.psum_scatter(blocks, 'dp', scatter_dimension=1, tiled=False)  110 us
    reduce_scatter x5, waiting for transfers between devices, reduce_columns(): part = lax.psum_scatter(part, 'mp', scatter_dimension=1, tiled=True)  100 us
    dot_general x8, matrix products, matmul(): return jnp.dot(left, right, preferred_element_type=jnp.float32)  91.4 us
    dot_general x8, matrix products, matmul_nt(): lax.dot_general(left, right, (((1,), (1,)), ((), ())), preferred_element_...  74.3 us
    all_gather x4, blocking collectives, gather_columns(): part = lax.all_gather(part, 'mp', axis=1, tiled=True)  73.2 us
    psum x1, blocking collectives, local(): lax.psum((feature, shared_part, query_part, bias_part, key_part), ('dp',...  69 us
    dot_general x8, matrix products, matmul_tn(): lax.dot_general(left, right, (((0,), (0,)), ((), ())), preferred_element_...  68.6 us
  transfers between devices with their start and end apart: 34, of which 21 were waited for; matrix products, arithmetic and copies ran while one was open for 18% of the time, Pallas kernels for 5%

profile of v1, /device:TPU:0, one launch (start us, length us, event | category | flops | bytes accessed | tf_op | source)
XLA Modules:
  0.0 1373.7 jit_solution(11560461754523194187)
XLA Ops:
  10.5 22.2 %all_gather.67 = bf16[128,2048]{1,0:T(8,128)(2,1)} all-gather(bf16[128,512]{1,0:T(8,128)(2,1)S(1)} %constant_dynamic-slice_fusion.3), channel_id=1, replica_groups=mesh['dp'=8,'mp'=4] {'mp'}, dimensions={1}, use_global_device_ids=true | all-gather | bytes 655360 | tf_op jit(solution)/shard_map/all_gather | solution.py:328
  33.7 21.3 %all_gather.65 = bf16[128,2048]{1,0:T(8,128)(2,1)} all-gather(bf16[128,512]{1,0:T(8,128)(2,1)S(1)} %constant_dynamic-slice_fusion.4), channel_id=1, replica_groups=mesh['dp'=8,'mp'=4] {'mp'}, dimensions={1}, use_global_device_ids=true | all-gather | bytes 655360 | tf_op jit(solution)/shard_map/all_gather | solution.py:328
  57.6 14.6 %all_gather.63 = bf16[128,1024]{1,0:T(8,128)(2,1)} all-gather(bf16[128,256]{1,0:T(8,128)(2,1)S(1)} %constant_dynamic-slice_fusion.5), channel_id=1, replica_groups=mesh['dp'=8,'mp'=4] {'mp'}, dimensions={1}, use_global_device_ids=true | all-gather | bytes 327680 | tf_op jit(solution)/shard_map/all_gather | solution.py:328
  73.1 15.1 %all_gather.61 = bf16[128,1024]{1,0:T(8,128)(2,1)} all-gather(bf16[128,256]{1,0:T(8,128)(2,1)S(1)} %constant_dynamic-slice_fusion.6), channel_id=1, replica_groups=mesh['dp'=8,'mp'=4] {'mp'}, dimensions={1}, use_global_device_ids=true | all-gather | bytes 327680 | tf_op jit(solution)/shard_map/all_gather | solution.py:328
  94.6 36.8 %all-to-all-done = bf16[4,1024,256]{2,1,0:T(8,128)(2,1)S(1)} async-done(((bf16[4,1024,256]{2,1,0:T(8,128)(2,1)}), bf16[4,1024,256]{2,1,0:T(8,128)(2,1)S(1)}, u32[]{:S(2)}, u32[]{:S(2)}) %all-to-all-start) | async-done | bytes 2097184 | tf_op jit(solution)/shard_map/all_to_all | solution.py:383
  131.4 4.5 all-to-all-start.2
  136.0 66.8 %all_gather.60 = f32[1024,67]{0,1:T(8,128)S(1)} all-gather(f32[256,67]{0,1:T(8,128)S(1)} %concatenate.9), channel_id=1, replica_groups=mesh['dp'=8,'mp'=4] {'mp'}, dimensions={0}, use_global_device_ids=true | all-gather | bytes 343040 | tf_op jit(solution)/shard_map/all_gather | solution.py:391
  205.6 13.3 norm_ends.1
  225.4 13.9 %ema.1 = (f32[1024,1024]{1,0:T(8,128)S(1)}, bf16[1024,1024]{1,0:T(8,128)(2,1)S(1)}) custom-call(bf16[1024,1024]{1,0:T(8,128)(2,1)S(1)} %copy-done.4, f32[16,8,128]{2,1,0:T(8,128)S(1)} %bitcast.160, f32[16,8,128]{2,1,0:T(8,128)S(1)} %bitcast.165, f32[1,1024]{1,0:T(1,128)S(1)} %get-tuple-element.59.omega_ref, f32[32,8,128]{2,1,0:T(8,128)S(1)} %collective-permute-done.start_ref), custom_call_target="tpu_custom_call" | custom-call | flops 67108864 | bytes 8388608 | tf_op jit(solution)/shard_map/ema/pallas_call | solution.py:253
  244.2 12.6 multiply_convert_fusion.2
  256.8 6.8 fusion.26
  263.6 15.2 %fusion.3 = (bf16[1024,2048]{1,0:T(8,128)(2,1)}, f32[1024,2048]{1,0:T(8,128)}) fusion(f32[8,128,2048]{2,1,0:T(8,128)} %fusion.26, bf16[1024,1024]{1,0:T(8,128)(2,1)} %copy-done.7, bf16[1024,2048]{1,0:T(8,128)(2,1)} %all-gather.20.cloned.1.call-done), kind=kOutput, calls=%fused_computation.9 | convolution fusion | flops 4307550208 | bytes 27262976 | tf_op jit(solution)/shard_map/dot_general | solution.py:21
  278.8 10.1 fusion.42
  288.9 7.8 convolution_add_fusion
  296.7 10.3 fusion.36
  307.0 13.4 all-gather.28.cloned.1.call-done
  320.4 19.6 %multiply_convert_fusion = (bf16[1024,4096]{1,0:T(8,128)(2,1)}, f32[1024,4096]{1,0:T(8,128)}) fusion(bf16[1024,4096]{1,0:T(8,128)(2,1)} %all-gather.28.cloned.1.call-done, f32[1024,1024]{1,0:T(8,128)} %get-tuple-element.50, f32[1024]{0:T(1024)S(1)} %bitcast.197, f32[1024]{0:T(1024)S(1)} %get-tuple-element.71, f32[1024]{0:T(1024)S(1)} %get-tuple-element.70), kind=kOutput, calls=%fused_computation.3 | convolution fusion | flops 8615100416 | bytes 37761024 | tf_op jit(solution)/shard_map/dot_general | solution.py:21
  339.9 61.4 %all-gather.30.cloned.1.call-done = bf16[4096,1024]{1,0:T(8,128)(2,1)} async-done(((bf16[128,1024]{1,0:T(8,128)(2,1)}), bf16[4096,1024]{1,0:T(8,128)(2,1)}) %all-gather.30.cloned.1.call-update) | async-done | bytes 8388624 | tf_op jit(solution)/shard_map/all_gather | solution.py:335
  401.3 19.5 %fusion.1 = bf16[1024,4096]{1,0:T(8,128)(2,1)} fusion(f32[1024,4096]{1,0:T(8,128)} %get-tuple-element.81, bf16[4096,1024]{1,0:T(8,128)(2,1)} %all-gather.30.cloned.1.call-done, bf16[1024,1024]{1,0:T(8,128)(2,1)} %bitcast.173), kind=kOutput, calls=%fused_computation.2 | convolution fusion | flops 8627683328 | bytes 35651584 | tf_op jit(solution)/shard_map/dot_general | solution.py:31
  420.9 16.6 %multiply_reduce_fusion = (f32[1024]{0:T(1024)}, f32[1024]{0:T(1024)S(1)}, f32[1024]{0:T(1024)S(1)}, f32[1024,1024]{1,0:T(8,128)}) fusion(f32[1024,1024]{1,0:T(8,128)S(1)} %copy-done.23, f32[1024]{0:T(1024)S(1)} %get-tuple-element.71, f32[1024]{0:T(1024)S(1)} %get-tuple-element.70, f32[1024]{0:T(1024)S(1)} %bitcast.198, bf16[1024,4096]{1,0:T(8,128)(2,1)} %fusion.1, ...), kind=kOutput, calls=%fused_computation.26 | convolution fusion | flops 8598320128 | bytes 25190400 | tf_op jit(solution)/shard_map/dot_general | solution.py:31
  437.5 5.1 subtract_multiply_fusion.1
  446.9 13.8 %fusion.5 = (bf16[1024,2048]{1,0:T(8,128)(2,1)}, bf16[1024,2048]{1,0:T(8,128)(2,1)}) fusion(f32[8,128,2048]{2,1,0:T(8,128)} %fusion.26, f32[1024,2048]{1,0:T(8,128)} %get-tuple-element.78, bf16[1024,1024]{1,0:T(8,128)(2,1)S(1)} %get-tuple-element.54, bf16[2048,1024]{1,0:T(8,128)(2,1)S(1)} %copy-done.51), kind=kOutput, calls=%fused_computation.11 | convolution fusion | flops 4322230272 | bytes 31457280 | tf_op jit(solution)/shard_map/dot_general | solution.py:31
  460.8 7.2 fusion.24
  467.9 7.5 fusion.2
  477.3 6.2 convolution_convert_fusion.4
  483.8 9.4 convolution_convert_fusion.3
  493.2 7.9 convolution_convert_fusion.2
  503.9 16.0 %convolution_convert_fusion.1 = bf16[1024,4096]{1,0:T(8,128)(2,1)} fusion(bf16[1024,4096]{1,0:T(8,128)(2,1)} %fusion.1, f32[1024,1024]{1,0:T(8,128)} %get-tuple-element.50, f32[1024]{0:T(1024)S(1)} %bitcast.200, f32[1024]{0:T(1024)S(1)} %get-tuple-element.71, f32[1024]{0:T(1024)S(1)} %get-tuple-element.70), kind=kOutput, calls=%fused_computation.18 | convolution fusion | flops 8598323200 | bytes 20983808 | tf_op jit(solution)/shard_map/dot_general | solution.py:25
  520.0 15.0 %convolution_convert_fusion = bf16[4096,1024]{1,0:T(8,128)(2,1)} fusion(bf16[1024,4096]{1,0:T(8,128)(2,1)} %get-tuple-element.80, bf16[1024,1024]{1,0:T(8,128)(2,1)} %bitcast.174), kind=kOutput, calls=%fused_computation.17 | convolution fusion | flops 8594128896 | bytes 18874368 | tf_op jit(solution)/shard_map/dot_general | solution.py:25
  535.0 8.3 copy.71
  543.9 6.5 convolution_convert_fusion.6
  550.4 6.1 convolution_convert_fusion.5
  557.2 31.4 %reduce-scatter.19.cloned.1.call-done = bf16[128,2048]{1,0:T(8,128)(2,1)} async-done(((bf16[1024,2048]{1,0:T(8,128)(2,1)}), bf16[128,2048]{1,0:T(8,128)(2,1)}) %reduce-scatter.19.cloned.1.call-update) | async-done | bytes 524304 | tf_op jit(solution)/shard_map/reduce_scatter | solution.py:339
  588.7 4.8 multiply_reduce_fusion.5
  593.6 50.3 %reduce-scatter.31.cloned.1.call-done = bf16[4,1,64,1024]{3,2,0,1:T(8,128)(2,1)} async-done(((bf16[4,8,64,1024]{3,2,0,1:T(8,128)(2,1)}), bf16[4,1,64,1024]{3,2,0,1:T(8,128)(2,1)}) %reduce-scatter.31.cloned.1.call-update) | async-done | bytes 524304 | tf_op jit(solution)/shard_map/reduce_scatter | solution.py:347
  646.2 6.6 fusion.44
  652.9 66.0 %reduce-scatter.35.cloned.1.call-done = bf16[128,4096]{1,0:T(8,128)(2,1)} async-done(((bf16[1024,4096]{1,0:T(8,128)(2,1)}), bf16[128,4096]{1,0:T(8,128)(2,1)}) %reduce-scatter.35.cloned.1.call-update) | async-done | bytes 1048592 | tf_op jit(solution)/shard_map/reduce_scatter | solution.py:339
  723.4 4.4 fusion.45
  727.8 6.1 fusion.43
  733.9 59.7 %reduce-scatter.39.cloned.1.call-done = bf16[4,1,128,1024]{3,2,0,1:T(8,128)(2,1)} async-done(((bf16[4,8,128,1024]{3,2,0,1:T(8,128)(2,1)}), bf16[4,1,128,1024]{3,2,0,1:T(8,128)(2,1)}) %reduce-scatter.39.cloned.1.call-update) | async-done | bytes 1048592 | tf_op jit(solution)/shard_map/reduce_scatter | solution.py:347
  793.7 8.5 multiply_multiply_fusion.grad_ref
  802.2 6.0 adjoint_start.1
  809.9 4.5 fusion.49.normed_ref
  816.0 25.6 %ema_params.1 = (f32[32,8,128]{2,1,0:T(8,128)S(1)}, f32[1,1024]{1,0:T(1,128)S(1)}) custom-call(f32[1024,1024]{1,0:T(8,128)S(1)} %multiply_multiply_fusion.grad_ref, bf16[1024,1024]{1,0:T(8,128)(2,1)S(1)} %copy-done.6, f32[16,8,128]{2,1,0:T(8,128)S(1)} %bitcast.162, f32[32,8,128]{2,1,0:T(8,128)S(1)} %collective-permute-done.start_ref), custom_call_target="tpu_custom_call" | custom-call | flops 134217728 | bytes 6291456 | tf_op jit(solution)/shard_map/ema_params/pallas_call | solution.py:283
  841.8 16.5 %token_grads.1 = (bf16[1024,1024]{1,0:T(8,128)(2,1)S(1)}, f32[1,1024]{1,0:T(1,128)S(1)}) custom-call(f32[1024,1024]{1,0:T(8,128)S(1)} %multiply_multiply_fusion.grad_ref, bf16[1024,1024]{1,0:T(8,128)(2,1)S(1)} %bitcast.158, f32[1024,1024]{1,0:T(8,128)S(1)} %fusion.49.normed_ref, f32[1024,1024]{1,0:T(8,128)S(1)} %copy-done.2, f32[1,1024]{1,0:T(1,128)S(1)} %copy-done.13, ...), custom_call_target="tpu_custom_call" | custom-call | flops 67108864 | bytes 14680064 | tf_op jit(solution)/shard_map/token_grads/pallas_call | solution.py:299
  861.1 22.3 %reduce-scatter.27.cloned.1.call-done = bf16[128,1024]{1,0:T(8,128)(2,1)} async-done(((bf16[1024,1024]{1,0:T(8,128)(2,1)}), bf16[128,1024]{1,0:T(8,128)(2,1)}) %reduce-scatter.27.cloned.1.call-update) | async-done | bytes 262160 | tf_op jit(solution)/shard_map/reduce_scatter | solution.py:339
  883.4 23.8 %reduce-scatter.17.cloned.1.call-done = bf16[128,512]{1,0:T(8,128)(2,1)} async-done(((bf16[128,2048]{1,0:T(8,128)(2,1)}), bf16[128,512]{1,0:T(8,128)(2,1)}) %reduce-scatter.17.cloned.1.call-update) | async-done | bytes 131088 | tf_op jit(solution)/shard_map/reduce_scatter | solution.py:340
  907.3 22.1 %reduce-scatter.21.cloned.1.call-done = bf16[128,512]{1,0:T(8,128)(2,1)} async-done(((bf16[128,2048]{1,0:T(8,128)(2,1)}), bf16[128,512]{1,0:T(8,128)(2,1)}) %reduce-scatter.21.cloned.1.call-update) | async-done | bytes 131088 | tf_op jit(solution)/shard_map/reduce_scatter | solution.py:340
  929.5 22.2 %reduce-scatter.33.cloned.1.call-done = bf16[1,64,1024]{2,1,0:T(8,128)(2,1)} async-done(((bf16[4,64,1024]{2,1,0:T(8,128)(2,1)}), bf16[1,64,1024]{2,1,0:T(8,128)(2,1)}) %reduce-scatter.33.cloned.1.call-update) | async-done | bytes 131088 | tf_op jit(solution)/shard_map/reduce_scatter | solution.py:348
  951.8 27.8 %reduce-scatter.37.cloned.1.call-done = bf16[128,1024]{1,0:T(8,128)(2,1)} async-done(((bf16[128,4096]{1,0:T(8,128)(2,1)}), bf16[128,1024]{1,0:T(8,128)(2,1)}) %reduce-scatter.37.cloned.1.call-update) | async-done | bytes 262160 | tf_op jit(solution)/shard_map/reduce_scatter | solution.py:340
  979.6 14.3 %add_convert_fusion = bf16[1024,1024]{1,0:T(8,128)(2,1)S(1)} fusion(f32[1024,1024]{1,0:T(8,128)} %get-tuple-element.50, bf16[1024,4096]{1,0:T(8,128)(2,1)} %get-tuple-element.80, bf16[4096,1024]{1,0:T(8,128)(2,1)} %all-gather.30.cloned.1.call-done), kind=kOutput, calls=%fused_computation.31 | convolution fusion | flops 8592031744 | bytes 23068672 | tf_op jit(solution)/shard_map/dot_general | solution.py:21
  995.4 4.5 all-to-all-start.1
  1001.3 52.7 %all-to-all-done.1 = bf16[1024,4,256]{2,0,1:T(8,128)(2,1)} async-done(((bf16[1024,4,256]{2,0,1:T(8,128)(2,1)}), bf16[1024,4,256]{2,0,1:T(8,128)(2,1)}, u32[]{:S(2)}, u32[]{:S(2)}) %all-to-all-start.1) | async-done | bytes 2097184 | tf_op jit(solution)/shard_map/all_to_all | solution.py:449
  1058.7 69.0 %all-reduce = (f32[128]{0:T(128)}, f32[128]{0:T(128)}, f32[128]{0:T(128)}) all-reduce(f32[128]{0:T(128)S(1)} %get-tuple-element.42, f32[128]{0:T(128)S(1)} %multiply_reduce_fusion.4, f32[128]{0:T(128)S(1)} %get-tuple-element.41), channel_id=1, replica_groups=mesh['dp'=8,'mp'=4] {'dp','mp'}, use_global_device_ids=true, to_apply=%region_11.12 | all-reduce | flops 384 | bytes 3072 | tf_op jit(solution)/shard_map/psum | solution.py:517
  1127.7 52.7 %all-reduce.4.cloned.1.call-done = (f32[35,1024]{1,0:T(8,128)}, f32[1024,128]{1,0:T(8,128)}) async-done(((f32[35,1024]{1,0:T(8,128)}, f32[1024,128]{1,0:T(8,128)}), (f32[35,1024]{1,0:T(8,128)}, f32[1024,128]{1,0:T(8,128)})) %all-reduce.4.cloned.1.call-update) | async-done | bytes 667664 | tf_op jit(solution)/shard_map/psum | solution.py:517
  1185.9 17.3 %reduce-scatter.25.cloned.1.call-done = bf16[128,256]{1,0:T(8,128)(2,1)} async-done(((bf16[128,1024]{1,0:T(8,128)(2,1)}), bf16[128,256]{1,0:T(8,128)(2,1)}) %reduce-scatter.25.cloned.1.call-update) | async-done | bytes 65552 | tf_op jit(solution)/shard_map/reduce_scatter | solution.py:340
  1203.2 10.2 all_gather.75
  1214.4 9.1 reduce-scatter.29.cloned.1.call-done
  1223.5 10.1 all_gather.76
  1234.7 12.4 all-gather.32.cloned.1.call-done
  1249.9 22.6 %all-gather.34.cloned.1.call-done = bf16[1024,512]{1,0:T(8,128)(2,1)} async-done(((bf16[128,512]{1,0:T(8,128)(2,1)}), bf16[1024,512]{1,0:T(8,128)(2,1)}) %all-gather.34.cloned.1.call-update) | async-done | bytes 1048592 | tf_op jit(solution)/shard_map/all_gather | solution.py:341
  1275.3 22.4 %all-gather.38.cloned.1.call-done = bf16[1,512,1024]{2,1,0:T(8,128)(2,1)} async-done(((bf16[1,64,1024]{2,1,0:T(8,128)(2,1)}), bf16[1,512,1024]{2,1,0:T(8,128)(2,1)}) %all-gather.38.cloned.1.call-update) | async-done | bytes 1048592 | tf_op jit(solution)/shard_map/all_gather | solution.py:349
  1300.5 26.9 %all-gather.36.cloned.1.call-done = bf16[1024,1024]{1,0:T(8,128)(2,1)} async-done(((bf16[128,1024]{1,0:T(8,128)(2,1)}), bf16[1024,1024]{1,0:T(8,128)(2,1)}) %all-gather.36.cloned.1.call-update) | async-done | bytes 2097168 | tf_op jit(solution)/shard_map/all_gather | solution.py:341
  1331.4 25.7 %all-gather.40.cloned.1.call-done = bf16[1,1024,1024]{2,1,0:T(8,128)(2,1)} async-done(((bf16[1,128,1024]{2,1,0:T(8,128)(2,1)}), bf16[1,1024,1024]{2,1,0:T(8,128)(2,1)}) %all-gather.40.cloned.1.call-update) | async-done | bytes 2097168 | tf_op jit(solution)/shard_map/all_gather | solution.py:349
  (236 shorter events, 89.0 us)
Async XLA Ops:
  7.2 81.1 %all-gather.26.cloned.1.call-start = ((), (), s32[]{:S(2)}) async-start(), calls=%async_computation.23 | async-start | bytes 1310720 | tf_op jit(solution)/shard_map/all_gather | solution.py:328
  9.5 234.6 %all-gather.22.cloned.1.call-start = ((), (), s32[]{:S(2)}) async-start(), calls=%async_computation.21 | async-start | bytes 4718592 | tf_op jit(solution)/shard_map/all_gather | solution.py:329
  32.8 230.9 %all-gather.20.cloned.1.call-start = ((), (), s32[]{:S(2)}) async-start(), calls=%async_computation.20 | async-start | bytes 4718592 | tf_op jit(solution)/shard_map/all_gather | solution.py:329
  55.0 223.8 %all-gather.24.cloned.1.call-start = ((), (), s32[]{:S(2)}) async-start(), calls=%async_computation.22 | async-start | bytes 4325376 | tf_op jit(solution)/shard_map/all_gather | solution.py:335
  56.7 232.3 %all-gather.18.cloned.1.call-start = ((), (), s32[]{:S(2)}) async-start(), calls=%async_computation.19 | async-start | bytes 2359296 | tf_op jit(solution)/shard_map/all_gather | solution.py:329
  72.2 224.5 %all-gather.16.cloned.1.call-start = ((), (), s32[]{:S(2)}) async-start(), calls=%async_computation.18 | async-start | bytes 2359296 | tf_op jit(solution)/shard_map/all_gather | solution.py:329
  88.2 232.1 %all-gather.28.cloned.1.call-start = ((), (), s32[]{:S(2)}) async-start(), calls=%async_computation.24 | async-start | bytes 9437184 | tf_op jit(solution)/shard_map/all_gather | solution.py:329
  89.0 46.9 %copy-start.37 = (f32[256,16]{0,1:T(8,128)S(1)}, f32[256,16]{0,1:T(8,128)}, u32[]{:S(2)}) copy-start(f32[256,16]{0,1:T(8,128)} %param.23) | copy-start | bytes 49156
  89.0 46.9 %copy-start.38 = (f32[256,16]{0,1:T(8,128)S(1)}, f32[256,16]{0,1:T(8,128)}, u32[]{:S(2)}) copy-start(f32[256,16]{0,1:T(8,128)} %param.24) | copy-start | bytes 49156
  89.0 46.9 %copy-start.39 = (f32[256,16]{0,1:T(8,128)S(1)}, f32[256,16]{0,1:T(8,128)}, u32[]{:S(2)}) copy-start(f32[256,16]{0,1:T(8,128)} %param.25) | copy-start | bytes 49156
  89.0 46.9 %copy-start.40 = (f32[256,16]{0,1:T(8,128)S(1)}, f32[256,16]{0,1:T(8,128)}, u32[]{:S(2)}) copy-start(f32[256,16]{0,1:T(8,128)} %param.26) | copy-start | bytes 49156
  89.0 46.9 %copy-start.42 = (f32[256]{0:T(256)S(1)}, f32[256]{0:T(256)}, u32[]{:S(2)}) copy-start(f32[256]{0:T(256)} %param.22) | copy-start | bytes 3076
  89.0 46.9 %copy-start.43 = (f32[256]{0:T(256)S(1)}, f32[256]{0:T(256)}, u32[]{:S(2)}) copy-start(f32[256]{0:T(256)} %param.27) | copy-start | bytes 3076
  89.1 46.9 %copy-start.44 = (f32[256]{0:T(256)S(1)}, f32[256]{0:T(256)}, u32[]{:S(2)}) copy-start(f32[256]{0:T(256)} %param.37) | copy-start | bytes 3076
  89.1 42.3 %all-to-all-start = ((bf16[4,1024,256]{2,1,0:T(8,128)(2,1)}), bf16[4,1024,256]{2,1,0:T(8,128)(2,1)S(1)}, u32[]{:S(2)}, u32[]{:S(2)}) async-start(bf16[4,1024,256]{2,1,0:T(8,128)(2,1)} %bitcast.187), calls=%async_computation | async-start | bytes 4194304 | tf_op jit(solution)/shard_map/all_to_all | solution.py:383
  92.8 308.5 %all-gather.30.cloned.1.call-start = ((), (), s32[]{:S(2)}) async-start(), calls=%async_computation.25 | async-start | bytes 8650752 | tf_op jit(solution)/shard_map/all_gather | solution.py:335
  131.4 71.5 %copy-start.17 = (bf16[4,1024,256]{2,1,0:T(8,128)(2,1)}, bf16[4,1024,256]{2,1,0:T(8,128)(2,1)S(1)}, u32[]{:S(2)}) copy-start(bf16[4,1024,256]{2,1,0:T(8,128)(2,1)S(1)} %all-to-all-done) | copy-start | bytes 6291460
  131.4 90.6 %all-to-all-start.2 = ((bf16[4,1024,256]{2,1,0:T(8,128)(2,1)}), bf16[4,1024,256]{2,1,0:T(8,128)(2,1)}, u32[]{:S(2)}, u32[]{:S(2)}) async-start(bf16[4,1024,256]{2,1,0:T(8,128)(2,1)} %bitcast.188), calls=%async_computation.2 | async-start | bytes 4194304 | tf_op jit(solution)/shard_map/all_to_all | solution.py:409
  135.9 420.8 %reduce-scatter.15.cloned.1.call-start = ((), (), s32[]{:S(2)}) async-start(), calls=%async_computation.26 | async-start | bytes 4718592 | tf_op jit(solution)/shard_map/reduce_scatter | solution.py:339
  203.6 18.4 %copy-start.12 = (f32[1,1024]{1,0:T(1,128)}, f32[1,1024]{1,0:T(1,128)S(1)}, u32[]{:S(2)}) copy-start(f32[1,1024]{1,0:T(1,128)S(1)} %get-tuple-element.60.gain_ref) | copy-start | bytes 12292
  205.6 35.0 %copy-start.33 = (bf16[1024,128]{1,0:T(8,128)(2,1)S(1)}, bf16[1024,128]{1,0:T(8,128)(2,1)}, u32[]{:S(2)}) copy-start(bf16[1024,128]{1,0:T(8,128)(2,1)} %param.28) | copy-start | bytes 786436
  205.6 35.0 %copy-start.45 = (f32[128]{0:T(128)S(1)}, f32[128]{0:T(128)}, u32[]{:S(2)}) copy-start(f32[128]{0:T(128)} %param.31) | copy-start | bytes 1540
  205.6 35.0 %copy-start.47 = (f32[128]{0:T(128)S(1)}, f32[128]{0:T(128)}, u32[]{:S(2)}) copy-start(f32[128]{0:T(128)} %param.29) | copy-start | bytes 1540
  205.6 35.0 %copy-start.53 = (f32[128]{0:T(128)S(1)}, f32[128]{0:T(128)}, u32[]{:S(2)}) copy-start(f32[128]{0:T(128)} %param.30) | copy-start | bytes 1540
  220.3 5.1 collective-permute-start
  243.2 13.6 copy-start.25
  401.3 19.5 %copy-start.23 = (f32[1024,1024]{1,0:T(8,128)S(1)}, f32[1024,1024]{1,0:T(8,128)}, u32[]{:S(2)}) copy-start(f32[1024,1024]{1,0:T(8,128)} %get-tuple-element.50) | copy-start | bytes 12582916
  420.8 16.7 %copy-start.14 = (f32[1024,1024]{1,0:T(8,128)S(1)}, f32[1024,1024]{1,0:T(8,128)}, u32[]{:S(2)}) copy-start(f32[1024,1024]{1,0:T(8,128)} %get-tuple-element.79) | copy-start | bytes 12582916
  420.9 16.7 %copy-start.18 = (bf16[4,128,8,256]{3,2,0,1:T(8,128)(2,1)S(1)}, bf16[4,128,8,256]{3,2,0,1:T(8,128)(2,1)}, u32[]{:S(2)}) copy-start(bf16[4,128,8,256]{3,2,0,1:T(8,128)(2,1)} %copy.83) | copy-start | bytes 6291460
  446.9 13.8 %copy-start.26 = (bf16[1024,1024]{1,0:T(8,128)(2,1)}, bf16[1024,1024]{1,0:T(8,128)(2,1)S(1)}, u32[]{:S(2)}) copy-start(bf16[1024,1024]{1,0:T(8,128)(2,1)S(1)} %get-tuple-element.54) | copy-start | bytes 6291460
  446.9 13.8 %copy-start.36 = (f32[8,128]{1,0:T(8,128)S(1)}, f32[8,128]{1,0:T(8,128)}, u32[]{:S(2)}) copy-start(f32[8,128]{1,0:T(8,128)} %copy-done.35) | copy-start | bytes 12292
  483.6 105.0 %reduce-scatter.19.cloned.1.call-start = ((), (), s32[]{:S(2)}) async-start(), calls=%async_computation.29 | async-start | bytes 4718592 | tf_op jit(solution)/shard_map/reduce_scatter | solution.py:339
  493.2 150.7 %reduce-scatter.31.cloned.1.call-start = ((), (), s32[]{:S(2)}) async-start(), calls=%async_computation.36 | async-start | bytes 4718592 | tf_op jit(solution)/shard_map/reduce_scatter | solution.py:347
  503.6 215.3 %reduce-scatter.35.cloned.1.call-start = ((), (), s32[]{:S(2)}) async-start(), calls=%async_computation.38 | async-start | bytes 9437184 | tf_op jit(solution)/shard_map/reduce_scatter | solution.py:339
  520.0 273.7 %reduce-scatter.39.cloned.1.call-start = ((), (), s32[]{:S(2)}) async-start(), calls=%async_computation.41 | async-start | bytes 9437184 | tf_op jit(solution)/shard_map/reduce_scatter | solution.py:347
  543.4 317.0 %reduce-scatter.23.cloned.1.call-start = ((), (), s32[]{:S(2)}) async-start(), calls=%async_computation.32 | async-start | bytes 2359296 | tf_op jit(solution)/shard_map/reduce_scatter | solution.py:339
  550.4 333.0 %reduce-scatter.27.cloned.1.call-start = ((), (), s32[]{:S(2)}) async-start(), calls=%async_computation.34 | async-start | bytes 2359296 | tf_op jit(solution)/shard_map/reduce_scatter | solution.py:339
  550.4 38.3 %copy-start.46 = (f32[128]{0:T(128)S(1)}, f32[128]{0:T(128)}, u32[]{:S(2)}) copy-start(f32[128]{0:T(128)} %param.31) | copy-start | bytes 1540
  550.4 38.3 %copy-start.48 = (f32[128]{0:T(128)S(1)}, f32[128]{0:T(128)}, u32[]{:S(2)}) copy-start(f32[128]{0:T(128)} %param.29) | copy-start | bytes 1540
  550.4 38.3 %copy-start.28 = (f32[8,128,128]{1,2,0:T(8,128)S(1)}, f32[8,128,128]{1,2,0:T(8,128)}, u32[]{:S(2)}) copy-start(f32[8,128,128]{1,2,0:T(8,128)} %get-tuple-element.76) | copy-start | bytes 1572868
  556.6 350.7 %reduce-scatter.17.cloned.1.call-start = ((), (), s32[]{:S(2)}) async-start(), calls=%async_computation.27 | async-start | bytes 655360 | tf_op jit(solution)/shard_map/reduce_scatter | solution.py:340
  557.1 372.3 %reduce-scatter.21.cloned.1.call-start = ((), (), s32[]{:S(2)}) async-start(), calls=%async_computation.30 | async-start | bytes 655360 | tf_op jit(solution)/shard_map/reduce_scatter | solution.py:340
  588.6 363.1 %reduce-scatter.33.cloned.1.call-start = ((), (), s32[]{:S(2)}) async-start(), calls=%async_computation.37 | async-start | bytes 655360 | tf_op jit(solution)/shard_map/reduce_scatter | solution.py:348
  588.7 56.5 %copy-start.30 = (bf16[1024,128]{1,0:T(8,128)(2,1)S(1)}, bf16[1024,128]{1,0:T(8,128)(2,1)}, u32[]{:S(2)}) copy-start(bf16[1024,128]{1,0:T(8,128)(2,1)} %copy-done.29) | copy-start | bytes 786436
  643.9 335.6 %reduce-scatter.37.cloned.1.call-start = ((), (), s32[]{:S(2)}) async-start(), calls=%async_computation.39 | async-start | bytes 1310720 | tf_op jit(solution)/shard_map/reduce_scatter | solution.py:340
  646.2 74.5 %copy-start.34 = (bf16[1024,128]{1,0:T(8,128)(2,1)S(1)}, bf16[1024,128]{1,0:T(8,128)(2,1)}, u32[]{:S(2)}) copy-start(bf16[1024,128]{1,0:T(8,128)(2,1)} %param.28) | copy-start | bytes 786436
  718.9 338.8 %reduce-scatter.41.cloned.1.call-start = ((), (), s32[]{:S(2)}) async-start(), calls=%async_computation.42 | async-start | bytes 1310720 | tf_op jit(solution)/shard_map/reduce_scatter | solution.py:348
  793.7 386.7 %all-reduce.4.cloned.1.call-start = ((), (), s32[]{:S(2)}) async-start(), calls=%async_computation.45 | async-start | bytes 1376256 | tf_op jit(solution)/shard_map/psum | solution.py:517
  793.7 16.2 %copy-start.49 = (bf16[1024,2048]{1,0:T(8,128)(2,1)S(1)}, bf16[1024,2048]{1,0:T(8,128)(2,1)}, u32[]{:S(2)}) copy-start(bf16[1024,2048]{1,0:T(8,128)(2,1)} %all-gather.22.cloned.1.call-done) | copy-start | bytes 12582916
  808.3 33.4 %collective-permute-start.1 = (f32[16,8,128]{2,1,0:T(8,128)S(1)}, f32[16,8,128]{2,1,0:T(8,128)S(1)}, u32[]{:S(2)}, u32[]{:S(2)}) collective-permute-start(f32[16,8,128]{2,1,0:T(8,128)S(1)} %adjoint_start.1), channel_id=1, source_target_pairs={{1,0},{3,2},{5,4},{7,6},{9,8},{11,10},{13,12},{15,14},{17,16},{19,... | collective-permute-start | bytes 196616 | tf_op jit(solution)/shard_map/ppermute | solution.py:507
  816.0 25.7 %copy-start.2 = (f32[1024,1024]{1,0:T(8,128)S(1)}, f32[1024,1024]{1,0:T(8,128)}, u32[]{:S(2)}) copy-start(f32[1024,1024]{1,0:T(8,128)} %get-tuple-element.48.direct_ref) | copy-start | bytes 12582916
  816.0 25.7 %copy-start.13 = (f32[1,1024]{1,0:T(1,128)S(1)}, f32[1,1024]{1,0:T(1,128)}, u32[]{:S(2)}) copy-start(f32[1,1024]{1,0:T(1,128)} %copy-done.12) | copy-start | bytes 12292
  841.7 17.8 %copy-start.41 = (f32[1024]{0:T(1024)S(1)}, f32[1024]{0:T(1024)}, u32[]{:S(2)}) copy-start(f32[1024]{0:T(1024)} %get-tuple-element.36) | copy-start | bytes 12292
  860.3 342.9 %reduce-scatter.25.cloned.1.call-start = ((), (), s32[]{:S(2)}) async-start(), calls=%async_computation.33 | async-start | bytes 327680 | tf_op jit(solution)/shard_map/reduce_scatter | solution.py:340
  861.0 362.5 %reduce-scatter.29.cloned.1.call-start = ((), (), s32[]{:S(2)}) async-start(), calls=%async_computation.35 | async-start | bytes 327680 | tf_op jit(solution)/shard_map/reduce_scatter | solution.py:340
  883.4 363.7 %all-gather.32.cloned.1.call-start = ((), (), s32[]{:S(2)}) async-start(), calls=%async_computation.28 | async-start | bytes 1179648 | tf_op jit(solution)/shard_map/all_gather | solution.py:341
  907.3 365.2 %all-gather.34.cloned.1.call-start = ((), (), s32[]{:S(2)}) async-start(), calls=%async_computation.31 | async-start | bytes 1179648 | tf_op jit(solution)/shard_map/all_gather | solution.py:341
  929.5 368.2 %all-gather.38.cloned.1.call-start = ((), (), s32[]{:S(2)}) async-start(), calls=%async_computation.43 | async-start | bytes 1179648 | tf_op jit(solution)/shard_map/all_gather | solution.py:349
  951.7 375.7 %all-gather.36.cloned.1.call-start = ((), (), s32[]{:S(2)}) async-start(), calls=%async_computation.40 | async-start | bytes 2359296 | tf_op jit(solution)/shard_map/all_gather | solution.py:341
  995.4 58.6 %all-to-all-start.1 = ((bf16[1024,4,256]{2,0,1:T(8,128)(2,1)}), bf16[1024,4,256]{2,0,1:T(8,128)(2,1)}, u32[]{:S(2)}, u32[]{:S(2)}) async-start(bf16[1024,4,256]{2,0,1:T(8,128)(2,1)} %bitcast.172), calls=%async_computation.1 | async-start | bytes 4194304 | tf_op jit(solution)/shard_map/all_to_all | solution.py:449
  999.8 180.5 %copy-start.20 = (f32[1024,67]{0,1:T(8,128)S(1)}, f32[1024,67]{0,1:T(8,128)}, u32[]{:S(2)}) copy-start(f32[1024,67]{0,1:T(8,128)} %copy-done.19) | copy-start | bytes 823300
  1054.0 131.9 %all-to-all-start.3 = ((bf16[1024,4,256]{2,0,1:T(8,128)(2,1)}), bf16[1024,4,256]{2,0,1:T(8,128)(2,1)S(1)}, u32[]{:S(2)}, u32[]{:S(2)}) async-start(bf16[1024,4,256]{2,0,1:T(8,128)(2,1)} %bitcast.170), calls=%async_computation.3 | async-start | bytes 4194304 | tf_op jit(solution)/shard_map/all_to_all | solution.py:512
  1057.6 299.6 %all-gather.40.cloned.1.call-start = ((), (), s32[]{:S(2)}) async-start(), calls=%async_computation.44 | async-start | bytes 2359296 | tf_op jit(solution)/shard_map/all_gather | solution.py:349
  1185.9 89.4 %copy-start.15 = (bf16[1024,4,256]{2,0,1:T(8,128)(2,1)}, bf16[1024,4,256]{2,0,1:T(8,128)(2,1)S(1)}, u32[]{:S(2)}) copy-start(bf16[1024,4,256]{2,0,1:T(8,128)(2,1)S(1)} %all-to-all-done.3) | copy-start | bytes 6291460
  (25 other events, 104.0 us)
Sparse Core Ops, SparseCore 0:
  10.2 41.8 all-gather.25
  54.0 35.8 all-gather.21
  91.7 36.7 all-gather.19
  131.7 73.6 all-gather.23
  207.1 27.1 all-gather.17
  236.1 27.8 all-gather.15
  265.9 54.3 all-gather.27
  323.8 77.4 all-gather.29
  483.7 49.9 reduce-scatter.14
  537.2 51.3 reduce-scatter.18
  592.5 51.3 reduce-scatter.30
  647.6 71.2 reduce-scatter.34
  722.4 71.2 reduce-scatter.38
  797.7 41.2 reduce-scatter.22
  842.1 41.1 reduce-scatter.26
  885.6 21.6 reduce-scatter.16
  909.5 19.9 reduce-scatter.20
  931.7 19.9 reduce-scatter.32
  954.1 25.4 reduce-scatter.36
  981.7 27.7 reduce-scatter.40
  1016.3 164.0 all-reduce.3
  1182.6 20.5 reduce-scatter.24
  1205.5 17.9 reduce-scatter.28
  1225.3 21.7 all-gather.31
  1248.9 23.4 all-gather.33
  1274.2 23.4 all-gather.37
  1299.4 27.8 all-gather.35
  1329.2 27.8 all-gather.39

commit v2 on v1

--- a/solution.py
+++ b/solution.py
@@ -312,6 +312,249 @@
     )(grad, x, normed_part, direct, gain, omega, keep, weight, start)
 
 
+MESH = pl.DeviceIdType.MESH
+
+
+def rank_of(index, order):
+    total = 0
+    for place, bit in enumerate(order):
+        total = total + lax.rem(lax.div(index, 1 << bit), 2) * (1 << place)
+    return total
+
+
+def flip(index, bit):
+    low = lax.rem(lax.div(index, 1 << bit), 2)
+    return index + (1 - 2 * low) * (1 << bit)
+
+
+def orders_of(dp):
+    bits = dp.bit_length() - 1
+    inner = list(range(1, bits))
+    return (inner + [0], inner[::-1] + [0])
+
+
+def gather_kernel(dp, mp, packs, swaps, small_ref, *refs):
+    pack_refs, refs = refs[:packs], refs[packs:]
+    swap_refs, refs = refs[:swaps], refs[swaps:]
+    small_out, refs = refs[0], refs[1:]
+    full_refs, refs = refs[:packs], refs[packs:]
+    row_refs, refs = refs[:swaps], refs[swaps:]
+    send_sem, recv_sem, pass_sem, swap_send, swap_recv, small_send, small_recv, own_sem = refs
+    me = lax.axis_index("dp")
+    part = lax.axis_index("mp")
+    bits = dp.bit_length() - 1
+    orders = orders_of(dp)
+
+    barrier = pltpu.get_barrier_semaphore()
+    for step in range(1, mp):
+        pl.semaphore_signal(
+            barrier, inc=1, device_id={"mp": lax.rem(part + step, mp)}, device_id_type=MESH
+        )
+    for bit in range(bits):
+        pl.semaphore_signal(barrier, inc=1, device_id={"dp": flip(me, bit)}, device_id_type=MESH)
+    pl.semaphore_wait(barrier, mp - 1 + bits)
+
+    local = []
+    sends = []
+
+    def own(src, dst, place):
+        copy = pltpu.make_async_copy(src, dst, own_sem.at[place])
+        copy.start()
+        local.append(copy)
+
+    small_rows = small_ref.shape[0]
+    own(small_ref, small_out.at[part], 0)
+    for step in range(1, mp):
+        to = lax.rem(part + step, mp)
+        copy = pltpu.make_async_remote_copy(
+            src_ref=small_ref, dst_ref=small_out.at[part],
+            send_sem=small_send.at[step], recv_sem=small_recv.at[part],
+            device_id={"mp": to}, device_id_type=MESH,
+        )
+        copy.start()
+        sends.append(copy)
+    def region(ref, half, held):
+        total, width = ref.shape[0], ref.shape[1] // 2
+        share = total // dp
+        rank = rank_of(me, orders[half])
+        first = lax.div(rank, 1 << held) * (share << held)
+        return ref.at[
+            pl.ds(pl.multiple_of(first, share), share << held), half * width : (half + 1) * width
+        ]
+
+    def send_on(place, source, up, src, sem):
+        dst = full_refs[place].at[source]
+        to = part + 1 if up else part - 1
+        copies = []
+        for half in range(2):
+            copies.append(
+                pltpu.make_async_remote_copy(
+                    src_ref=region(src, half, 0), dst_ref=region(dst, half, 0),
+                    send_sem=send_sem.at[place, 0, sem, half],
+                    recv_sem=recv_sem.at[place, 0, source, half],
+                    device_id={"mp": to}, device_id_type=MESH,
+                )
+            )
+        there = part < mp - 1 if up else part > 0
+
+        @pl.when(there)
+        def _():
+            for copy in copies:
+                copy.start()
+
+        guarded.append((there, copies))
+
+    guarded = []
+    for place in range(packs):
+        src, dst = pack_refs[place], full_refs[place]
+        send_on(place, part, True, src, 0)
+        send_on(place, part, False, src, mp)
+    for place in range(packs):
+        own(pack_refs[place], full_refs[place].at[part], 1 + swaps + place)
+
+    for place in range(swaps):
+        src, dst = swap_refs[place], row_refs[place]
+        count, width = dst.shape[0], src.shape[1]
+        columns = pl.ds(pl.multiple_of(part * width, width), width)
+
+        def rows(index):
+            return pl.ds(pl.multiple_of(index * count, count), count)
+
+        own(src.at[rows(part), :], dst.at[:, columns], 1 + place)
+        for step in range(1, mp):
+            to = lax.rem(part + step, mp)
+            copy = pltpu.make_async_remote_copy(
+                src_ref=src.at[rows(to), :], dst_ref=dst.at[:, columns],
+                send_sem=swap_send.at[place, step], recv_sem=swap_recv.at[place, part],
+                device_id={"mp": to}, device_id_type=MESH,
+            )
+            copy.start()
+            sends.append(copy)
+
+    def arrived(ref, sem):
+        pltpu.make_async_copy(ref, ref, sem).wait()
+
+    def source_of(step):
+        near = [lax.rem(part + 1, 2) + part - lax.rem(part, 2)]
+        low = lax.div(part, mp // 2) == 0
+        far = [
+            jnp.where(low, mp // 2 + place, mp // 2 - 1 - place) for place in range(mp // 2)
+        ]
+        return (near + far)[step - 1]
+
+    def advance(place, step, stage):
+        source = source_of(step)
+        dst = full_refs[place].at[source]
+        for half in range(2):
+            if stage == 0:
+                came = region(dst, half, 0)
+            else:
+                total, width = dst.shape[0], dst.shape[1] // 2
+                share = total // dp
+                bit = orders[half][stage - 1]
+                rank = rank_of(flip(me, bit), orders[half])
+                first = lax.div(rank, 1 << (stage - 1)) * (share << (stage - 1))
+                came = dst.at[
+                    pl.ds(pl.multiple_of(first, share), share << (stage - 1)),
+                    half * width : (half + 1) * width,
+                ]
+            arrived(came, recv_sem.at[place, stage, source, half])
+        if stage == 0:
+            forward(place, source, dst)
+        for half in range(2):
+            if stage < bits:
+                bit = orders[half][stage]
+                held = region(dst, half, stage)
+                copy = pltpu.make_async_remote_copy(
+                    src_ref=held, dst_ref=held,
+                    send_sem=send_sem.at[place, stage + 1, step, half],
+                    recv_sem=recv_sem.at[place, stage + 1, source, half],
+                    device_id={"dp": flip(me, bit)}, device_id_type=MESH,
+                )
+                copy.start()
+                sends.append(copy)
+
+    def forward(place, source, dst):
+        below = source < part
+        there = jnp.logical_or(
+            jnp.logical_and(below, part < mp - 1), jnp.logical_and(source > part, part > 0)
+        )
+        to = jnp.where(below, part + 1, part - 1)
+        copies = [
+            pltpu.make_async_remote_copy(
+                src_ref=region(dst, half, 0), dst_ref=region(dst, half, 0),
+                send_sem=pass_sem.at[place, source, half],
+                recv_sem=recv_sem.at[place, 0, source, half],
+                device_id={"mp": to}, device_id_type=MESH,
+            )
+            for half in range(2)
+        ]
+
+        @pl.when(there)
+        def _():
+            for copy in copies:
+                copy.start()
+
+        guarded.append((there, copies))
+
+    jobs = [(place, step) for place in range(packs) for step in range(1, mp)]
+    for wave in range(len(jobs) + bits):
+        for stage in range(bits, -1, -1):
+            number = wave - stage
+            if 0 <= number < len(jobs):
+                advance(jobs[number][0], jobs[number][1], stage)
+    for place in range(swaps):
+        width = swap_refs[place].shape[1]
+        for step in range(1, mp):
+            source = lax.rem(part + step, mp)
+            columns = pl.ds(pl.multiple_of(source * width, width), width)
+            arrived(row_refs[place].at[:, columns], swap_recv.at[place, source])
+    for step in range(1, mp):
+        source = lax.rem(part + step, mp)
+        arrived(small_out.at[source], small_recv.at[source])
+    for copy in sends:
+        copy.wait_send()
+    for there, copies in guarded:
+
+        @pl.when(there)
+        def _(copies=copies):
+            for copy in copies:
+                copy.wait_send()
+
+    for copy in local:
+        copy.wait()
+
+
+def gather(dp, mp, small, packs, swaps):
+    hbm = pl.BlockSpec(memory_space=pl.ANY)
+    bits = dp.bit_length() - 1
+    outs = [sds((mp,) + small.shape, small.dtype)]
+    outs += [sds((mp,) + item.shape, item.dtype) for item in packs]
+    outs += [sds((item.shape[0] // mp, item.shape[1] * mp), item.dtype) for item in swaps]
+    dma = pltpu.SemaphoreType.DMA
+    results = pl.pallas_call(
+        functools.partial(gather_kernel, dp, mp, len(packs), len(swaps)),
+        in_specs=[hbm] * (1 + len(packs) + len(swaps)),
+        out_specs=[hbm] * len(outs),
+        out_shape=outs,
+        scratch_shapes=[
+            dma((len(packs), bits + 1, mp + 1, 2)),
+            dma((len(packs), bits + 1, mp, 2)),
+            dma((len(packs), mp, 2)),
+            dma((len(swaps), mp)),
+            dma((len(swaps), mp)),
+            dma((mp,)),
+            dma((mp,)),
+            dma((1 + len(swaps) + len(packs),)),
+        ],
+        compiler_params=pltpu.CompilerParams(
+            collective_id=0, has_side_effects=True, vmem_limit_bytes=4 << 20
+        ),
+        name="gather",
+    )(small, *packs, *swaps)
+    return results[0], results[1 : 1 + len(packs)], results[1 + len(packs) :]
+
+
 def group_scores(query, keys):
     blocks = query.shape[0] // GROUP
     query_blocks = query.reshape(blocks, GROUP, query.shape[1])
@@ -320,19 +563,6 @@
     raw = raw * query.shape[1] ** (-0.5)
     place = jnp.arange(GROUP)
     return jnp.where((place[:, None] >= place[None, :])[None], raw, -1e30)
-
-
-def gather_columns(shard, dp, index):
-    share = shard.shape[0] // dp
-    part = lax.dynamic_slice_in_dim(shard, index * share, share, 0)
-    part = lax.all_gather(part, "mp", axis=1, tiled=True)
-    return lax.all_gather(part, "dp", axis=0, tiled=True)
-
-
-def gather_rows(shard, dp, index):
-    share = shard.shape[0] // dp
-    part = lax.dynamic_slice_in_dim(shard, index * share, share, 0)
-    return lax.all_gather(part, ("mp", "dp"), axis=0, tiled=True)
 
 
 def reduce_columns(grad):
@@ -374,22 +604,38 @@
     down_proj,
 ):
     width = tokens.shape[1]
-    index = lax.axis_index("dp")
     part = lax.axis_index("mp")
     count = tokens.shape[0] // mp
     span = LEN // count
     head_scale = query_gain.shape[0] ** (-0.5)
 
-    x_low = lax.all_to_all(tokens, "mp", 0, 1, tiled=True)
     small = jnp.concatenate(
         [
             ema_delta, ema_alpha, ema_beta, ema_eta,
             norm_gain[:, None], ema_omega[:, None], ffn_gain[:, None],
         ],
         axis=1,
-    )
-    small = lax.all_gather(small, "mp", axis=0, tiled=True)
-    small = small.T
+    ).T
+    small = jnp.pad(small, ((0, -small.shape[0] % 8), (0, 0)))
+    pack_one = jnp.concatenate([value_proj, gate_proj, mixer_proj, update_proj], axis=1)
+    pack_two = jnp.concatenate([up_proj, down_proj], axis=1)
+    small, (one, outs, two), (x_low, grad_out) = gather(
+        dp, mp, small, (pack_one, output_proj, pack_two), (tokens, cotangent)
+    )
+    small = small.transpose(1, 0, 2).reshape(small.shape[1], D)
+    wide, narrow = value_proj.shape[1], mixer_proj.shape[1]
+
+    def columns(first, size, pack):
+        block = lax.slice_in_dim(pack, first, first + size, axis=2)
+        return block.transpose(1, 0, 2).reshape(block.shape[1], mp * size)
+
+    value_all = columns(0, wide, one)
+    gate_all = columns(wide, wide, one)
+    mixer_all = columns(2 * wide, narrow, one)
+    update_all = columns(2 * wide + narrow, narrow, one)
+    output_all = outs.reshape(-1, D)
+    up_all = columns(0, up_proj.shape[1], two)
+    down_all = lax.slice_in_dim(two, up_proj.shape[1], two.shape[2], axis=2).reshape(-1, D)
     delta, alpha, beta, eta = (small[NDIM * i : NDIM * (i + 1)] for i in range(4))
     gain = small[4 * NDIM : 4 * NDIM + 1]
     omega = small[4 * NDIM + 1 : 4 * NDIM + 2]
@@ -398,15 +644,6 @@
     damp = jax.nn.sigmoid(alpha)
     keep = (1.0 - rate * damp).reshape(STATE)
     weight = (rate * beta * eta).reshape(STATE)
-
-    value_all = gather_columns(value_proj, dp, index)
-    gate_all = gather_columns(gate_proj, dp, index)
-    update_all = gather_columns(update_proj, dp, index)
-    mixer_all = gather_columns(mixer_proj, dp, index)
-    output_all = gather_rows(output_proj, dp, index)
-    up_all = gather_columns(up_proj, dp, index)
-    down_all = gather_rows(down_proj, dp, index)
-    grad_out = lax.all_to_all(cotangent, "mp", 0, 1, tiled=True)
 
     xn, ends = norm_ends(x_low, gain, keep)
     forward = [(i, i + 1) for i in range(mp - 1) if (i + 1) % span]

time: 1380 us -> 1260 us (0.913)
  waiting for transfers between devices: 682 us -> 431 us
  Pallas kernels: 75.4 us -> 305 us
  blocking collectives: 229 us -> 91 us
  local copies, waits for them, and re-layouts: 43.2 us -> 106 us
  matrix products: 256 us -> 231 us
    pallas_call x0 -> x1, Pallas kernels: none -> 229 us  [gather(): pl.pallas_call(functools.partial(gather_kernel, dp, mp, len(packs), len(s...]
    all_gather x5 -> x0, blocking collectives: 140 us -> none  [the longest x4 73.2 us: gather_columns(): part = lax.all_gather(part, 'mp', axis=1, tiled=True)]
    all_gather x8 -> x0, waiting for transfers between devices: 74.8 us -> none  [the longest x2 61.4 us: gather_rows(): return lax.all_gather(part, ('mp', 'dp'), axis=0, tiled=True)]
    psum x1, waiting for transfers between devices: 52.7 us -> 0.01 us  [local(): lax.psum((feature, shared_part, query_part, bias_part, key_part), ('dp',...]
    transpose x0 -> x7, local copies, waits for them, and re-layouts: none -> 42.4 us  [columns(): return block.transpose(1, 0, 2).reshape(block.shape[1], mp * size)]
    all_to_all x2 -> x0, waiting for transfers between devices: 36.8 us -> none  [the longest x1 36.8 us: local(): x_low = lax.all_to_all(tokens, 'mp', 0, 1, tiled=True)]
    all_gather x3, waiting for transfers between devices: 61.8 us -> 26.9 us  [reduce_columns(): return lax.all_gather(part, 'dp', axis=0, tiled=True).astype(jnp.float32)]
    reduce_scatter x5, waiting for transfers between devices: 100 us -> 74.1 us  [reduce_columns(): part = lax.psum_scatter(part, 'mp', scatter_dimension=1, tiled=True)]
  transfers between devices with their start and end apart: 34 -> 24, of which waited for: 21 -> 13; matrix products, arithmetic and copies ran while one was open for 18% -> 19% of each run, Pallas kernels for 5% -> 4%
where the time goes in v2:
time: 1260 us; the launch traced here: 1250 us
  waiting for transfers between devices  431 us (34%)
  Pallas kernels  305 us (24%)
  matrix products  231 us (18%)
  local copies, waits for them, and re-layouts  106 us (8%)
  blocking collectives  91 us (7%)
  other arithmetic  59.7 us (5%)
  between operations  16.8 us (1%)
  starting transfers between devices  12.7 us (1%)
    pallas_call x1, Pallas kernels, gather(): pl.pallas_call(functools.partial(gather_kernel, dp, mp, len(packs), len(s...  229 us
    reduce_scatter x2, waiting for transfers between devices, reduce_rows(): part = lax.psum_scatter(blocks, 'dp', scatter_dimension=1, tiled=False)  110 us
    reduce_scatter x5, waiting for transfers between devices, reduce_columns(): lax.psum_scatter(grad.astype(jnp.bfloat16), 'dp', scatter_dimension=0, ti...  104 us
    reduce_scatter x5, waiting for transfers between devices, reduce_columns(): part = lax.psum_scatter(part, 'mp', scatter_dimension=1, tiled=True)  74.1 us
    dot_general x8, matrix products, matmul_nt(): lax.dot_general(left, right, (((1,), (1,)), ((), ())), preferred_element_...  72.8 us
    dot_general x8, matrix products, matmul(): return jnp.dot(left, right, preferred_element_type=jnp.float32)  71.5 us
    psum x1, blocking collectives, local(): lax.psum((feature, shared_part, query_part, bias_part, key_part), ('dp',...  69.8 us
    dot_general x8, matrix products, matmul_tn(): lax.dot_general(left, right, (((0,), (0,)), ((), ())), preferred_element_...  64.7 us
  transfers between devices with their start and end apart: 24, of which 13 were waited for; matrix products, arithmetic and copies ran while one was open for 19% of the time, Pallas kernels for 4%

profile of v2, /device:TPU:0, one launch (start us, length us, event | category | flops | bytes accessed | tf_op | source)
XLA Modules:
  0.0 1253.6 jit_solution(8221688233712273701)
XLA Ops:
  8.2 4.9 pad_maximum_fusion.refs_2_
  19.7 229.5 %gather.1 = (f32[4,72,256]{2,1,0:T(8,128)S(1)}, bf16[4,1024,1536]{2,1,0:T(8,128)(2,1)S(1)}, bf16[4,512,1024]{2,1,0:T(8,128)(2,1)S(1)}, bf16[4,1024,2048]{2,1,0:T...) custom-call(f32[72,256]{1,0:T(8,128)S(1)} %pad.4.small_ref, ...), custom_call_target="tpu_custom_call" | custom-call | tf_op jit(solution)/shard_map/gather/pallas_call | solution.py:535
  249.2 5.8 copy-done.1
  254.9 4.6 copy-done.4
  263.7 13.3 %norm_ends.1 = (bf16[1024,1024]{1,0:T(8,128)(2,1)S(1)}, f32[32,8,128]{2,1,0:T(8,128)S(1)}) custom-call(bf16[1024,1024]{1,0:T(8,128)(2,1)S(1)} %get-tuple-element.34.x_ref, f32[1,1024]{1,0:T(1,128)S(1)} %bitcast.175, f32[16,8,128]{2,1,0:T(8,128)S(1)} %reshape.207.keep_ref), custom_call_target="tpu_custom_call" | custom-call | flops 67108864 | bytes 4194304 | tf_op jit(solution)/shard_map/norm_ends/pallas_call | solution.py:238
  278.4 5.9 slice_bitcast_fusion.2
  284.2 6.3 copy.85
  290.5 13.5 %fusion.38 = (bf16[4,1024,1024]{2,1,0:T(8,128)(2,1)}, bf16[1024,4,1024]{2,0,1:T(8,128)(2,1)}) fusion(bf16[4,1024,2048]{2,1,0:T(8,128)(2,1)} %copy-done.1), kind=kLoop, calls=%fused_computation.116 | loop fusion | bytes 33554432 | tf_op jit(solution)/shard_map/slice | solution.py:638
  304.1 8.2 multiply_convert_fusion.3
  312.3 4.5 slice_bitcast_fusion.3
  316.9 6.4 copy.84
  323.3 3.9 copy.83
  327.2 3.9 copy.81
  331.1 11.5 copy.89
  344.2 13.7 %ema.1 = (f32[1024,1024]{1,0:T(8,128)S(1)}, bf16[1024,1024]{1,0:T(8,128)(2,1)S(1)}) custom-call(bf16[1024,1024]{1,0:T(8,128)(2,1)S(1)} %copy-done.7, f32[16,8,128]{2,1,0:T(8,128)S(1)} %reshape.207.keep_ref, f32[16,8,128]{2,1,0:T(8,128)S(1)} %reshape.208.weight_ref, f32[1,1024]{1,0:T(1,128)S(1)} %bitcast.173, f32[32,8,128]{2,1,0:T(8,128)S(1)} %collective-permute-done.start_ref), custom_call_target="tpu_custom_call" | custom-call | flops 67108864 | bytes 8388608 | tf_op jit(solution)/shard_map/ema/pallas_call | solution.py:253
  362.8 6.9 fusion.25
  369.7 13.9 %fusion.2 = (bf16[1024,2048]{1,0:T(8,128)(2,1)S(1)}, f32[1024,2048]{1,0:T(8,128)}) fusion(f32[8,128,2048]{2,1,0:T(8,128)} %fusion.25, bf16[1024,1024]{1,0:T(8,128)(2,1)} %copy-done.10, bf16[1024,2048]{0,1:T(8,128)(2,1)} %bitcast.189), kind=kOutput, calls=%fused_computation.8 | convolution fusion | flops 4307550208 | bytes 27262976 | tf_op jit(solution)/shard_map/dot_general | solution.py:21
  383.6 4.5 fusion.43
  390.6 7.1 fusion.36
  397.7 19.5 %multiply_convert_fusion.1 = (bf16[1024,4096]{1,0:T(8,128)(2,1)}, f32[1024,4096]{1,0:T(8,128)}) fusion(bf16[1024,4096]{0,1:T(8,128)(2,1)} %bitcast.179, f32[1024,1024]{1,0:T(8,128)} %get-tuple-element.62, f32[1024]{0:T(1024)S(1)} %bitcast.221, f32[1024]{0:T(1024)S(1)} %get-tuple-element.93, f32[1024]{0:T(1024)S(1)} %get-tuple-element.92), kind=kOutput, calls=%fused_computation.2 | convolution fusion | flops 8615100416 | bytes 37761024 | tf_op jit(solution)/shard_map/dot_general | solution.py:21
  417.1 19.2 %multiply_convert_fusion = bf16[1024,4096]{1,0:T(8,128)(2,1)} fusion(f32[1024,4096]{1,0:T(8,128)} %get-tuple-element.103, bf16[1024,1024]{1,0:T(8,128)(2,1)} %copy-done.19, bf16[4096,1024]{1,0:T(8,128)(2,1)} %bitcast.185), kind=kOutput, calls=%fused_computation.1 | convolution fusion | flops 8627683328 | bytes 35651584 | tf_op jit(solution)/shard_map/dot_general | solution.py:31
  436.3 16.0 %multiply_reduce_fusion = (f32[1024]{0:T(1024)}, f32[1024]{0:T(1024)S(1)}, f32[1024]{0:T(1024)S(1)}, f32[1024,1024]{1,0:T(8,128)S(1)}) fusion(f32[1024,1024]{1,0:T(8,128)} %get-tuple-element.62, f32[1024]{0:T(1024)S(1)} %get-tuple-element.93, f32[1024]{0:T(1024)S(1)} %get-tuple-element.92, f32[1024]{0:T(1024)S(1)} %bitcast.222, ...), kind=kOutput, calls=%fused_computation.27 | convolution fusion | flops 8598320128 | bytes 25190400 | tf_op jit(solution)/shard_map/dot_general | solution.py:31
  455.8 4.2 fusion.10
  460.0 13.3 %fusion.4 = (bf16[1024,2048]{1,0:T(8,128)(2,1)S(1)}, bf16[1024,2048]{1,0:T(8,128)(2,1)}) fusion(f32[8,128,2048]{2,1,0:T(8,128)} %fusion.25, f32[1024,2048]{1,0:T(8,128)} %get-tuple-element.100, bf16[1024,1024]{1,0:T(8,128)(2,1)S(1)} %get-tuple-element.68, bf16[2048,1024]{1,0:T(8,128)(2,1)S(1)} %bitcast.178), kind=kOutput, calls=%fused_computation.10 | convolution fusion | flops 4322230272 | bytes 31457280 | tf_op jit(solution)/shard_map/dot_general | solution.py:31
  475.2 6.5 convolution_convert_fusion.3
  482.4 7.4 fusion.23
  489.8 8.8 fusion.1
  500.7 6.2 convolution_convert_fusion.4
  507.4 7.4 convolution_convert_fusion.2
  517.4 15.6 %convolution_convert_fusion.1 = bf16[1024,4096]{1,0:T(8,128)(2,1)} fusion(bf16[1024,4096]{1,0:T(8,128)(2,1)} %multiply_convert_fusion, f32[1024,1024]{1,0:T(8,128)} %get-tuple-element.62, f32[1024]{0:T(1024)S(1)} %bitcast.224, f32[1024]{0:T(1024)S(1)} %get-tuple-element.93, f32[1024]{0:T(1024)S(1)} %get-tuple-element.92), kind=kOutput, calls=%fused_computation.18 | convolution fusion | flops 8598323200 | bytes 20983808 | tf_op jit(solution)/shard_map/dot_general | solution.py:25
  533.2 15.0 %convolution_convert_fusion = bf16[4096,1024]{1,0:T(8,128)(2,1)} fusion(bf16[1024,4096]{1,0:T(8,128)(2,1)} %get-tuple-element.102, bf16[1024,1024]{1,0:T(8,128)(2,1)} %copy-done.19), kind=kOutput, calls=%fused_computation.17 | convolution fusion | flops 8594128896 | bytes 18874368 | tf_op jit(solution)/shard_map/dot_general | solution.py:25
  548.2 8.8 copy.102
  557.0 6.4 convolution_convert_fusion.5
  563.5 6.0 convolution_convert_fusion.6
  570.4 17.6 %reduce-scatter.15.cloned.1.call-done = bf16[128,2048]{1,0:T(8,128)(2,1)} async-done(((bf16[1024,2048]{1,0:T(8,128)(2,1)}), bf16[128,2048]{1,0:T(8,128)(2,1)}) %reduce-scatter.15.cloned.1.call-update) | async-done | bytes 524304 | tf_op jit(solution)/shard_map/reduce_scatter | solution.py:569
  588.0 4.7 multiply_reduce_fusion.5
  592.9 50.1 %reduce-scatter.31.cloned.1.call-done = bf16[4,1,64,1024]{3,2,0,1:T(8,128)(2,1)} async-done(((bf16[4,8,64,1024]{3,2,0,1:T(8,128)(2,1)}), bf16[4,1,64,1024]{3,2,0,1:T(8,128)(2,1)}) %reduce-scatter.31.cloned.1.call-update) | async-done | bytes 524304 | tf_op jit(solution)/shard_map/reduce_scatter | solution.py:577
  646.5 6.6 fusion.45
  653.1 64.5 %reduce-scatter.35.cloned.1.call-done = bf16[128,4096]{1,0:T(8,128)(2,1)} async-done(((bf16[1024,4096]{1,0:T(8,128)(2,1)}), bf16[128,4096]{1,0:T(8,128)(2,1)}) %reduce-scatter.35.cloned.1.call-update) | async-done | bytes 1048592 | tf_op jit(solution)/shard_map/reduce_scatter | solution.py:569
  722.1 4.4 fusion.46
  726.6 6.0 fusion.44
  732.6 60.0 %reduce-scatter.39.cloned.1.call-done = bf16[4,1,128,1024]{3,2,0,1:T(8,128)(2,1)} async-done(((bf16[4,8,128,1024]{3,2,0,1:T(8,128)(2,1)}), bf16[4,1,128,1024]{3,2,0,1:T(8,128)(2,1)}) %reduce-scatter.39.cloned.1.call-update) | async-done | bytes 1048592 | tf_op jit(solution)/shard_map/reduce_scatter | solution.py:577
  792.7 8.5 multiply_multiply_fusion.grad_ref
  801.2 6.0 adjoint_start.1
  809.0 4.5 fusion.50.normed_ref
  815.1 25.6 %ema_params.1 = (f32[32,8,128]{2,1,0:T(8,128)S(1)}, f32[1,1024]{1,0:T(1,128)S(1)}) custom-call(f32[1024,1024]{1,0:T(8,128)S(1)} %multiply_multiply_fusion.grad_ref, bf16[1024,1024]{1,0:T(8,128)(2,1)S(1)} %copy-done.9, f32[16,8,128]{2,1,0:T(8,128)S(1)} %reshape.207.keep_ref, f32[32,8,128]{2,1,0:T(8,128)S(1)} %collective-permute-done.start_ref), custom_call_target="tpu_custom_call" | custom-call | flops 134217728 | bytes 6291456 | tf_op jit(solution)/shard_map/ema_params/pallas_call | solution.py:283
  840.8 16.5 %token_grads.1 = (bf16[1024,1024]{1,0:T(8,128)(2,1)S(1)}, f32[1,1024]{1,0:T(1,128)S(1)}) custom-call(f32[1024,1024]{1,0:T(8,128)S(1)} %multiply_multiply_fusion.grad_ref, bf16[1024,1024]{1,0:T(8,128)(2,1)S(1)} %get-tuple-element.34.x_ref, f32[1024,1024]{1,0:T(8,128)S(1)} %fusion.50.normed_ref, f32[1024,1024]{1,0:T(8,128)S(1)} %copy-done.2, ...), custom_call_target="tpu_custom_call" | custom-call | flops 67108864 | bytes 14680064 | tf_op jit(solution)/shard_map/token_grads/pallas_call | solution.py:299
  860.1 22.1 %reduce-scatter.23.cloned.1.call-done = bf16[128,1024]{1,0:T(8,128)(2,1)} async-done(((bf16[1024,1024]{1,0:T(8,128)(2,1)}), bf16[128,1024]{1,0:T(8,128)(2,1)}) %reduce-scatter.23.cloned.1.call-update) | async-done | bytes 262160 | tf_op jit(solution)/shard_map/reduce_scatter | solution.py:569
  882.3 23.8 %reduce-scatter.21.cloned.1.call-done = bf16[128,512]{1,0:T(8,128)(2,1)} async-done(((bf16[128,2048]{1,0:T(8,128)(2,1)}), bf16[128,512]{1,0:T(8,128)(2,1)}) %reduce-scatter.21.cloned.1.call-update) | async-done | bytes 131088 | tf_op jit(solution)/shard_map/reduce_scatter | solution.py:570
  906.2 21.9 %reduce-scatter.17.cloned.1.call-done = bf16[128,512]{1,0:T(8,128)(2,1)} async-done(((bf16[128,2048]{1,0:T(8,128)(2,1)}), bf16[128,512]{1,0:T(8,128)(2,1)}) %reduce-scatter.17.cloned.1.call-update) | async-done | bytes 131088 | tf_op jit(solution)/shard_map/reduce_scatter | solution.py:570
  928.2 22.0 %reduce-scatter.33.cloned.1.call-done = bf16[1,64,1024]{2,1,0:T(8,128)(2,1)} async-done(((bf16[4,64,1024]{2,1,0:T(8,128)(2,1)}), bf16[1,64,1024]{2,1,0:T(8,128)(2,1)}) %reduce-scatter.33.cloned.1.call-update) | async-done | bytes 131088 | tf_op jit(solution)/shard_map/reduce_scatter | solution.py:578
  950.3 28.3 %reduce-scatter.37.cloned.1.call-done = bf16[128,1024]{1,0:T(8,128)(2,1)} async-done(((bf16[128,4096]{1,0:T(8,128)(2,1)}), bf16[128,1024]{1,0:T(8,128)(2,1)}) %reduce-scatter.37.cloned.1.call-update) | async-done | bytes 262160 | tf_op jit(solution)/shard_map/reduce_scatter | solution.py:570
  978.6 14.4 %add_convert_fusion = bf16[1024,1024]{1,0:T(8,128)(2,1)S(1)} fusion(f32[1024,1024]{1,0:T(8,128)} %get-tuple-element.62, bf16[1024,4096]{1,0:T(8,128)(2,1)} %get-tuple-element.102, bf16[4096,1024]{1,0:T(8,128)(2,1)} %bitcast.186), kind=kOutput, calls=%fused_computation.32 | convolution fusion | flops 8592031744 | bytes 23068672 | tf_op jit(solution)/shard_map/dot_general | solution.py:21
  994.4 4.5 all-to-all-start
  1000.4 56.3 %all-to-all-done = bf16[1024,4,256]{2,0,1:T(8,128)(2,1)} async-done(((bf16[1024,4,256]{2,0,1:T(8,128)(2,1)}), bf16[1024,4,256]{2,0,1:T(8,128)(2,1)}, u32[]{:S(2)}, u32[]{:S(2)}) %all-to-all-start) | async-done | bytes 2097184 | tf_op jit(solution)/shard_map/all_to_all | solution.py:686
  1056.7 3.6 all-to-all-start.1
  1063.3 69.8 %all-reduce.1 = (f32[128]{0:T(128)}, f32[128]{0:T(128)}, f32[128]{0:T(128)}) all-reduce(f32[128]{0:T(128)S(1)} %get-tuple-element.54, f32[128]{0:T(128)S(1)} %multiply_reduce_fusion.4, f32[128]{0:T(128)S(1)} %get-tuple-element.53), channel_id=1, replica_groups=mesh['dp'=8,'mp'=4] {'dp','mp'}, use_global_device_ids=true, to_apply=%region_11.12 | all-reduce | flops 384 | bytes 3072 | tf_op jit(solution)/shard_map/psum | solution.py:754
  1138.6 12.0 all_gather.24
  1151.6 9.2 all_gather.23
  1167.5 9.7 all-gather.14.cloned.1.call-done
  1180.0 26.9 %all-gather.12.cloned.1.call-done = bf16[1024,1024]{1,0:T(8,128)(2,1)} async-done(((bf16[128,1024]{1,0:T(8,128)(2,1)}), bf16[1024,1024]{1,0:T(8,128)(2,1)}) %all-gather.12.cloned.1.call-update) | async-done | bytes 2097168 | tf_op jit(solution)/shard_map/all_gather | solution.py:571
  1206.9 4.1 convert_element_type.127
  1211.0 25.7 %all-gather.16.cloned.1.call-done = bf16[1,1024,1024]{2,1,0:T(8,128)(2,1)} async-done(((bf16[1,128,1024]{2,1,0:T(8,128)(2,1)}), bf16[1,1024,1024]{2,1,0:T(8,128)(2,1)}) %all-gather.16.cloned.1.call-update) | async-done | bytes 2097168 | tf_op jit(solution)/shard_map/all_gather | solution.py:579
  1236.7 4.1 bitcast_convert_fusion
  (240 shorter events, 75.0 us)
Async XLA Ops:
  8.0 351.2 %copy-start = (bf16[1024,128]{1,0:T(8,128)(2,1)S(1)}, bf16[1024,128]{1,0:T(8,128)(2,1)}, u32[]{:S(2)}) copy-start(bf16[1024,128]{1,0:T(8,128)(2,1)} %param.28) | copy-start | bytes 786436
  8.0 5.0 copy-start.59
  8.1 5.0 copy-start.60
  8.1 5.0 copy-start.54
  8.1 5.0 copy-start.55
  8.1 5.0 copy-start.56
  8.1 5.8 copy-start.44
  8.1 5.8 copy-start.43
  8.1 561.5 %reduce-scatter.19.cloned.1.call-start = ((), (), s32[]{:S(2)}) async-start(), calls=%async_computation.19 | async-start | bytes 4718592 | tf_op jit(solution)/shard_map/reduce_scatter | solution.py:569
  249.2 5.8 copy-start.1
  263.6 20.6 %copy-start.22 = (f32[1,4,256]{2,0,1:T(1,128)}, f32[1,4,256]{2,0,1:T(1,128)S(1)}, u32[]{:S(2)}) copy-start(f32[1,4,256]{2,0,1:T(1,128)S(1)} %get-tuple-element.84) | copy-start | bytes 12292
  277.1 7.2 copy-start.5
  277.1 65.6 %collective-permute-start = (f32[32,8,128]{2,1,0:T(8,128)S(1)}, f32[32,8,128]{2,1,0:T(8,128)S(1)}, u32[]{:S(2)}, u32[]{:S(2)}) collective-permute-start(f32[32,8,128]{2,1,0:T(8,128)S(1)} %get-tuple-element.37), channel_id=1, source_target_pairs={{0,1},{2,3},{4,5},{6,7},{8,9},{10,11},{12,13},{14,15},{16,17},{18,... | collective-permute-start | bytes 393224 | tf_op jit(solution)/shard_map/ppermute | solution.py:651
  290.5 13.5 %copy-start.6 = (bf16[1024,1024]{1,0:T(8,128)(2,1)S(1)}, bf16[1024,1024]{1,0:T(8,128)(2,1)}, u32[]{:S(2)}) copy-start(bf16[1024,1024]{1,0:T(8,128)(2,1)} %copy-done.5) | copy-start | bytes 6291460
  290.5 13.5 %copy-start.30 = (bf16[1024,4,512]{0,2,1:T(8,128)(2,1)S(1)}, bf16[1024,4,512]{0,2,1:T(8,128)(2,1)}, u32[]{:S(2)}) copy-start(bf16[1024,4,512]{0,2,1:T(8,128)(2,1)} %copy.85) | copy-start | bytes 12582916
  331.1 28.1 %copy-start.61 = (f32[128]{0:T(128)S(1)}, f32[128]{0:T(128)}, u32[]{:S(2)}) copy-start(f32[128]{0:T(128)} %param.31) | copy-start | bytes 1540
  331.1 28.1 %copy-start.63 = (f32[128]{0:T(128)S(1)}, f32[128]{0:T(128)}, u32[]{:S(2)}) copy-start(f32[128]{0:T(128)} %param.29) | copy-start | bytes 1540
  331.1 28.1 %copy-start.65 = (f32[128]{0:T(128)S(1)}, f32[128]{0:T(128)}, u32[]{:S(2)}) copy-start(f32[128]{0:T(128)} %param.30) | copy-start | bytes 1540
  361.8 7.8 copy-start.36
  362.8 6.9 copy-start.52
  369.7 13.9 %copy-start.25 = (bf16[4,512,1024]{2,1,0:T(8,128)(2,1)S(1)}, bf16[4,512,1024]{2,1,0:T(8,128)(2,1)}, u32[]{:S(2)}) copy-start(bf16[4,512,1024]{2,1,0:T(8,128)(2,1)} %copy-done.24) | copy-start | bytes 12582916
  390.6 7.1 copy-start.34
  436.3 16.0 %copy-start.20 = (bf16[1024,1024]{1,0:T(8,128)(2,1)S(1)}, bf16[1024,1024]{1,0:T(8,128)(2,1)}, u32[]{:S(2)}) copy-start(bf16[1024,1024]{1,0:T(8,128)(2,1)} %copy-done.19) | copy-start | bytes 6291460
  436.3 16.0 %copy-start.27 = (f32[1024,1024]{1,0:T(8,128)S(1)}, f32[1024,1024]{1,0:T(8,128)}, u32[]{:S(2)}) copy-start(f32[1024,1024]{1,0:T(8,128)} %get-tuple-element.101) | copy-start | bytes 12582916
  436.3 16.0 %copy-start.33 = (f32[1024,1024]{1,0:T(8,128)S(1)}, f32[1024,1024]{1,0:T(8,128)}, u32[]{:S(2)}) copy-start(f32[1024,1024]{1,0:T(8,128)} %get-tuple-element.62) | copy-start | bytes 12582916
  459.9 13.3 %copy-start.37 = (bf16[1024,1024]{1,0:T(8,128)(2,1)}, bf16[1024,1024]{1,0:T(8,128)(2,1)S(1)}, u32[]{:S(2)}) copy-start(bf16[1024,1024]{1,0:T(8,128)(2,1)S(1)} %get-tuple-element.68) | copy-start | bytes 6291460
  460.0 15.3 %copy-start.12 = (bf16[1024,1024]{1,0:T(8,128)(2,1)S(1)}, bf16[1024,1024]{1,0:T(8,128)(2,1)}, u32[]{:S(2)}) copy-start(bf16[1024,1024]{1,0:T(8,128)(2,1)} %copy-done.10) | copy-start | bytes 6291460
  481.8 106.1 %reduce-scatter.15.cloned.1.call-start = ((), (), s32[]{:S(2)}) async-start(), calls=%async_computation.16 | async-start | bytes 4718592 | tf_op jit(solution)/shard_map/reduce_scatter | solution.py:569
  489.8 11.0 copy-start.8
  507.0 136.0 %reduce-scatter.31.cloned.1.call-start = ((), (), s32[]{:S(2)}) async-start(), calls=%async_computation.26 | async-start | bytes 4718592 | tf_op jit(solution)/shard_map/reduce_scatter | solution.py:577
  517.4 200.2 %reduce-scatter.35.cloned.1.call-start = ((), (), s32[]{:S(2)}) async-start(), calls=%async_computation.28 | async-start | bytes 9437184 | tf_op jit(solution)/shard_map/reduce_scatter | solution.py:569
  533.0 259.6 %reduce-scatter.39.cloned.1.call-start = ((), (), s32[]{:S(2)}) async-start(), calls=%async_computation.31 | async-start | bytes 9437184 | tf_op jit(solution)/shard_map/reduce_scatter | solution.py:577
  557.0 302.4 %reduce-scatter.27.cloned.1.call-start = ((), (), s32[]{:S(2)}) async-start(), calls=%async_computation.24 | async-start | bytes 2359296 | tf_op jit(solution)/shard_map/reduce_scatter | solution.py:569
  563.4 24.5 %copy-start.62 = (f32[128]{0:T(128)S(1)}, f32[128]{0:T(128)}, u32[]{:S(2)}) copy-start(f32[128]{0:T(128)} %param.31) | copy-start | bytes 1540
  563.5 24.5 %copy-start.64 = (f32[128]{0:T(128)S(1)}, f32[128]{0:T(128)}, u32[]{:S(2)}) copy-start(f32[128]{0:T(128)} %param.29) | copy-start | bytes 1540
  563.5 24.6 %copy-start.42 = (f32[8,128,128]{1,2,0:T(8,128)S(1)}, f32[8,128,128]{1,2,0:T(8,128)}, u32[]{:S(2)}) copy-start(f32[8,128,128]{1,2,0:T(8,128)} %get-tuple-element.98) | copy-start | bytes 1572868
  563.5 318.8 %reduce-scatter.23.cloned.1.call-start = ((), (), s32[]{:S(2)}) async-start(), calls=%async_computation.22 | async-start | bytes 2359296 | tf_op jit(solution)/shard_map/reduce_scatter | solution.py:569
  569.6 336.6 %reduce-scatter.21.cloned.1.call-start = ((), (), s32[]{:S(2)}) async-start(), calls=%async_computation.20 | async-start | bytes 655360 | tf_op jit(solution)/shard_map/reduce_scatter | solution.py:570
  570.3 357.8 %reduce-scatter.17.cloned.1.call-start = ((), (), s32[]{:S(2)}) async-start(), calls=%async_computation.17 | async-start | bytes 655360 | tf_op jit(solution)/shard_map/reduce_scatter | solution.py:570
  587.9 362.2 %reduce-scatter.33.cloned.1.call-start = ((), (), s32[]{:S(2)}) async-start(), calls=%async_computation.27 | async-start | bytes 655360 | tf_op jit(solution)/shard_map/reduce_scatter | solution.py:578
  643.0 335.5 %reduce-scatter.37.cloned.1.call-start = ((), (), s32[]{:S(2)}) async-start(), calls=%async_computation.29 | async-start | bytes 1310720 | tf_op jit(solution)/shard_map/reduce_scatter | solution.py:570
  717.6 342.7 %reduce-scatter.41.cloned.1.call-start = ((), (), s32[]{:S(2)}) async-start(), calls=%async_computation.32 | async-start | bytes 1310720 | tf_op jit(solution)/shard_map/reduce_scatter | solution.py:578
  792.7 340.4 %all-reduce.5.cloned.1.call-start = ((), (), s32[]{:S(2)}) async-start(), calls=%async_computation.35 | async-start | bytes 1376256 | tf_op jit(solution)/shard_map/psum | solution.py:754
  792.7 16.2 %copy-start.31 = (bf16[1024,4,512]{0,2,1:T(8,128)(2,1)S(1)}, bf16[1024,4,512]{0,2,1:T(8,128)(2,1)}, u32[]{:S(2)}) copy-start(bf16[1024,4,512]{0,2,1:T(8,128)(2,1)} %copy.85) | copy-start | bytes 12582916
  801.2 7.7 copy-start.29
  807.3 6.2 copy-start.13
  807.3 33.5 %collective-permute-start.1 = (f32[16,8,128]{2,1,0:T(8,128)S(1)}, f32[16,8,128]{2,1,0:T(8,128)S(1)}, u32[]{:S(2)}, u32[]{:S(2)}) collective-permute-start(f32[16,8,128]{2,1,0:T(8,128)S(1)} %adjoint_start.1), channel_id=1, source_target_pairs={{1,0},{3,2},{5,4},{7,6},{9,8},{11,10},{13,12},{15,14},{17,16},{19,... | collective-permute-start | bytes 196616 | tf_op jit(solution)/shard_map/ppermute | solution.py:744
  815.1 25.7 %copy-start.2 = (f32[1024,1024]{1,0:T(8,128)S(1)}, f32[1024,1024]{1,0:T(8,128)}, u32[]{:S(2)}) copy-start(f32[1024,1024]{1,0:T(8,128)} %get-tuple-element.60.direct_ref) | copy-start | bytes 12582916
  815.1 25.7 %copy-start.23 = (f32[1,4,256]{2,0,1:T(1,128)S(1)}, f32[1,4,256]{2,0,1:T(1,128)}, u32[]{:S(2)}) copy-start(f32[1,4,256]{2,0,1:T(1,128)} %copy-done.22) | copy-start | bytes 12292
  840.8 17.8 %copy-start.58 = (f32[1024]{0:T(1024)S(1)}, f32[1024]{0:T(1024)}, u32[]{:S(2)}) copy-start(f32[1024]{0:T(1024)} %get-tuple-element.48) | copy-start | bytes 12292
  859.3 279.2 %reduce-scatter.29.cloned.1.call-start = ((), (), s32[]{:S(2)}) async-start(), calls=%async_computation.25 | async-start | bytes 327680 | tf_op jit(solution)/shard_map/reduce_scatter | solution.py:570
  860.1 291.6 %reduce-scatter.25.cloned.1.call-start = ((), (), s32[]{:S(2)}) async-start(), calls=%async_computation.23 | async-start | bytes 327680 | tf_op jit(solution)/shard_map/reduce_scatter | solution.py:570
  882.3 279.6 %all-gather.10.cloned.1.call-start = ((), (), s32[]{:S(2)}) async-start(), calls=%async_computation.21 | async-start | bytes 1179648 | tf_op jit(solution)/shard_map/all_gather | solution.py:571
  906.2 258.5 %all-gather.8.cloned.1.call-start = ((), (), s32[]{:S(2)}) async-start(), calls=%async_computation.18 | async-start | bytes 1179648 | tf_op jit(solution)/shard_map/all_gather | solution.py:571
  928.2 249.1 %all-gather.14.cloned.1.call-start = ((), (), s32[]{:S(2)}) async-start(), calls=%async_computation.33 | async-start | bytes 1179648 | tf_op jit(solution)/shard_map/all_gather | solution.py:579
  950.2 256.7 %all-gather.12.cloned.1.call-start = ((), (), s32[]{:S(2)}) async-start(), calls=%async_computation.30 | async-start | bytes 2359296 | tf_op jit(solution)/shard_map/all_gather | solution.py:571
  993.0 6.0 copy-start.16
  994.4 62.3 %all-to-all-start = ((bf16[1024,4,256]{2,0,1:T(8,128)(2,1)}), bf16[1024,4,256]{2,0,1:T(8,128)(2,1)}, u32[]{:S(2)}, u32[]{:S(2)}) async-start(bf16[1024,4,256]{2,0,1:T(8,128)(2,1)} %bitcast.184), calls=%async_computation | async-start | bytes 4194304 | tf_op jit(solution)/shard_map/all_to_all | solution.py:686
  998.9 62.1 %copy-start.51 = (f32[4,2,8,256]{3,2,1,0:T(8,128)S(1)}, f32[4,2,8,256]{3,2,1,0:T(8,128)}, u32[]{:S(2)}) copy-start(f32[4,2,8,256]{3,2,1,0:T(8,128)} %get-tuple-element.81) | copy-start | bytes 196612
  998.9 62.1 %copy-start.50 = (f32[4,2,8,256]{3,2,1,0:T(8,128)S(1)}, f32[4,2,8,256]{3,2,1,0:T(8,128)}, u32[]{:S(2)}) copy-start(f32[4,2,8,256]{3,2,1,0:T(8,128)} %get-tuple-element.76) | copy-start | bytes 196612
  998.9 62.2 %copy-start.49 = (f32[4,2,8,256]{3,2,1,0:T(8,128)S(1)}, f32[4,2,8,256]{3,2,1,0:T(8,128)}, u32[]{:S(2)}) copy-start(f32[4,2,8,256]{3,2,1,0:T(8,128)} %get-tuple-element.78) | copy-start | bytes 196612
  999.0 62.2 %copy-start.48 = (f32[4,2,8,256]{3,2,1,0:T(8,128)S(1)}, f32[4,2,8,256]{3,2,1,0:T(8,128)}, u32[]{:S(2)}) copy-start(f32[4,2,8,256]{3,2,1,0:T(8,128)} %get-tuple-element.77) | copy-start | bytes 196612
  1056.7 81.9 %all-to-all-start.1 = ((bf16[1024,4,256]{2,0,1:T(8,128)(2,1)}), bf16[1024,4,256]{2,0,1:T(8,128)(2,1)S(1)}, u32[]{:S(2)}, u32[]{:S(2)}) async-start(bf16[1024,4,256]{2,0,1:T(8,128)(2,1)} %bitcast.183), calls=%async_computation.1 | async-start | bytes 4194304 | tf_op jit(solution)/shard_map/all_to_all | solution.py:749
  1060.3 176.4 %all-gather.16.cloned.1.call-start = ((), (), s32[]{:S(2)}) async-start(), calls=%async_computation.34 | async-start | bytes 2359296 | tf_op jit(solution)/shard_map/all_gather | solution.py:579
  (29 other events, 83.1 us)
Sparse Core Ops, SparseCore 0:
  481.9 51.2 reduce-scatter.18
  536.6 51.2 reduce-scatter.14
  591.6 51.3 reduce-scatter.30
  646.3 71.2 reduce-scatter.34
  721.3 71.2 reduce-scatter.38
  795.8 41.1 reduce-scatter.26
  840.6 41.5 reduce-scatter.22
  884.5 21.5 reduce-scatter.20
  908.4 19.6 reduce-scatter.16
  930.3 19.8 reduce-scatter.32
  952.5 26.0 reduce-scatter.36
  980.8 30.5 reduce-scatter.40
  1013.6 43.9 reduce-scatter.28
  1059.9 27.1 reduce-scatter.24
  1088.8 37.9 all-gather.9
  1128.6 24.0 all-gather.7
  1154.4 22.7 all-gather.13
  1179.0 27.8 all-gather.11
  1208.8 27.8 all-gather.15
Sparse Core Ops, SparseCore 1:
  859.4 165.3 all-reduce.4

commit v3 on v1

v3 whole, which is shorter than its diff:
```python
import functools

import jax
import jax.numpy as jnp
from jax import lax
from jax.experimental import pallas as pl
from jax.experimental.pallas import tpu as pltpu
from jax.sharding import PartitionSpec as P

D = 1024
GROUP = 128
LEN = 2048
NDIM = 16
LANES = 128
SUB = D // LANES
EPS = 1e-05
TB = 128


def matmul(left, right):
    return jnp.dot(left, right, preferred_element_type=jnp.float32)


def matmul_tn(left, right):
    return lax.dot_general(
        left, right, (((0,), (0,)), ((), ())), preferred_element_type=jnp.float32
    )


def matmul_nt(left, right):
    return lax.dot_general(
        left, right, (((1,), (1,)), ((), ())), preferred_element_type=jnp.float32
    )


def to_rows(scratch, value):
    for part in range(SUB):
        scratch[pl.ds(part, TB, stride=SUB), :] = value[:, part * LANES : (part + 1) * LANES]


def from_rows(scratch):
    return jnp.concatenate(
        [scratch[pl.ds(part, TB, stride=SUB), :] for part in range(SUB)], axis=1
    )


def row(scratch, index):
    return scratch[pl.ds(pl.multiple_of(index * SUB, SUB), SUB), :]


def sds(shape, dtype=jnp.float32):
    return jax.ShapeDtypeStruct(shape, dtype)


def block(reverse=None):
    if reverse is None:
        return pl.BlockSpec((TB, D), lambda i: (i, 0))
    return pl.BlockSpec((TB, D), lambda i: (reverse - 1 - i, 0))


def whole(*shape):
    return pl.BlockSpec(shape, lambda i: (0,) * len(shape))


STATE = (NDIM, SUB, LANES)
STATES = (2 * NDIM, SUB, LANES)
ROWS = pltpu.VMEM((TB * SUB, LANES), jnp.float32)
PARAMS = pltpu.CompilerParams(vmem_limit_bytes=32 << 20)


ROWS_C = 256


def sigmoid(value):
    return 0.5 + 0.5 * jnp.tanh(0.5 * value)


def causal_probs(query, keys, head_scale):
    scores = matmul_nt(query, keys) * head_scale
    down = lax.broadcasted_iota(jnp.int32, scores.shape, 0)
    across = lax.broadcasted_iota(jnp.int32, scores.shape, 1)
    scores = jnp.where(down >= across, scores, -1e30)
    weights = jnp.exp(scores - jnp.max(scores, axis=1, keepdims=True))
    return weights / jnp.sum(weights, axis=1, keepdims=True)


def mixer_forward_kernel(
    xn_ref, xp_ref, x_ref, one_ref, shared_ref, qgain_ref, qbias_ref, kgain_ref,
    vpre_ref, gpre_ref, att_ref, hid_ref, act_ref, upd_ref, mid_ref, spre_ref,
):
    mp = one_ref.shape[0]
    narrow = D // mp
    wide = vpre_ref.shape[1] // mp
    base = 2 * (wide + narrow)
    groups = ROWS_C // GROUP
    xn, xp = xn_ref[...], xp_ref[...]
    shared_pre = matmul(xp, shared_ref[...])
    spre_ref[...] = shared_pre
    shared = shared_pre * sigmoid(shared_pre)
    query = (shared * qgain_ref[...] + qbias_ref[...]).astype(jnp.bfloat16)
    keys = (shared * kgain_ref[...]).astype(jnp.bfloat16)
    head_scale = shared.shape[1] ** (-0.5)
    probs = [
        causal_probs(
            query[g * GROUP : (g + 1) * GROUP], keys[g * GROUP : (g + 1) * GROUP], head_scale
        ).astype(jnp.bfloat16)
        for g in range(groups)
    ]
    attn_out = None
    for m in range(mp):
        span = slice(m * wide, (m + 1) * wide)
        value_pre = matmul(xn, one_ref[m, :, 0:wide])
        values = (value_pre * sigmoid(value_pre)).astype(jnp.bfloat16)
        vpre_ref[:, span] = value_pre.astype(jnp.bfloat16)
        gate_pre = matmul(xp, one_ref[m, :, wide : 2 * wide])
        gate = gate_pre * sigmoid(gate_pre)
        gpre_ref[:, span] = gate_pre.astype(jnp.bfloat16)
        attended = jnp.concatenate(
            [matmul(probs[g], values[g * GROUP : (g + 1) * GROUP]) for g in range(groups)], axis=0
        )
        att_ref[:, span] = attended.astype(jnp.bfloat16)
        hidden = (gate * attended).astype(jnp.bfloat16)
        hid_ref[:, span] = hidden
        term = jnp.concatenate(
            [matmul(hidden, one_ref[m, 0:wide, base:]), matmul(hidden, one_ref[m, wide:, base:])], axis=1
        )
        attn_out = term if attn_out is None else attn_out + term
    for m in range(mp):
        span = slice(m * narrow, (m + 1) * narrow)
        act = matmul(xp, one_ref[m, :, 2 * wide : 2 * wide + narrow]) + attn_out[:, span]
        upd = matmul(xp, one_ref[m, :, 2 * wide + narrow : base])
        update = sigmoid(upd)
        act_ref[:, span] = act.astype(jnp.bfloat16)
        upd_ref[:, span] = upd.astype(jnp.bfloat16)
        x = x_ref[:, span].astype(jnp.float32)
        mid_ref[:, span] = x + update * (act * sigmoid(act) - x)


def ffn_kernel(
    mid_ref, grad_ref, x_ref, act_ref, upd_ref, two_ref, gain_ref,
    layer_ref, ffn_ref, upper_ref, dup_ref, dact_ref, dupd_ref, dx_ref, gsum_ref,
):
    mp, _, total = two_ref.shape
    units = total - D
    sub = 512
    middle = mid_ref[...]
    grad = grad_ref[...]
    mean = jnp.mean(middle, axis=1, keepdims=True)
    power = jnp.mean(middle * middle, axis=1, keepdims=True)
    scale = lax.rsqrt(power - mean * mean + EPS)
    normed = (middle - mean) * scale
    gain = gain_ref[...]
    ffn_in = (normed * gain).astype(jnp.bfloat16)
    ffn_ref[...] = ffn_in
    down_out = None
    d_ffn = None
    for m in range(mp):
        for first in range(0, units, sub):
            columns = slice(m * units + first, m * units + first + sub)
            up_weights = two_ref[m, :, first : first + sub]
            down_weights = two_ref[m, first : first + sub, units:]
            up_pre = matmul(ffn_in, up_weights)
            logistic = sigmoid(up_pre)
            value = up_pre * logistic
            upper = value.astype(jnp.bfloat16)
            upper_ref[:, columns] = upper
            slope = logistic + value - value * logistic
            d_up = (matmul_nt(grad, down_weights) * slope).astype(jnp.bfloat16)
            dup_ref[:, columns] = d_up
            term = matmul(upper, down_weights)
            down_out = term if down_out is None else down_out + term
            term = matmul_nt(d_up, up_weights)
            d_ffn = term if d_ffn is None else d_ffn + term
    layer_ref[...] = (middle + down_out).astype(jnp.bfloat16)

    @pl.when(pl.program_id(0) == 0)
    def _():
        gsum_ref[...] = jnp.zeros_like(gsum_ref)

    gsum_ref[...] += jnp.sum(d_ffn * normed, axis=0, keepdims=True)
    scaled = d_ffn * gain
    first = jnp.mean(scaled, axis=1, keepdims=True)
    second = jnp.mean(scaled * normed, axis=1, keepdims=True)
    d_middle = grad.astype(jnp.float32) + scale * (scaled - first - normed * second)
    act = act_ref[...].astype(jnp.float32)
    update = sigmoid(upd_ref[...].astype(jnp.float32))
    logistic = sigmoid(act)
    value = act * logistic
    x = x_ref[...].astype(jnp.float32)
    d_update = d_middle * update
    dact_ref[...] = (d_update * (logistic + value - value * logistic)).astype(jnp.bfloat16)
    dupd_ref[...] = (d_update * (value - x) * (1.0 - update)).astype(jnp.bfloat16)
    dx_ref[...] = (d_middle - d_update).astype(jnp.bfloat16)


def mixer_backward_kernel(
    dact_ref, dupd_ref, vpre_ref, gpre_ref, att_ref, spre_ref, mix_ref, one_ref, shared_ref,
    qgain_ref, qbias_ref, kgain_ref,
    dv_ref, dg_ref, dshared_ref, dmix_ref, dxn_ref, sums_ref,
):
    mp = one_ref.shape[0]
    narrow = D // mp
    wide = vpre_ref.shape[1] // mp
    base = 2 * (wide + narrow)
    groups = ROWS_C // GROUP
    shared_pre = spre_ref[...]
    logistic = sigmoid(shared_pre)
    shared = shared_pre * logistic
    query = (shared * qgain_ref[...] + qbias_ref[...]).astype(jnp.bfloat16)
    keys = (shared * kgain_ref[...]).astype(jnp.bfloat16)
    head_scale = shared.shape[1] ** (-0.5)
    rows = [slice(g * GROUP, (g + 1) * GROUP) for g in range(groups)]
    probs = [causal_probs(query[rows[g]], keys[rows[g]], head_scale) for g in range(groups)]
    probs_low = [item.astype(jnp.bfloat16) for item in probs]
    d_act = dact_ref[...]
    d_probs = [None] * groups
    d_xp = None
    d_xn = None
    for m in range(mp):
        span = slice(m * wide, (m + 1) * wide)
        thin = slice(m * narrow, (m + 1) * narrow)
        d_hidden = matmul_nt(d_act[:, : D // 2], one_ref[m, 0:wide, base:]) + matmul_nt(
            d_act[:, D // 2 :], one_ref[m, wide:, base:]
        )
        gate_pre = gpre_ref[:, span].astype(jnp.float32)
        gate_log = sigmoid(gate_pre)
        gate = gate_pre * gate_log
        attended = att_ref[:, span].astype(jnp.float32)
        d_gate = (d_hidden * attended * (gate_log + gate - gate * gate_log)).astype(jnp.bfloat16)
        dg_ref[:, span] = d_gate
        d_att = (d_hidden * gate).astype(jnp.bfloat16)
        value_pre = vpre_ref[:, span].astype(jnp.float32)
        value_log = sigmoid(value_pre)
        value = value_pre * value_log
        values = value.astype(jnp.bfloat16)
        parts = []
        for g in range(groups):
            term = matmul_nt(d_att[rows[g]], values[rows[g]])
            d_probs[g] = term if d_probs[g] is None else d_probs[g] + term
            parts.append(matmul_tn(probs_low[g], d_att[rows[g]]))
        d_value = jnp.concatenate(parts, axis=0)
        d_value_pre = (d_value * (value_log + value - value * value_log)).astype(jnp.bfloat16)
        dv_ref[:, span] = d_value_pre
        term = (
            matmul_nt(d_gate, one_ref[m, :, wide : 2 * wide])
            + matmul_nt(d_act[:, thin], one_ref[m, :, 2 * wide : 2 * wide + narrow])
            + matmul_nt(dupd_ref[:, thin], one_ref[m, :, 2 * wide + narrow : base])
        )
        d_xp = term if d_xp is None else d_xp + term
        term = matmul_nt(d_value_pre, one_ref[m, :, 0:wide])
        d_xn = term if d_xn is None else d_xn + term
    dxn_ref[...] = d_xn.astype(jnp.bfloat16)
    d_query, d_keys = [], []
    for g in range(groups):
        d_scores = probs[g] * (d_probs[g] - jnp.sum(probs[g] * d_probs[g], axis=1, keepdims=True))
        low = d_scores.astype(jnp.bfloat16)
        d_query.append(matmul(low, keys[rows[g]]) * head_scale)
        d_keys.append(matmul_tn(low, query[rows[g]]) * head_scale)
    d_query = jnp.concatenate(d_query, axis=0)
    d_keys = jnp.concatenate(d_keys, axis=0)

    @pl.when(pl.program_id(0) == 0)
    def _():
        sums_ref[...] = jnp.zeros_like(sums_ref)

    sums_ref[0:1, :] += jnp.sum(d_query * shared, axis=0, keepdims=True)
    sums_ref[1:2, :] += jnp.sum(d_query, axis=0, keepdims=True)
    sums_ref[2:3, :] += jnp.sum(d_keys * shared, axis=0, keepdims=True)
    d_shared = (d_query * qgain_ref[...] + d_keys * kgain_ref[...]) * (
        logistic + shared - shared * logistic
    )
    d_shared = d_shared.astype(jnp.bfloat16)
    dshared_ref[...] = d_shared
    d_xp = d_xp + matmul_nt(d_shared, shared_ref[...])
    mix = mix_ref[...]
    mix_log = sigmoid(mix)
    mix_value = mix * mix_log
    dmix_ref[...] = d_xp * (mix_log + mix_value - mix_value * mix_log)


def mixer_weights_kernel(
    xn_ref, xp_ref, hid_ref, dact_all_ref, dv_ref, dg_ref, dact_ref, dupd_ref, dshared_ref,
    one_ref, shared_ref, xnt, xpt,
):
    wide, narrow = dv_ref.shape[1], dact_ref.shape[1]

    @pl.when(pl.program_id(0) == 0)
    def _():
        xnt[...] = xn_ref[...].T
        xpt[...] = xp_ref[...].T
        shared_ref[...] = matmul(xpt[...], dshared_ref[...]).astype(jnp.bfloat16)

    one_ref[0, :, 0:wide] = matmul(xnt[...], dv_ref[...]).astype(jnp.bfloat16)
    one_ref[0, :, wide : 2 * wide] = matmul(xpt[...], dg_ref[...]).astype(jnp.bfloat16)
    one_ref[0, :, 2 * wide : 2 * wide + narrow] = matmul(xpt[...], dact_ref[...]).astype(jnp.bfloat16)
    base = 2 * (wide + narrow)
    one_ref[0, :, 2 * wide + narrow : base] = matmul(xpt[...], dupd_ref[...]).astype(jnp.bfloat16)
    out = matmul_tn(hid_ref[...], dact_all_ref[...]).astype(jnp.bfloat16)
    one_ref[0, 0:wide, base:] = out[:, : D // 2]
    one_ref[0, wide:, base:] = out[:, D // 2 :]


def ffn_weights_kernel(ffn_ref, grad_ref, upper_ref, dup_ref, two_ref, fft):
    units = dup_ref.shape[1]

    @pl.when(pl.program_id(0) == 0)
    def _():
        fft[...] = ffn_ref[...].T

    two_ref[0, :, 0:units] = matmul(fft[...], dup_ref[...]).astype(jnp.bfloat16)
    two_ref[0, :, units:] = matmul_tn(upper_ref[...], grad_ref[...]).astype(jnp.bfloat16)


def held(*shape):
    return pl.BlockSpec(shape, lambda i: (0,) * len(shape), pipeline_mode=pl.Buffered(1))


def rows_block(width):
    return pl.BlockSpec((ROWS_C, width), lambda i: (i, 0))


BIG = pltpu.CompilerParams(vmem_limit_bytes=60 << 20)


def cost(flops, bytes_accessed):
    return pl.CostEstimate(flops=int(flops), transcendentals=0, bytes_accessed=int(bytes_accessed))


def ffn(middle, grad, x, act, upd, two, gain):
    count = x.shape[0]
    units = two.shape[0] * (two.shape[2] - D)
    low = jnp.bfloat16
    return pl.pallas_call(
        ffn_kernel,
        grid=(count // ROWS_C,),
        in_specs=[rows_block(D)] * 5 + [held(*two.shape), held(1, D)],
        out_specs=[rows_block(D)] * 2 + [rows_block(units)] * 2 + [rows_block(D)] * 3 + [whole(1, D)],
        out_shape=[sds((count, D), low)] * 2
        + [sds((count, units), low)] * 2
        + [sds((count, D), low)] * 3
        + [sds((1, D))],
        compiler_params=BIG,
        cost_estimate=cost(4 * count * two.size, 60 << 20),
        name="ffn",
    )(middle, grad, x, act, upd, two, gain)


def mixer_backward(d_act, d_upd, vpre, gpre, att, spre, mix, one, shared, qgain, qbias, kgain):
    count = d_act.shape[0]
    units = vpre.shape[1]
    z = shared.shape[1]
    low = jnp.bfloat16
    return pl.pallas_call(
        mixer_backward_kernel,
        grid=(count // ROWS_C,),
        in_specs=[rows_block(D)] * 2
        + [rows_block(units)] * 3
        + [rows_block(z), rows_block(D)]
        + [held(*one.shape), held(*shared.shape)]
        + [held(1, z)] * 3,
        out_specs=[rows_block(units)] * 2
        + [rows_block(z), rows_block(D), rows_block(D), whole(8, z)],
        out_shape=[sds((count, units), low)] * 2
        + [sds((count, z), low), sds((count, D)), sds((count, D), low), sds((8, z))],
        compiler_params=BIG,
        cost_estimate=cost(2 * count * (one.size + shared.size), 60 << 20),
        name="mixer_backward",
    )(d_act, d_upd, vpre, gpre, att, spre, mix, one, shared, qgain, qbias, kgain)


def mixer_weights(mp, xn, xp, hidden, d_act, d_value, d_gate, d_upd, d_shared):
    count = xn.shape[0]
    wide, narrow, z = d_value.shape[1] // mp, D // mp, d_shared.shape[1]
    low = jnp.bfloat16

    def part(width):
        return pl.BlockSpec((count, width), lambda i: (0, i))

    return pl.pallas_call(
        mixer_weights_kernel,
        grid=(mp,),
        in_specs=[held(count, D), held(count, D), part(wide), held(count, D)]
        + [part(wide), part(wide), part(narrow), part(narrow), held(count, z)],
        out_specs=[
            pl.BlockSpec((1, D, 2 * (wide + narrow) + D // 2), lambda i: (i, 0, 0)),
            whole(D, z),
        ],
        out_shape=[sds((mp, D, 2 * (wide + narrow) + D // 2), low), sds((D, z), low)],
        scratch_shapes=[pltpu.VMEM((D, count), low), pltpu.VMEM((D, count), low)],
        compiler_params=BIG,
        cost_estimate=cost(2 * count * D * mp * (3 * wide + 2 * narrow), 40 << 20),
        name="mixer_weights",
    )(xn, xp, hidden, d_act, d_value, d_gate, d_act, d_upd, d_shared)


def ffn_weights(mp, ffn_in, grad, upper, d_up):
    count = ffn_in.shape[0]
    units = upper.shape[1] // mp
    low = jnp.bfloat16

    def part(width):
        return pl.BlockSpec((count, width), lambda i: (0, i))

    return pl.pallas_call(
        ffn_weights_kernel,
        grid=(mp,),
        in_specs=[held(count, D), held(count, D), part(units), part(units)],
        out_specs=pl.BlockSpec((1, D, units + D), lambda i: (i, 0, 0)),
        out_shape=sds((mp, D, units + D), low),
        scratch_shapes=[pltpu.VMEM((D, count), low)],
        compiler_params=BIG,
        cost_estimate=cost(4 * count * D * mp * units, 40 << 20),
        name="ffn_weights",
    )(ffn_in, grad, upper, d_up)


MESH = pl.DeviceIdType.MESH


def rank_of(index, order):
    total = 0
    for place, bit in enumerate(order):
        total = total + lax.rem(lax.div(index, 1 << bit), 2) * (1 << place)
    return total


def flip(index, bit):
    low = lax.rem(lax.div(index, 1 << bit), 2)
    return index + (1 - 2 * low) * (1 << bit)


def orders_of(dp):
    bits = dp.bit_length() - 1
    inner = list(range(1, bits))
    return (inner + [0], inner[::-1] + [0])


def greet(dp, mp):
    me = lax.axis_index("dp")
    part = lax.axis_index("mp")
    bits = dp.bit_length() - 1
    barrier = pltpu.get_barrier_semaphore()
    for step in range(1, mp):
        pl.semaphore_signal(
            barrier, inc=1, device_id={"mp": lax.rem(part + step, mp)}, device_id_type=MESH
        )
    for bit in range(bits):
        pl.semaphore_signal(barrier, inc=1, device_id={"dp": flip(me, bit)}, device_id_type=MESH)
    pl.semaphore_wait(barrier, mp - 1 + bits)


def arrived(ref, sem):
    pltpu.make_async_copy(ref, ref, sem).wait()


def remote(src, dst, send_sem, recv_sem, axis, to):
    return pltpu.make_async_remote_copy(
        src_ref=src, dst_ref=dst, send_sem=send_sem, recv_sem=recv_sem,
        device_id={axis: to}, device_id_type=MESH,
    )


def span_of(index, size):
    return pl.ds(pl.multiple_of(index * size, size), size)


class Swap:
    def __init__(self, mp, src, dst, sems, back=False):
        self.mp, self.src, self.dst, self.back = mp, src, dst, back
        self.send, self.recv, self.own = sems
        self.part = lax.axis_index("mp")
        if back:
            self.rows, self.width = src.shape[0], dst.shape[1]
        else:
            self.rows, self.width = dst.shape[0], src.shape[1]

    def piece(self, index):
        if self.back:
            return self.src.at[:, span_of(index, self.width)]
        return self.src.at[span_of(index, self.rows), :]

    def place(self, index):
        if self.back:
            return self.dst.at[span_of(index, self.rows), :]
        return self.dst.at[:, span_of(index, self.width)]

    def local(self):
        return pltpu.make_async_copy(self.piece(self.part), self.place(self.part), self.own.at[0])

    def copies(self):
        for step in range(1, self.mp):
            to = lax.rem(self.part + step, self.mp)
            yield remote(
                self.piece(to), self.place(self.part),
                self.send.at[step], self.recv.at[self.part], "mp", to,
            )

    def start(self):
        self.local().start()
        for copy in self.copies():
            copy.start()

    def receive(self):
        self.local().wait()
        for step in range(1, self.mp):
            source = lax.rem(self.part + step, self.mp)
            arrived(self.place(source), self.recv.at[source])

    def close(self):
        for copy in self.copies():
            copy.wait_send()


class Gather:
    def __init__(self, dp, mp, src, dst, sems):
        self.dp, self.mp, self.src, self.dst = dp, mp, src, dst
        self.line_send, self.pass_send, self.line_recv, self.send, self.recv, self.own = sems
        self.me, self.part = lax.axis_index("dp"), lax.axis_index("mp")
        self.bits = dp.bit_length() - 1
        self.orders = orders_of(dp)

    def region(self, ref, half, index, held):
        total, width = ref.shape[0], ref.shape[1] // 2
        share = total // self.dp
        first = lax.div(rank_of(index, self.orders[half]), 1 << held) * (share << held)
        return ref.at[
            pl.ds(pl.multiple_of(first, share), share << held), half * width : (half + 1) * width
        ]

    def local(self):
        return pltpu.make_async_copy(self.src, self.dst.at[self.part], self.own.at[0])

    def first(self, up):
        to = self.part + 1 if up else self.part - 1
        for half in range(2):
            yield remote(
                self.region(self.src, half, self.me, 0),
                self.region(self.dst.at[self.part], half, self.me, 0),
                self.line_send.at[int(up), half], self.line_recv.at[self.part, half], "mp", to,
            )

    def passed(self, source):
        to = jnp.where(source < self.part, self.part + 1, self.part - 1)
        for half in range(2):
            held = self.region(self.dst.at[source], half, self.me, 0)
            yield remote(
                held, held, self.pass_send.at[source, half], self.line_recv.at[source, half], "mp", to
            )

    def passes(self, source):
        return jnp.logical_or(
            jnp.logical_and(source < self.part, self.part < self.mp - 1),
            jnp.logical_and(source > self.part, self.part > 0),
        )

    def doubled(self, source, stage):
        for half in range(2):
            held = self.region(self.dst.at[source], half, self.me, stage)
            yield remote(
                held, held, self.send.at[stage, source, half], self.recv.at[stage, source, half],
                "dp", flip(self.me, self.orders[half][stage]),
            )

    def source(self, step):
        mp, part = self.mp, self.part
        near = [lax.rem(part + 1, 2) + part - lax.rem(part, 2)]
        low = lax.div(part, mp // 2) == 0
        far = [jnp.where(low, mp // 2 + i, mp // 2 - 1 - i) for i in range(mp // 2)]
        return (near + far)[step]

    def start(self):
        for up in (True, False):

            @pl.when(self.part < self.mp - 1 if up else self.part > 0)
            def _(up=up):
                for copy in self.first(up):
                    copy.start()

        self.local().start()

    def advance(self, step, stage):
        source = self.source(step)
        for half in range(2):
            if stage == 0:
                came = self.region(self.dst.at[source], half, self.me, 0)
                arrived(came, self.line_recv.at[source, half])
            else:
                other = flip(self.me, self.orders[half][stage - 1])
                came = self.region(self.dst.at[source], half, other, stage - 1)
                arrived(came, self.recv.at[stage - 1, source, half])
        if stage == 0:

            @pl.when(self.passes(source))
            def _():
                for copy in self.passed(source):
                    copy.start()

        if stage < self.bits:
            for copy in self.doubled(source, stage):
                copy.start()

    def waves(self):
        return self.mp - 1 + self.bits

    def wave(self, number):
        for stage in range(self.bits, -1, -1):
            if 0 <= number - stage < self.mp - 1:
                self.advance(number - stage, stage)

    def close(self):
        self.local().wait()
        for up in (True, False):

            @pl.when(self.part < self.mp - 1 if up else self.part > 0)
            def _(up=up):
                for copy in self.first(up):
                    copy.wait_send()

        for step in range(self.mp - 1):
            source = self.source(step)

            @pl.when(self.passes(source))
            def _(source=source):
                for copy in self.passed(source):
                    copy.wait_send()

            for stage in range(self.bits):
                for copy in self.doubled(source, stage):
                    copy.wait_send()


def swap_sems(mp):
    dma = pltpu.SemaphoreType.DMA
    return [dma((mp,)), dma((mp,)), dma((1,))]


def gather_sems(dp, mp):
    dma = pltpu.SemaphoreType.DMA
    bits = dp.bit_length() - 1
    return [dma((2, 2)), dma((mp, 2)), dma((mp, 2)), dma((bits, mp, 2)), dma((bits, mp, 2)), dma((1,))]


HBM = pl.BlockSpec(memory_space=pl.ANY)


def opening_kernel(dp, mp, small_ref, pack_ref, tok_ref, small_out, full_ref, rows_ref, *sems):
    swap = Swap(mp, tok_ref, rows_ref, sems[0:3])
    tiny = Swap(mp, small_ref, small_out, sems[3:6], back=True)
    plan = Gather(dp, mp, pack_ref, full_ref, sems[6:12])
    greet(dp, mp)
    tiny.start()
    plan.start()
    for number in range(plan.waves()):
        plan.wave(number)
        if number == mp - 2:
            swap.start()
    for item in (tiny, swap):
        item.receive()
        item.close()
    plan.close()


def opening(dp, mp, small, pack, tokens):
    return pl.pallas_call(
        functools.partial(opening_kernel, dp, mp),
        in_specs=[HBM] * 3,
        out_specs=[HBM] * 3,
        out_shape=[
            sds((mp * small.shape[0], small.shape[1] // mp)),
            sds((mp,) + pack.shape, pack.dtype),
            sds((tokens.shape[0] // mp, tokens.shape[1] * mp), tokens.dtype),
        ],
        scratch_shapes=swap_sems(mp) * 2 + gather_sems(dp, mp),
        compiler_params=pltpu.CompilerParams(
            collective_id=0, has_side_effects=True, vmem_limit_bytes=4 << 20
        ),
        name="opening",
    )(small, pack, tokens)


def forward_kernel(
    dp, mp, span,
    x_ref, gain_ref, keep_ref, weight_ref, omega_ref,
    one_ref, shared_ref, qgain_ref, qbias_ref, kgain_ref, pack_ref, cot_ref,
    xn_ref, xp_ref, mix_ref, starts_ref,
    vpre_ref, gpre_ref, att_ref, hid_ref, act_ref, upd_ref, mid_ref, spre_ref,
    full_ref, grad_ref,
    xn_all, rows, outs, ends, starts, state_ref, carry_send, carry_recv, *sems,
):
    index = pl.program_id(0)
    steps = pl.num_programs(0) // 2
    part = lax.axis_index("mp")
    swap = Swap(mp, cot_ref, grad_ref, sems[0:3])
    plan = Gather(dp, mp, pack_ref, full_ref, sems[3:9])
    gives = lax.rem(part + 1, span) != 0
    takes = lax.rem(part, span) != 0

    def carry():
        return remote(ends, starts, carry_send.at[0], carry_recv.at[0], "mp", part + 1)

    @pl.when(index == 0)
    def _():
        greet(dp, mp)
        plan.start()
        ends[...] = jnp.zeros_like(ends)

    @pl.when(index < steps)
    def _():
        keep = [keep_ref[j] for j in range(NDIM)]
        for piece in range(ROWS_C // TB):
            here = slice(piece * TB, (piece + 1) * TB)
            x = x_ref[here, :].astype(jnp.float32)
            mean = jnp.mean(x, axis=1, keepdims=True)
            power = jnp.mean(x * x, axis=1, keepdims=True)
            scale = lax.rsqrt(power - mean * mean + EPS)
            xn = ((x - mean) * scale * gain_ref[...]).astype(jnp.bfloat16)
            xn_ref[here, :] = xn
            xn_all[pl.ds(pl.multiple_of(index * ROWS_C + piece * TB, TB), TB), :] = xn
            to_rows(rows, xn.astype(jnp.float32))

            def step(t, carried):
                state, slope = carried
                now = row(rows, t)
                slope = tuple(keep[j] * slope[j] + state[j] for j in range(NDIM))
                state = tuple(keep[j] * state[j] + now for j in range(NDIM))
                return (state, slope)

            state = tuple(ends[j] for j in range(NDIM))
            slope = tuple(ends[NDIM + j] for j in range(NDIM))
            state, slope = lax.fori_loop(0, TB, step, (state, slope), unroll=4)
            for j in range(NDIM):
                ends[j] = state[j]
                ends[NDIM + j] = slope[j]

    @pl.when(index == steps - 1)
    def _():
        @pl.when(gives)
        def _():
            carry().start()

        plan.wave(0)

    @pl.when(index == steps)
    def _():
        @pl.when(jnp.logical_not(takes))
        def _():
            starts[...] = jnp.zeros_like(starts)

        @pl.when(takes)
        def _():
            arrived(starts, carry_recv.at[0])

        @pl.when(gives)
        def _():
            carry().wait_send()

        for j in range(NDIM):
            state_ref[j] = starts[j]
        starts_ref[...] = starts[...]

    @pl.when(index >= steps)
    def _():
        for piece in range(ROWS_C // TB):
            here = slice(piece * TB, (piece + 1) * TB)
            xn = xn_all[
                pl.ds(pl.multiple_of((index - steps) * ROWS_C + piece * TB, TB), TB), :
            ].astype(jnp.float32)
            to_rows(rows, xn)
            keep = [keep_ref[j] for j in range(NDIM)]

            def step(t, state):
                now = row(rows, t)
                state = tuple(keep[j] * state[j] + now for j in range(NDIM))
                terms = [weight_ref[j] * state[j] for j in range(NDIM)]
                while len(terms) > 1:
                    terms = [a + b for a, b in zip(terms[::2], terms[1::2])]
                outs[pl.ds(pl.multiple_of(t * SUB, SUB), SUB), :] = terms[0]
                return state

            state = lax.fori_loop(0, TB, step, tuple(state_ref[j] for j in range(NDIM)), unroll=4)
            for j in range(NDIM):
                state_ref[j] = state[j]
            mix = from_rows(outs) + omega_ref[...] * xn
            mix_ref[here, :] = mix
            xp_ref[here, :] = (mix * sigmoid(mix)).astype(jnp.bfloat16)

        xn_block = xn_all.at[pl.ds(pl.multiple_of((index - steps) * ROWS_C, ROWS_C), ROWS_C), :]
        mixer_forward_kernel(
            xn_block, xp_ref, x_ref, one_ref, shared_ref, qgain_ref, qbias_ref, kgain_ref,
            vpre_ref, gpre_ref, att_ref, hid_ref, act_ref, upd_ref, mid_ref, spre_ref,
        )

    for number in range(1, plan.waves()):
        at = jnp.minimum(steps + number - 1, 2 * steps - 1)

        @pl.when(index == at)
        def _(number=number):
            plan.wave(number)
            if number == mp - 2:
                swap.start()

    @pl.when(index == 2 * steps - 1)
    def _():
        swap.receive()
        swap.close()
        plan.close()


def forward(dp, mp, span, units, x, gain, keep, weight, omega, one, shared, vectors, pack, cotangent):
    count = x.shape[0]
    steps = count // ROWS_C
    z = shared.shape[1]
    low = jnp.bfloat16
    early = pl.BlockSpec((ROWS_C, D), lambda i: (jnp.minimum(i, steps - 1), 0))

    def late(width):
        return pl.BlockSpec((ROWS_C, width), lambda i: (jnp.maximum(i - steps, 0), 0))

    dma = pltpu.SemaphoreType.DMA
    return pl.pallas_call(
        functools.partial(forward_kernel, dp, mp, span),
        grid=(2 * steps,),
        in_specs=[pl.BlockSpec((ROWS_C, D), lambda i: (lax.rem(i, steps), 0))]
        + [held(1, D), held(*STATE), held(*STATE), held(1, D)]
        + [held(*one.shape), held(*shared.shape)]
        + [held(1, z)] * 3
        + [HBM] * 2,
        out_specs=[early, late(D), late(D), whole(*STATES)]
        + [late(units)] * 4
        + [late(D)] * 3
        + [late(z)]
        + [HBM] * 2,
        out_shape=[sds((count, D), low), sds((count, D), low), sds((count, D)), sds(STATES)]
        + [sds((count, units), low)] * 4
        + [sds((count, D), low)] * 2
        + [sds((count, D)), sds((count, z))]
        + [sds((mp,) + pack.shape, low), sds((count, D), low)],
        scratch_shapes=[
            pltpu.VMEM((count, D), low), ROWS, ROWS,
            pltpu.VMEM(STATES, jnp.float32), pltpu.VMEM(STATES, jnp.float32),
            pltpu.VMEM(STATE, jnp.float32), dma((1,)), dma((1,)),
        ]
        + swap_sems(mp)
        + gather_sems(dp, mp),
        compiler_params=pltpu.CompilerParams(
            collective_id=1, has_side_effects=True, vmem_limit_bytes=60 << 20
        ),
        name="forward",
    )(x, gain, keep, weight, omega, one, shared, *vectors, pack, cotangent)


def add_rows(acc, first, other, count):
    chunk = min(count, 32)

    def step(index, _):
        there = pl.ds(pl.multiple_of(first + index * chunk, chunk), chunk)
        here = pl.ds(pl.multiple_of(index * chunk, chunk), chunk)
        total = acc[there, :].astype(jnp.float32) + other[here, :].astype(jnp.float32)
        acc[there, :] = total.astype(jnp.bfloat16)
        return 0

    lax.fori_loop(0, count // chunk, step, 0)


class Reduce:
    def __init__(self, dp, mp, src, out, stage, recvs, lines, last, sems, waits):
        self.dp, self.mp, self.src, self.out, self.stage = dp, mp, src, out, stage
        self.recvs, self.lines, self.last, self.waits = recvs, lines, last, waits
        (
            self.load, self.send, self.recv, self.line_send, self.line_recv,
            self.last_send, self.last_recv, self.ring_send, self.ring_recv, self.own,
        ) = sems
        self.me, self.part = lax.axis_index("dp"), lax.axis_index("mp")
        self.bits = dp.bit_length() - 1
        self.orders = orders_of(dp)
        self.share = src.shape[1] // dp
        self.width = src.shape[2] // 2

    def shard(self, i):
        near, far = flip(self.part, 0), flip(self.part, 1)
        return (near, flip(far, 0), far, self.part)[i]

    def rank(self, half, index):
        return rank_of(index, self.orders[half])

    def push(self, copy):
        copy.start()
        self.waits.append(copy.wait_send)

    def begin(self, i, slot):
        m = self.shard(i)
        count = self.share << (self.bits - 1)
        for half in range(2):
            columns = slice(half * self.width, (half + 1) * self.width)
            other = flip(self.me, self.orders[half][self.bits - 1])

            def rows(index):
                return span_of(lax.div(self.rank(half, index), 1 << (self.bits - 1)), count)

            self.push(
                remote(
                    self.src.at[m, rows(other), columns], self.recvs[0].at[m, half],
                    self.send.at[0, i, half], self.recv.at[0, m, half], "dp", other,
                )
            )
            pltpu.make_async_copy(
                self.src.at[m, rows(self.me), columns], self.stage.at[slot, half],
                self.load.at[slot, half],
            ).start()

    def offset(self, half, index, stage):
        low = lax.rem(self.rank(half, index), 1 << (self.bits - 1))
        left = self.bits - 1 - stage
        return lax.div(low, 1 << left) * (self.share << left)

    def fold(self, i, stage, slot):
        m = self.shard(i)
        count = self.share << (self.bits - 1 - stage)
        for half in range(2):
            acc = self.recvs[0].at[m, half]
            came = self.recvs[stage].at[m, half]
            arrived(came, self.recv.at[stage, m, half])
            if stage == 0:
                own = self.stage.at[slot, half]
                arrived(own, self.load.at[slot, half])
                add_rows(acc, 0, own, count)
            else:
                add_rows(acc, self.offset(half, self.me, stage), came, count)
            if stage < self.bits - 1:
                other = flip(self.me, self.orders[half][self.bits - 2 - stage])
                give = self.offset(half, other, stage + 1)
                self.push(
                    remote(
                        acc.at[pl.ds(pl.multiple_of(give, self.share), count // 2), :],
                        self.recvs[stage + 1].at[m, half],
                        self.send.at[stage + 1, i, half], self.recv.at[stage + 1, m, half],
                        "dp", other,
                    )
                )
                continue
            first = self.offset(half, self.me, stage)
            mine = acc.at[pl.ds(pl.multiple_of(first, self.share), self.share), :]
            if i >= 2:
                came = self.lines.at[m, half]
                arrived(came, self.line_recv.at[m, half])
                add_rows(acc, first, came, self.share)
            if i < 2:
                self.push(
                    remote(
                        mine, self.lines.at[m, half],
                        self.line_send.at[i, half], self.line_recv.at[m, half],
                        "mp", flip(self.part, 0),
                    )
                )
            elif i == 2:
                self.push(
                    remote(
                        mine, self.last.at[half], self.last_send.at[half], self.last_recv.at[half],
                        "mp", flip(self.part, 1),
                    )
                )
            else:
                came = self.last.at[half]
                arrived(came, self.last_recv.at[half])
                add_rows(acc, first, came, self.share)
                pltpu.make_async_copy(mine, self.rows_at(half, self.me, 0), self.own.at[half]).start()

    def rows_at(self, half, index, stage):
        first = lax.div(self.rank(half, index), 1 << stage) * (self.share << stage)
        return self.out.at[
            pl.ds(pl.multiple_of(first, self.share), self.share << stage),
            half * self.width : (half + 1) * self.width,
        ]

    def spread(self, stage):
        for half in range(2):
            mine = self.rows_at(half, self.me, stage)
            if stage == 0:
                arrived(mine, self.own.at[half])
            else:
                other = flip(self.me, self.orders[half][stage - 1])
                arrived(self.rows_at(half, other, stage - 1), self.ring_recv.at[stage - 1, half])
            if stage < self.bits:
                self.push(
                    remote(
                        mine, mine, self.ring_send.at[stage, half], self.ring_recv.at[stage, half],
                        "dp", flip(self.me, self.orders[half][stage]),
                    )
                )


def reduce_sems(dp, mp):
    dma = pltpu.SemaphoreType.DMA
    bits = dp.bit_length() - 1
    return [
        dma((bits, mp, 2)), dma((bits, mp, 2)), dma((2, 2)), dma((mp, 2)),
        dma((2,)), dma((2,)), dma((bits, 2)), dma((bits, 2)), dma((2,)),
    ]


class Tiny:
    def __init__(self, dp, mp, piece, line, ring, came, sems, waits):
        self.dp, self.mp, self.piece, self.waits = dp, mp, piece, waits
        self.line, self.ring, self.came = line, ring, came
        self.send, self.recv, self.ring_send, self.ring_recv = sems
        self.me, self.part = lax.axis_index("dp"), lax.axis_index("mp")
        self.bits = dp.bit_length() - 1

    def push(self, copy):
        copy.start()
        self.waits.append(copy.wait_send)

    def start(self):
        for step in range(1, self.mp):
            to = lax.rem(self.part + step, self.mp)
            self.push(
                remote(
                    self.piece(to), self.line.at[self.part],
                    self.send.at[step], self.recv.at[self.part], "mp", to,
                )
            )

    def fold(self, stage):
        if stage == 0:
            total = self.piece(self.part)[...].astype(jnp.float32)
            for step in range(1, self.mp):
                source = lax.rem(self.part + step, self.mp)
                arrived(self.line.at[source], self.recv.at[source])
                total = total + self.line[source].astype(jnp.float32)
        else:
            arrived(self.came.at[stage - 1], self.ring_recv.at[stage - 1])
            total = self.ring[stage - 1] + self.came[stage - 1]
        self.ring[stage] = total
        if stage < self.bits:
            self.push(
                remote(
                    self.ring.at[stage], self.came.at[stage],
                    self.ring_send.at[stage], self.ring_recv.at[stage],
                    "dp", flip(self.me, stage),
                )
            )


def tiny_sems(dp, mp):
    dma = pltpu.SemaphoreType.DMA
    bits = dp.bit_length() - 1
    return [dma((mp,)), dma((mp,)), dma((bits,)), dma((bits,))]


FEATURES = 40


def closing_kernel(
    dp, mp, span,
    one_ref, two_ref, layer_ref, grad_ref, xn_ref, x_ref, normed_ref, direct_ref, shared_ref, vector_ref,
    keep_ref, weight_ref, gain_ref, omega_ref, ffn_ref, starts_ref,
    one_out, two_out, layer_out, token_out, feat_out, shared_out, vector_out,
    stage, *refs,
):
    bits = dp.bit_length() - 1
    me, part = lax.axis_index("dp"), lax.axis_index("mp")
    waits = []
    taken = 0

    def take(count):
        nonlocal taken
        taken += count
        return refs[taken - count : taken]

    recvs = [take(bits), take(bits)]
    lines = take(2)
    last = take(2)
    grad, xn, x, normed_part, direct, tokens, rows, outs, states, ahead, sums, feat = take(12)
    shared, shared_line, shared_ring, shared_came, shared_low = take(5)
    feat_line, feat_ring, feat_came = take(3)
    vector, vector_line, vector_ring, vector_came = take(4)
    (load_sem,) = take(1)
    (in_sem,) = take(1)
    carry_send, carry_recv = take(2)
    spread_send, spread_recv, spread_own = take(3)
    packs = [
        Reduce(dp, mp, src, out, stage, recvs[i], lines[i], last[i], (load_sem,) + take(9), waits)
        for i, (src, out) in enumerate(((two_ref, two_out), (one_ref, one_out)))
    ]
    layer = Swap(mp, layer_ref, layer_out, take(3), back=True)
    token = Swap(mp, tokens, token_out, take(3), back=True)
    quarter = shared.shape[0] // mp
    columns = feat.shape[1] // mp
    tiny_shared = Tiny(
        dp, mp, lambda m: shared.at[span_of(m, quarter), :],
        shared_line, shared_ring, shared_came, take(4), waits,
    )
    tiny_vector = Tiny(
        dp, mp, lambda m: vector, vector_line, vector_ring, vector_came, take(4), waits
    )
    tiny_feat = Tiny(
        dp, mp, lambda m: feat.at[:, span_of(m, columns)],
        feat_line, feat_ring, feat_came, take(4), waits,
    )
    loads = [
        pltpu.make_async_copy(src, dst, in_sem.at[i])
        for i, (src, dst) in enumerate(
            (
                (grad_ref, grad), (xn_ref, xn), (x_ref, x), (normed_ref, normed_part),
                (direct_ref, direct), (shared_ref, shared), (vector_ref, vector),
            )
        )
    ]
    count = grad.shape[0]
    blocks = count // TB
    keep = lambda dims: [keep_ref[j] for j in dims]
    every = range(NDIM)
    gives = lax.rem(part, span) != 0
    takes = lax.rem(part + 1, span) != 0

    def carry():
        return remote(outs.at[0 : NDIM * SUB, :], ahead, carry_send.at[0], carry_recv.at[0], "mp", part - 1)

    def slot_of(j):
        return slice(j * SUB, (j + 1) * SUB)

    def adjoint():
        loads[0].wait()
        kept = keep(every)

        def block_step(number, state):
            first = pl.multiple_of((blocks - 1 - number) * TB, TB)
            to_rows(rows, grad[pl.ds(first, TB), :])

            def step(t, state):
                now = row(rows, TB - 1 - t)
                return tuple(kept[j] * state[j] + now for j in every)

            return lax.fori_loop(0, TB, step, state, unroll=4)

        zero = jnp.zeros((SUB, LANES), jnp.float32)
        state = lax.fori_loop(0, blocks, block_step, tuple(zero for _ in every))
        for j in every:
            outs[slot_of(j), :] = state[j]

        @pl.when(gives)
        def _():
            carry().start()

        for j in range(2 * NDIM):
            states[j] = starts_ref[j]
        sums[...] = jnp.zeros_like(sums)
        feat[...] = jnp.zeros_like(feat)
        feat[34:35, :] = ffn_ref[...]
        loads[1].wait()

    def params(low, high):
        half = NDIM // 2

        def block_step(number, _):
            first = pl.multiple_of(number * TB, TB)
            now_xn = xn[pl.ds(first, TB), :].astype(jnp.float32)
            now_grad = grad[pl.ds(first, TB), :]
            to_rows(rows, now_xn)
            for piece in range(SUB):
                turned[pl.ds(piece, TB, stride=SUB), :] = now_grad[:, piece * LANES : (piece + 1) * LANES]
            feat[32:33, :] += jnp.sum(now_grad * now_xn, axis=0, keepdims=True)
            for start in (0, half):
                dims = range(start, start + half)
                kept = keep(dims)

                def step(t, carried):
                    state, slope, weight_sum, keep_sum = carried
                    now = row(rows, t)
                    grad_now = row(turned, t)
                    slope = tuple(kept[j] * slope[j] + state[j] for j in range(half))
                    state = tuple(kept[j] * state[j] + now for j in range(half))
                    weight_sum = tuple(weight_sum[j] + grad_now * state[j] for j in range(half))
                    keep_sum = tuple(keep_sum[j] + grad_now * slope[j] for j in range(half))
                    return (state, slope, weight_sum, keep_sum)

                carried = (
                    tuple(states[j] for j in dims),
                    tuple(states[NDIM + j] for j in dims),
                    tuple(sums[slot_of(j), :] for j in dims),
                    tuple(sums[slot_of(NDIM + j), :] for j in dims),
                )
                state, slope, weight_sum, keep_sum = lax.fori_loop(0, TB, step, carried, unroll=4)
                for place, j in enumerate(dims):
                    states[j] = state[place]
                    states[NDIM + j] = slope[place]
                    sums[slot_of(j), :] = weight_sum[place]
                    sums[slot_of(NDIM + j), :] = keep_sum[place]
            return 0

        lax.fori_loop(low, high, block_step, 0)

    def meet():
        @pl.when(gives)
        def _():
            carry().wait_send()

        @pl.when(jnp.logical_not(takes))
        def _():
            ahead[...] = jnp.zeros_like(ahead)

        @pl.when(takes)
        def _():
            arrived(ahead, carry_recv.at[0])

        for copy in loads[2:5]:
            copy.wait()

    def token_rows(low, high):
        kept = keep(every)

        def block_step(number, state):
            there = pl.ds(pl.multiple_of((blocks - 1 - number) * TB, TB), TB)
            now_grad = grad[there, :]
            to_rows(rows, now_grad)

            def step(t, state):
                place = TB - 1 - t
                now = row(rows, place)
                state = tuple(kept[j] * state[j] + now for j in every)
                terms = [weight_ref[j] * state[j] for j in every]
                while len(terms) > 1:
                    terms = [a + b for a, b in zip(terms[::2], terms[1::2])]
                outs[pl.ds(pl.multiple_of(place * SUB, SUB), SUB), :] = terms[0]
                return state

            state = lax.fori_loop(0, TB, step, state, unroll=4)
            d_xn = from_rows(outs) + now_grad * omega_ref[...]
            d_xn = d_xn + normed_part[there, :].astype(jnp.float32)
            now_x = x[there, :].astype(jnp.float32)
            mean = jnp.mean(now_x, axis=1, keepdims=True)
            power = jnp.mean(now_x * now_x, axis=1, keepdims=True)
            scale = lax.rsqrt(power - mean * mean + EPS)
            normed = (now_x - mean) * scale
            feat[33:34, :] += jnp.sum(d_xn * normed, axis=0, keepdims=True)
            scaled = d_xn * gain_ref[...]
            first = jnp.mean(scaled, axis=1, keepdims=True)
            second = jnp.mean(scaled * normed, axis=1, keepdims=True)
            back = scale * (scaled - first - normed * second)
            tokens[there, :] = (direct[there, :].astype(jnp.float32) + back).astype(jnp.bfloat16)
            return state

        state = tuple(ahead[slot_of(j), :] for j in every)
        state = lax.fori_loop(low, high, block_step, state)
        for j in every:
            ahead[slot_of(j), :] = state[j]

    def gathered():
        for piece in range(SUB):
            feat[0 : 2 * NDIM, piece * LANES : (piece + 1) * LANES] = sums[
                pl.ds(piece, 2 * NDIM, stride=SUB), :
            ]
        token.start()
        tiny_feat.start()

    def shared_back():
        low = shared_ring[bits].astype(jnp.bfloat16)
        shared_low[...] = low
        there = shared_out.at[span_of(part, quarter), :]
        pltpu.make_async_copy(shared_low, there, spread_own.at[0]).start()
        for step in range(1, mp):
            to = lax.rem(part + step, mp)
            copy = remote(shared_low, there, spread_send.at[step], spread_recv.at[part], "mp", to)
            copy.start()
            waits.append(copy.wait_send)

    (turned,) = take(1)

    greet(dp, mp)
    for copy in loads:
        copy.start()
    layer.start()
    work = {
        0: [adjoint],
        1: [lambda: params(0, blocks // 2)],
        2: [lambda: params(blocks // 2, blocks)],
        3: [meet, lambda: token_rows(0, blocks // 2)],
        4: [lambda: token_rows(blocks // 2, blocks), gathered],
    }
    jobs = [(pack, i) for pack in packs for i in range(mp)]
    finals = {}
    for wave in range(len(jobs) + bits + bits + 2):
        for stage_number in range(bits - 1, -1, -1):
            number = wave - stage_number - 1
            if 0 <= number < len(jobs):
                pack, i = jobs[number]
                pack.fold(i, stage_number, number % 2)
                if stage_number == bits - 1 and i == mp - 1:
                    for step in range(bits + 1):
                        finals.setdefault(wave + step, []).append((pack, step))
        if wave < len(jobs):
            jobs[wave][0].begin(jobs[wave][1], wave % 2)
        for pack, step in finals.get(wave, []):
            pack.spread(step)
        for item in work.get(wave, []):
            item()
        if wave == 1:
            loads[5].wait()
            loads[6].wait()
            tiny_shared.start()
            tiny_vector.start()
        for item, first in ((tiny_shared, 3), (tiny_vector, 3), (tiny_feat, 7)):
            if 0 <= wave - first <= bits:
                item.fold(wave - first)
        if wave == 3 + bits:
            shared_back()
            vector_out[...] = vector_ring[bits]
        if wave == 7 + bits:
            feat_out[...] = feat_ring[bits]
    arrived(shared_low, spread_own.at[0])
    for step in range(1, mp):
        source = lax.rem(part + step, mp)
        arrived(shared_out.at[span_of(source, quarter), :], spread_recv.at[source])
    for item in (layer, token):
        item.receive()
        item.close()
    for wait in waits:
        wait()


def closing(dp, mp, span, packs, layer_rows, inputs, shared, vector, params, starts):
    one, two = packs
    low, full = jnp.bfloat16, jnp.float32
    bits = dp.bit_length() - 1
    dma = pltpu.SemaphoreType.DMA
    count = layer_rows.shape[0]
    _, total, width = one.shape
    z = shared.shape[1]
    quarter, columns = D // mp, D // mp

    def vmem(*shape, dtype=full):
        return pltpu.VMEM(shape, dtype)

    scratch = [vmem(2, 2, total // 2, width // 2, dtype=low)]
    for _ in range(2):
        scratch += [vmem(mp, 2, total >> (i + 1), width // 2, dtype=low) for i in range(bits)]
    scratch += [vmem(mp, 2, total // dp, width // 2, dtype=low)] * 2
    scratch += [vmem(2, total // dp, width // 2, dtype=low)] * 2
    scratch += [vmem(count, D)] + [vmem(count, D, dtype=low)] * 5
    scratch += [ROWS, ROWS, pltpu.VMEM(STATES, full), vmem(NDIM * SUB, LANES)]
    scratch += [vmem(2 * NDIM * SUB, LANES), vmem(FEATURES, D)]
    scratch += [
        vmem(D, z, dtype=low), vmem(mp, quarter, z, dtype=low), vmem(bits + 1, quarter, z),
        vmem(bits, quarter, z), vmem(quarter, z, dtype=low),
    ]
    scratch += [vmem(mp, FEATURES, columns), vmem(bits + 1, FEATURES, columns), vmem(bits, FEATURES, columns)]
    scratch += [vmem(8, z), vmem(mp, 8, z), vmem(bits + 1, 8, z), vmem(bits, 8, z)]
    scratch += [dma((2, 2)), dma((7,)), dma((1,)), dma((1,)), dma((mp,)), dma((mp,)), dma((1,))]
    scratch += reduce_sems(dp, mp) * 2 + swap_sems(mp) * 2 + tiny_sems(dp, mp) * 3
    scratch += [ROWS]
    near = pl.BlockSpec(memory_space=pltpu.VMEM)
    return pl.pallas_call(
        functools.partial(closing_kernel, dp, mp, span),
        in_specs=[HBM] * 10 + [near] * 6,
        out_specs=[HBM] * 4 + [near, HBM, near],
        out_shape=[
            sds((total, width), low), sds((total, width), low),
            sds((count * mp, D // mp), low), sds((count * mp, D // mp), low),
            sds((FEATURES, columns)), sds((D, z), low), sds((8, z)),
        ],
        scratch_shapes=scratch,
        compiler_params=pltpu.CompilerParams(
            collective_id=2, has_side_effects=True, vmem_limit_bytes=61 << 20
        ),
        name="closing",
    )(one, two, layer_rows, *inputs, shared, vector, *params, starts)


def local(
    dp,
    mp,
    tokens,
    cotangent,
    norm_gain,
    ema_delta,
    ema_alpha,
    ema_beta,
    ema_eta,
    ema_omega,
    shared_proj,
    query_gain,
    query_bias,
    key_gain,
    value_proj,
    gate_proj,
    mixer_proj,
    update_proj,
    output_proj,
    ffn_gain,
    up_proj,
    down_proj,
):
    width = tokens.shape[1]
    count = tokens.shape[0] // mp
    span = LEN // count
    small = jnp.concatenate(
        [
            ema_delta, ema_alpha, ema_beta, ema_eta,
            norm_gain[:, None], ema_omega[:, None], ffn_gain[:, None],
        ],
        axis=1,
    ).T
    lines = small.shape[0]
    small = jnp.pad(small, ((0, -lines % 8), (0, 0)))
    folded = jnp.concatenate([output_proj[:, : D // 2], output_proj[:, D // 2 :]], axis=0)
    pack_one = jnp.concatenate([value_proj, gate_proj, mixer_proj, update_proj, folded], axis=1)
    pack_two = jnp.concatenate([up_proj, down_proj], axis=1)
    small, one, x_low = opening(dp, mp, jnp.tile(small, (1, mp)), pack_one, tokens)
    small = small.reshape(mp, -1, width).transpose(1, 0, 2).reshape(-1, D)
    delta, alpha, beta, eta = (small[NDIM * i : NDIM * (i + 1)] for i in range(4))
    gain = small[4 * NDIM : 4 * NDIM + 1]
    omega = small[4 * NDIM + 1 : 4 * NDIM + 2]
    gain_two = small[4 * NDIM + 2 : 4 * NDIM + 3]
    rate = jax.nn.sigmoid(delta)
    damp = jax.nn.sigmoid(alpha)
    keep = (1.0 - rate * damp).reshape(STATE)
    weight = (rate * beta * eta).reshape(STATE)

    vectors = (query_gain[None], query_bias[None], key_gain[None])
    wide, narrow = value_proj.shape[1], mixer_proj.shape[1]
    (
        xn, xp, mix_pre, starts, vpre, gpre, att, hidden, act_pre, upd_pre, middle, spre, two, grad_out,
    ) = forward(
        dp, mp, span, mp * wide, x_low, gain, keep, weight, omega, one, shared_proj, vectors,
        pack_two, cotangent,
    )
    layer_rows, ffn_in, upper, d_up, d_act, d_upd, d_inputs, ffn_part = ffn(
        middle, grad_out, x_low, act_pre, upd_pre, two, gain_two
    )
    two_grad = ffn_weights(mp, ffn_in, grad_out, upper, d_up)
    d_value, d_gate, d_shared, d_mix_pre, normed_part, vector_sums = mixer_backward(
        d_act, d_upd, vpre, gpre, att, spre, mix_pre, one, shared_proj, *vectors
    )
    one_grad, shared_part = mixer_weights(
        mp, xn, xp, hidden, d_act, d_value, d_gate, d_upd, d_shared
    )

    one_grad, two_grad, layer_out, token_grad, feature, shared_grad, vector_sums = closing(
        dp, mp, span, (one_grad, two_grad), layer_rows,
        (d_mix_pre, xn, x_low, normed_part, d_inputs), shared_part, vector_sums,
        (keep, weight, gain, omega, ffn_part), starts,
    )
    up_grad = two_grad[:, : up_proj.shape[1]].astype(jnp.float32)
    down_grad = two_grad[:, up_proj.shape[1] :].astype(jnp.float32)
    base = 2 * (wide + narrow)
    value_grad = one_grad[:, :wide].astype(jnp.float32)
    gate_grad = one_grad[:, wide : 2 * wide].astype(jnp.float32)
    mixer_grad = one_grad[:, 2 * wide : 2 * wide + narrow].astype(jnp.float32)
    update_grad = one_grad[:, 2 * wide + narrow : base].astype(jnp.float32)
    output_grad = jnp.concatenate(
        [one_grad[:wide, base:], one_grad[wide:, base:]], axis=1
    ).astype(jnp.float32)

    shared_grad = shared_grad.astype(jnp.float32)
    query_grad, bias_grad, key_grad = vector_sums[0], vector_sums[1], vector_sums[2]
    delta, alpha, beta, eta = (
        item.T for item in (ema_delta, ema_alpha, ema_beta, ema_eta)
    )
    rate = jax.nn.sigmoid(delta)
    damp = jax.nn.sigmoid(alpha)
    weight_sum = feature[:NDIM]
    keep_sum = feature[NDIM : 2 * NDIM] * (rate * beta * eta)
    d_rate = weight_sum * beta * eta - keep_sum * damp
    delta_grad = (d_rate * rate * (1.0 - rate)).T
    alpha_grad = (-keep_sum * rate * damp * (1.0 - damp)).T
    beta_grad = (weight_sum * rate * eta).T
    eta_grad = (weight_sum * rate * beta).T
    omega_grad, gain_grad, ffn_grad = feature[2 * NDIM], feature[2 * NDIM + 1], feature[2 * NDIM + 2]
    return (
        layer_out, token_grad, gain_grad, delta_grad, alpha_grad, beta_grad, eta_grad, omega_grad,
        shared_grad, query_grad, bias_grad, key_grad, value_grad, gate_grad, mixer_grad,
        update_grad, output_grad, ffn_grad, up_grad, down_grad,
    )


def solution(mesh):
    dp, mp = mesh.shape["dp"], mesh.shape["mp"]
    params = (
        P("mp"), P("mp", None), P("mp", None), P("mp", None), P("mp", None), P("mp"),
        P(), P(), P(), P(),
        P(None, "mp"), P(None, "mp"), P(None, "mp"), P(None, "mp"), P("mp", None),
        P("mp"), P(None, "mp"), P("mp", None),
    )
    specs = (P("dp", "mp"), P("dp", "mp")) + params
    return jax.shard_map(
        functools.partial(local, dp, mp), mesh=mesh, in_specs=specs, out_specs=specs, check_vma=False
    )
```

time: 1380 us -> 709 us (0.51)
  waiting for transfers between devices: 682 us -> 0 us
  Pallas kernels: 75.4 us -> 659 us
  matrix products: 256 us -> 0 us
  blocking collectives: 229 us -> 0 us
  other arithmetic: 51.4 us -> 16 us
  starting transfers between devices: 21.5 us -> 0 us
  local copies, waits for them, and re-layouts: 43.2 us -> 25.4 us
  between operations: 15.5 us -> 1.34 us
    pallas_call x5 -> x7, Pallas kernels: 75.4 us -> 659 us  [the longest x1 248 us: closing(): pl.pallas_call(functools.partial(closing_kernel, dp, mp, span), in_specs=...]
    reduce_scatter x14 -> x0, waiting for transfers between devices: 352 us -> none  [the longest x5 120 us: reduce_columns(): lax.psum_scatter(grad.astype(jnp.bfloat16), 'dp', scatter_dimension=0, ti...]
    dot_general x30 -> x0, matrix products: 256 us -> none  [the longest x8 91.4 us: matmul(): return jnp.dot(left, right, preferred_element_type=jnp.float32)]
    all_gather x13 -> x0, waiting for transfers between devices: 185 us -> none  [the longest x3 61.8 us: reduce_columns(): return lax.all_gather(part, 'dp', axis=0, tiled=True).astype(jnp.float32)]
    all_gather x7 -> x0, blocking collectives: 160 us -> none  [the longest x4 73.2 us: gather_columns(): part = lax.all_gather(part, 'mp', axis=1, tiled=True)]
    all_to_all x4 -> x0, waiting for transfers between devices: 89.5 us -> none  [the longest x1 52.7 us: local(): layer_out = lax.all_to_all(layer_rows, 'mp', 1, 0, tiled=True)]
    psum x1 -> x0, blocking collectives: 69 us -> none  [local(): lax.psum((feature, shared_part, query_part, bias_part, key_part), ('dp',...]
    psum x1 -> x0, waiting for transfers between devices: 52.7 us -> none  [local(): lax.psum((feature, shared_part, query_part, bias_part, key_part), ('dp',...]
  transfers between devices with their start and end apart: 34 -> 0, of which waited for: 21 -> 0; matrix products, arithmetic and copies ran while one was open for 18% -> 0% of each run, Pallas kernels for 5% -> 0%
where the time goes in v3:
time: 709 us; the launch traced here: 701 us
  Pallas kernels  659 us (93%)
  local copies, waits for them, and re-layouts  25.4 us (4%)
  other arithmetic  16 us (2%)
    pallas_call x1, Pallas kernels, closing(): pl.pallas_call(functools.partial(closing_kernel, dp, mp, span), in_specs=...  248 us
    pallas_call x1, Pallas kernels, forward(): pl.pallas_call(functools.partial(forward_kernel, dp, mp, span), grid=(2 *...  159 us
    pallas_call x1, Pallas kernels, opening(): pl.pallas_call(functools.partial(opening_kernel, dp, mp), in_specs=[HBM]...  107 us
    pallas_call x1, Pallas kernels, ffn(): pl.pallas_call(ffn_kernel, grid=(count // ROWS_C,), in_specs=[rows_block(...  57 us
    pallas_call x1, Pallas kernels, mixer_backward(): pl.pallas_call(mixer_backward_kernel, grid=(count // ROWS_C,), in_specs=[...  36.6 us
    pallas_call x1, Pallas kernels, mixer_weights(): pl.pallas_call(mixer_weights_kernel, grid=(mp,), in_specs=[held(count, D)...  26.4 us
    pallas_call x1, Pallas kernels, ffn_weights(): pl.pallas_call(ffn_weights_kernel, grid=(mp,), in_specs=[held(count, D),...  24.2 us
    unnamed x43, local copies, waits for them, and re-layouts  14.9 us

profile of v3, /device:TPU:0, one launch (start us, length us, event | category | flops | bytes accessed | tf_op | source)
XLA Modules:
  0.0 701.2 jit_solution(17375427587074241857)
XLA Ops:
  0.7 0.0 copy-start.10
  0.7 0.0 copy-start.9
  0.7 3.7 concatenate.15
  4.4 0.0 copy-start.11
  4.4 0.1 tile.4
  4.5 0.1 copy.41
  4.5 1.3 fusion.17
  5.8 0.0 copy-start.7
  5.9 0.0 copy-start.8
  5.9 1.5 constant_dynamic-update-slice_fusion.3
  7.4 0.0 copy-done.9
  7.4 0.1 constant_dynamic-update-slice_fusion.2
  7.6 0.0 copy-done.10
  7.6 0.1 constant_dynamic-update-slice_fusion.1
  7.6 0.0 copy-done.11
  7.6 0.1 constant_dynamic-update-slice_fusion
  7.7 0.2 maximum_dynamic-update-slice_fusion.pack_ref
  7.9 0.0 copy-done.7
  7.9 0.5 copy-done.8
  8.4 0.0 copy-start.2
  8.4 2.5 pad_maximum_fusion.pack_ref
  10.8 0.0 copy-done.2
  10.8 107.4 %opening.1 = (f32[288,256]{1,0:T(8,128)S(1)}, bf16[4,1024,2048]{2,1,0:T(8,128)(2,1)S(1)}, bf16[1024,1024]{1,0:T(8,128)(2,1)S(1)}) custom-call(f32[72,1024]{1,0:T(8,128)S(1)} %bitcast.103, bf16[1024,2048]{1,0:T(8,128)(2,1)S(1)} %maximum_dynamic-update-slice_fusion.pack_ref, bf16[4096,256]{1,0:T(8,128)(2,1)S(1)} %copy-done.2), custom_call_target="tpu_custom_call" | custom-call | tf_op jit(solution)/shard_map/opening/pallas_call | solution.py:664
  118.2 0.0 copy-start
  118.2 5.7 copy-done
  124.0 0.0 copy-start.1
  124.0 1.3 copy-done.1
  125.3 0.1 copy.46
  125.4 0.1 slice_multiply_fusion
  125.5 0.6 reshape.79.weight_ref
  126.1 0.6 copy.44
  126.7 0.6 copy.43
  127.3 0.6 copy.42
  127.9 0.7 reshape.78.keep_ref
  128.6 158.8 %forward.1 = (bf16[1024,1024]{1,0:T(8,128)(2,1)}, bf16[1024,1024]{1,0:T(8,128)(2,1)}, f32[1024,1024]{1,0:T(8,128)}, f32[32,8,128]{2,1,0:T(8,128)}, bf16[1024,204...) custom-call(bf16[1024,1024]{1,0:T(8,128)(2,1)} %copy-done.1, ...), custom_call_target="tpu_custom_call" | custom-call | tf_op jit(solution)/shard_map/forward/pallas_call | solution.py:820
  287.4 57.0 %ffn.1 = (bf16[1024,1024]{1,0:T(8,128)(2,1)}, bf16[1024,1024]{1,0:T(8,128)(2,1)}, bf16[1024,4096]{1,0:T(8,128)(2,1)}, bf16[1024,4096]{1,0:T(8,128)(2,1)}, bf16[1...) custom-call(f32[1024,1024]{1,0:T(8,128)} %get-tuple-element.66.mid_ref, ...), custom_call_target="tpu_custom_call" | custom-call | flops 34359738368 | bytes 62914560 | tf_op jit(solution)/shard_map/ffn/pallas_call | solution.py:333
  344.4 36.6 %mixer_backward.1 = (bf16[1024,2048]{1,0:T(8,128)(2,1)}, bf16[1024,2048]{1,0:T(8,128)(2,1)}, bf16[1024,128]{1,0:T(8,128)(2,1)}, f32[1024,1024]{1,0:T(8,128)}, bf...) custom-call(bf16[1024,1024]{1,0:T(8,128)(2,1)} %get-tuple-element.71.dact_ref.dact_all_ref, ...), custom_call_target="tpu_custom_call" | custom-call | flops 17448304640 | bytes 62914560 | tf_op jit(solution)/shard_map/mixer_backward/pallas_call | solution.py:353
  381.0 24.2 %ffn_weights.1.two_ref = bf16[4,1024,2048]{2,1,0:T(8,128)(2,1)} custom-call(bf16[1024,1024]{1,0:T(8,128)(2,1)} %get-tuple-element.82.ffn_ref, bf16[1024,1024]{1,0:T(8,128)(2,1)} %get-tuple-element.67.grad_ref, bf16[1024,4096]{1,0:T(8,128)(2,1)} %get-tuple-element.83.upper_ref, bf16[1024,4096]{1,0:T(8,128)(2,1)} %get-tuple-element.84.dup_ref), custom_call_target="tpu_custom_call" | custom-call | flops 17179869184 | bytes 41943040 | tf_op jit(solution)/shard_map/ffn_weights/pallas_call | solution.py:404
  405.2 26.4 %mixer_weights.1 = (bf16[4,1024,2048]{2,1,0:T(8,128)(2,1)}, bf16[1024,128]{1,0:T(8,128)(2,1)}) custom-call(bf16[1024,1024]{1,0:T(8,128)(2,1)} %get-tuple-element.63.xn_ref, bf16[1024,1024]{1,0:T(8,128)(2,1)} %get-tuple-element.64.xp_ref, bf16[1024,2048]{1,0:T(8,128)(2,1)} %get-tuple-element.65.hid_ref, ...), custom_call_target="tpu_custom_call" | custom-call | flops 17179869184 | bytes 41943040 | tf_op jit(solution)/shard_map/mixer_weights/pallas_call | solution.py:379
  431.6 0.0 copy-start.12
  431.6 0.0 copy-start.14
  431.6 0.0 copy-start.15
  431.6 248.1 %closing.1 = (bf16[1024,2048]{1,0:T(8,128)(2,1)}, bf16[1024,2048]{1,0:T(8,128)(2,1)}, bf16[4096,256]{1,0:T(8,128)(2,1)}, bf16[4096,256]{1,0:T(8,128)(2,1)}, f32[...) custom-call(bf16[4,1024,2048]{2,1,0:T(8,128)(2,1)} %get-tuple-element.81.one_ref, ...), custom_call_target="tpu_custom_call" | custom-call | tf_op jit(solution)/shard_map/closing/pallas_call | solution.py:1352
  679.8 0.0 copy-start.4
  679.8 1.4 slice_bitcast_fusion.3
  681.1 1.4 fusion.18
  682.5 0.0 copy-done.12
  682.5 0.0 copy-done.13
  682.5 0.0 copy-done.14
  682.5 0.0 copy-done.15
  682.5 1.4 fusion.11
  683.9 1.8 convert_element_type.26
  685.7 1.3 fusion.16
  687.0 1.6 maximum_convert_fusion
  688.6 0.0 copy-done.4
  688.6 0.0 copy-start.3
  688.6 1.5 slice_convert_fusion.4
  690.1 2.6 slice_convert_fusion.2
  692.7 0.0 copy-done.3
  692.7 4.4 slice_convert_fusion
  697.1 0.0 copy-done.6
  697.1 1.3 copy.53
  698.4 1.0 copy-done.5
  699.5 1.3 copy.54
  (5 shorter events, 0.0 us)
Async XLA Ops:
  0.7 6.9 copy-start.10
  0.7 6.7 copy-start.9
  4.4 3.2 copy-start.11
  5.8 2.0 copy-start.7
  5.9 2.5 copy-start.8
  8.4 2.5 copy-start.2
  118.2 5.7 copy-start
  124.0 1.3 copy-start.1
  431.6 250.9 %copy-start.12 = (f32[256,16]{0,1:T(8,128)S(1)}, f32[256,16]{0,1:T(8,128)}, u32[]{:S(2)}) copy-start(f32[256,16]{0,1:T(8,128)} %param.23) | copy-start | bytes 49156
  431.6 250.9 %copy-start.13 = (f32[256,16]{0,1:T(8,128)S(1)}, f32[256,16]{0,1:T(8,128)}, u32[]{:S(2)}) copy-start(f32[256,16]{0,1:T(8,128)} %param.24) | copy-start | bytes 49156
  431.6 250.9 %copy-start.14 = (f32[256,16]{0,1:T(8,128)S(1)}, f32[256,16]{0,1:T(8,128)}, u32[]{:S(2)}) copy-start(f32[256,16]{0,1:T(8,128)} %param.25) | copy-start | bytes 49156
  431.6 250.9 %copy-start.15 = (f32[256,16]{0,1:T(8,128)S(1)}, f32[256,16]{0,1:T(8,128)}, u32[]{:S(2)}) copy-start(f32[256,16]{0,1:T(8,128)} %param.26) | copy-start | bytes 49156
  679.8 8.8 %copy-start.4 = (bf16[1024,2048]{1,0:T(8,128)(2,1)S(1)}, bf16[1024,2048]{1,0:T(8,128)(2,1)}, u32[]{:S(2)}) copy-start(bf16[1024,2048]{1,0:T(8,128)(2,1)} %get-tuple-element.98) | copy-start | bytes 12582916
  688.6 4.1 copy-start.3
  692.7 4.4 copy-start.6
  697.1 2.3 copy-start.5

commit v4 on v3

--- a/solution.py
+++ b/solution.py
@@ -467,7 +467,7 @@
 class Swap:
     def __init__(self, mp, src, dst, sems, back=False):
         self.mp, self.src, self.dst, self.back = mp, src, dst, back
-        self.send, self.recv, self.own = sems
+        self.hold, self.send, self.recv, self.own = sems
         self.part = lax.axis_index("mp")
         if back:
             self.rows, self.width = src.shape[0], dst.shape[1]
@@ -484,8 +484,11 @@
             return self.dst.at[span_of(index, self.rows), :]
         return self.dst.at[:, span_of(index, self.width)]
 
-    def local(self):
-        return pltpu.make_async_copy(self.piece(self.part), self.place(self.part), self.own.at[0])
+    def load(self):
+        return pltpu.make_async_copy(self.piece(self.part), self.hold, self.own.at[0])
+
+    def store(self):
+        return pltpu.make_async_copy(self.hold, self.place(self.part), self.own.at[1])
 
     def copies(self):
         for step in range(1, self.mp):
@@ -496,12 +499,16 @@
             )
 
     def start(self):
-        self.local().start()
+        self.load().start()
         for copy in self.copies():
             copy.start()
 
+    def turn(self):
+        self.load().wait()
+        self.store().start()
+
     def receive(self):
-        self.local().wait()
+        self.store().wait()
         for step in range(1, self.mp):
             source = lax.rem(self.part + step, self.mp)
             arrived(self.place(source), self.recv.at[source])
@@ -514,21 +521,28 @@
 class Gather:
     def __init__(self, dp, mp, src, dst, sems):
         self.dp, self.mp, self.src, self.dst = dp, mp, src, dst
-        self.line_send, self.pass_send, self.line_recv, self.send, self.recv, self.own = sems
+        self.hold, self.line_send, self.pass_send, self.line_recv, self.send, self.recv, self.own = sems
         self.me, self.part = lax.axis_index("dp"), lax.axis_index("mp")
         self.bits = dp.bit_length() - 1
         self.orders = orders_of(dp)
 
     def region(self, ref, half, index, held):
-        total, width = ref.shape[0], ref.shape[1] // 2
+        total = ref.shape[0] // 2
         share = total // self.dp
         first = lax.div(rank_of(index, self.orders[half]), 1 << held) * (share << held)
-        return ref.at[
-            pl.ds(pl.multiple_of(first, share), share << held), half * width : (half + 1) * width
-        ]
-
-    def local(self):
-        return pltpu.make_async_copy(self.src, self.dst.at[self.part], self.own.at[0])
+        return ref.at[pl.ds(pl.multiple_of(half * total + first, share), share << held), :]
+
+    def load(self):
+        there = self.dst.at[self.part] if self.hold is None else self.hold
+        return pltpu.make_async_copy(self.src, there, self.own.at[0])
+
+    def store(self):
+        return pltpu.make_async_copy(self.hold, self.dst.at[self.part], self.own.at[1])
+
+    def turn(self):
+        self.load().wait()
+        if self.hold is not None:
+            self.store().start()
 
     def first(self, up):
         to = self.part + 1 if up else self.part - 1
@@ -576,7 +590,7 @@
                 for copy in self.first(up):
                     copy.start()
 
-        self.local().start()
+        self.load().start()
 
     def advance(self, step, stage):
         source = self.source(step)
@@ -608,7 +622,8 @@
                 self.advance(number - stage, stage)
 
     def close(self):
-        self.local().wait()
+        if self.hold is not None:
+            self.store().wait()
         for up in (True, False):
 
             @pl.when(self.part < self.mp - 1 if up else self.part > 0)
@@ -629,87 +644,94 @@
                     copy.wait_send()
 
 
-def swap_sems(mp):
+def swap_scratch(mp, rows, width, dtype=jnp.bfloat16):
     dma = pltpu.SemaphoreType.DMA
-    return [dma((mp,)), dma((mp,)), dma((1,))]
-
-
-def gather_sems(dp, mp):
+    return [pltpu.VMEM((rows, width), dtype), dma((mp,)), dma((mp,)), dma((2,))]
+
+
+def gather_scratch(dp, mp, pack):
     dma = pltpu.SemaphoreType.DMA
     bits = dp.bit_length() - 1
-    return [dma((2, 2)), dma((mp, 2)), dma((mp, 2)), dma((bits, mp, 2)), dma((bits, mp, 2)), dma((1,))]
+    return [
+        pltpu.VMEM(pack.shape, pack.dtype), dma((2, 2)), dma((mp, 2)), dma((mp, 2)),
+        dma((bits, mp, 2)), dma((bits, mp, 2)), dma((2,)),
+    ]
 
 
 HBM = pl.BlockSpec(memory_space=pl.ANY)
-
-
-def opening_kernel(dp, mp, small_ref, pack_ref, tok_ref, small_out, full_ref, rows_ref, *sems):
-    swap = Swap(mp, tok_ref, rows_ref, sems[0:3])
-    tiny = Swap(mp, small_ref, small_out, sems[3:6], back=True)
-    plan = Gather(dp, mp, pack_ref, full_ref, sems[6:12])
-    greet(dp, mp)
-    tiny.start()
-    plan.start()
-    for number in range(plan.waves()):
-        plan.wave(number)
-        if number == mp - 2:
-            swap.start()
-    for item in (tiny, swap):
-        item.receive()
-        item.close()
-    plan.close()
-
-
-def opening(dp, mp, small, pack, tokens):
-    return pl.pallas_call(
-        functools.partial(opening_kernel, dp, mp),
-        in_specs=[HBM] * 3,
-        out_specs=[HBM] * 3,
-        out_shape=[
-            sds((mp * small.shape[0], small.shape[1] // mp)),
-            sds((mp,) + pack.shape, pack.dtype),
-            sds((tokens.shape[0] // mp, tokens.shape[1] * mp), tokens.dtype),
-        ],
-        scratch_shapes=swap_sems(mp) * 2 + gather_sems(dp, mp),
-        compiler_params=pltpu.CompilerParams(
-            collective_id=0, has_side_effects=True, vmem_limit_bytes=4 << 20
-        ),
-        name="opening",
-    )(small, pack, tokens)
 
 
 def forward_kernel(
     dp, mp, span,
-    x_ref, gain_ref, keep_ref, weight_ref, omega_ref,
-    one_ref, shared_ref, qgain_ref, qbias_ref, kgain_ref, pack_ref, cot_ref,
-    xn_ref, xp_ref, mix_ref, starts_ref,
+    small_ref, first_ref, tok_ref, shared_ref, qgain_ref, qbias_ref, kgain_ref, pack_ref, cot_ref,
+    xn_ref, xp_ref, mix_ref, starts_ref, keep_ref, weight_ref, gains_ref,
     vpre_ref, gpre_ref, att_ref, hid_ref, act_ref, upd_ref, mid_ref, spre_ref,
-    full_ref, grad_ref,
-    xn_all, rows, outs, ends, starts, state_ref, carry_send, carry_recv, *sems,
+    one_out, x_out, full_ref, grad_ref,
+    one_ref, x_all, small_all, xn_all, rows, outs, ends, starts, state_ref,
+    carry_send, carry_recv, out_sem, *sems,
 ):
     index = pl.program_id(0)
     steps = pl.num_programs(0) // 2
     part = lax.axis_index("mp")
-    swap = Swap(mp, cot_ref, grad_ref, sems[0:3])
-    plan = Gather(dp, mp, pack_ref, full_ref, sems[3:9])
+    swap = Swap(mp, cot_ref, grad_ref, sems[0:4])
+    plan = Gather(dp, mp, pack_ref, full_ref, sems[4:11])
+    tokens = Swap(mp, tok_ref, x_all, sems[11:15])
+    tiny = Swap(mp, small_ref, small_all, sems[15:19], back=True)
+    opening = Gather(dp, mp, first_ref, one_ref, (None,) + tuple(sems[19:25]))
     gives = lax.rem(part + 1, span) != 0
     takes = lax.rem(part, span) != 0
+    gain_ref, omega_ref = gains_ref.at[0:1, :], gains_ref.at[1:2, :]
 
     def carry():
         return remote(ends, starts, carry_send.at[0], carry_recv.at[0], "mp", part + 1)
+
+    def one_copy():
+        return pltpu.make_async_copy(one_ref, one_out, out_sem.at[0])
+
+    def x_copy():
+        return pltpu.make_async_copy(x_all, x_out, out_sem.at[1])
 
     @pl.when(index == 0)
     def _():
         greet(dp, mp)
+        tiny.start()
+        opening.start()
+        tiny.turn()
+        opening.turn()
+        for number in range(opening.waves()):
+            opening.wave(number)
+            if number == mp - 2:
+                tokens.start()
         plan.start()
+        tokens.turn()
+        tiny.receive()
+        lines = small_all.shape[0] // mp
+        width = small_all.shape[1]
+        gains_ref[...] = jnp.zeros_like(gains_ref)
+        for m in range(mp):
+            block = small_all[m * lines : (m + 1) * lines, :]
+            delta, alpha, beta, eta = (block[NDIM * i : NDIM * (i + 1), :] for i in range(4))
+            rate = jax.nn.sigmoid(delta)
+            keep = 1.0 - rate * jax.nn.sigmoid(alpha)
+            weight = rate * beta * eta
+            for piece in range(width // LANES):
+                there = pl.ds(m * (width // LANES) + piece, NDIM, stride=SUB)
+                keep_ref[there, :] = keep[:, piece * LANES : (piece + 1) * LANES]
+                weight_ref[there, :] = weight[:, piece * LANES : (piece + 1) * LANES]
+            gains_ref[0:3, m * width : (m + 1) * width] = block[4 * NDIM : 4 * NDIM + 3, :]
+        tokens.receive()
+        one_copy().start()
+        x_copy().start()
         ends[...] = jnp.zeros_like(ends)
 
     @pl.when(index < steps)
     def _():
-        keep = [keep_ref[j] for j in range(NDIM)]
+        keep = [keep_ref[j * SUB : (j + 1) * SUB, :] for j in range(NDIM)]
         for piece in range(ROWS_C // TB):
             here = slice(piece * TB, (piece + 1) * TB)
-            x = x_ref[here, :].astype(jnp.float32)
+            x = x_all[
+                pl.ds(pl.multiple_of(index * ROWS_C + piece * TB, TB), TB), :
+            ].astype(jnp.float32)
             mean = jnp.mean(x, axis=1, keepdims=True)
             power = jnp.mean(x * x, axis=1, keepdims=True)
             scale = lax.rsqrt(power - mean * mean + EPS)
@@ -738,7 +760,7 @@
         def _():
             carry().start()
 
-        plan.wave(0)
+        plan.turn()
 
     @pl.when(index == steps)
     def _():
@@ -766,12 +788,12 @@
                 pl.ds(pl.multiple_of((index - steps) * ROWS_C + piece * TB, TB), TB), :
             ].astype(jnp.float32)
             to_rows(rows, xn)
-            keep = [keep_ref[j] for j in range(NDIM)]
+            keep = [keep_ref[j * SUB : (j + 1) * SUB, :] for j in range(NDIM)]
 
             def step(t, state):
                 now = row(rows, t)
                 state = tuple(keep[j] * state[j] + now for j in range(NDIM))
-                terms = [weight_ref[j] * state[j] for j in range(NDIM)]
+                terms = [weight_ref[j * SUB : (j + 1) * SUB, :] * state[j] for j in range(NDIM)]
                 while len(terms) > 1:
                     terms = [a + b for a, b in zip(terms[::2], terms[1::2])]
                 outs[pl.ds(pl.multiple_of(t * SUB, SUB), SUB), :] = terms[0]
@@ -784,30 +806,32 @@
             mix_ref[here, :] = mix
             xp_ref[here, :] = (mix * sigmoid(mix)).astype(jnp.bfloat16)
 
-        xn_block = xn_all.at[pl.ds(pl.multiple_of((index - steps) * ROWS_C, ROWS_C), ROWS_C), :]
+        there = pl.ds(pl.multiple_of((index - steps) * ROWS_C, ROWS_C), ROWS_C)
         mixer_forward_kernel(
-            xn_block, xp_ref, x_ref, one_ref, shared_ref, qgain_ref, qbias_ref, kgain_ref,
+            xn_all.at[there, :], xp_ref, x_all.at[there, :], one_ref, shared_ref, qgain_ref, qbias_ref, kgain_ref,
             vpre_ref, gpre_ref, att_ref, hid_ref, act_ref, upd_ref, mid_ref, spre_ref,
         )
 
-    for number in range(1, plan.waves()):
-        at = jnp.minimum(steps + number - 1, 2 * steps - 1)
-
-        @pl.when(index == at)
+    for number in range(plan.waves()):
+
+        @pl.when(index == jnp.minimum(number + 2, 2 * steps - 1))
         def _(number=number):
             plan.wave(number)
-            if number == mp - 2:
+            if number == 0:
                 swap.start()
 
     @pl.when(index == 2 * steps - 1)
     def _():
+        swap.turn()
         swap.receive()
-        swap.close()
-        plan.close()
-
-
-def forward(dp, mp, span, units, x, gain, keep, weight, omega, one, shared, vectors, pack, cotangent):
-    count = x.shape[0]
+        for item in (swap, plan, tokens, tiny, opening):
+            item.close()
+        one_copy().wait()
+        x_copy().wait()
+
+
+def forward(dp, mp, span, units, small, first, tokens, shared, vectors, pack, cotangent):
+    count = tokens.shape[0] // mp
     steps = count // ROWS_C
     z = shared.shape[1]
     low = jnp.bfloat16
@@ -817,36 +841,42 @@
         return pl.BlockSpec((ROWS_C, width), lambda i: (jnp.maximum(i - steps, 0), 0))
 
     dma = pltpu.SemaphoreType.DMA
+    lines, width = small.shape[0], small.shape[1] // mp
     return pl.pallas_call(
         functools.partial(forward_kernel, dp, mp, span),
         grid=(2 * steps,),
-        in_specs=[pl.BlockSpec((ROWS_C, D), lambda i: (lax.rem(i, steps), 0))]
-        + [held(1, D), held(*STATE), held(*STATE), held(1, D)]
-        + [held(*one.shape), held(*shared.shape)]
-        + [held(1, z)] * 3
-        + [HBM] * 2,
+        in_specs=[HBM] * 3 + [held(*shared.shape)] + [held(1, z)] * 3 + [HBM] * 2,
         out_specs=[early, late(D), late(D), whole(*STATES)]
+        + [whole(NDIM * SUB, LANES)] * 2
+        + [whole(8, D)]
         + [late(units)] * 4
         + [late(D)] * 3
         + [late(z)]
-        + [HBM] * 2,
+        + [HBM] * 4,
         out_shape=[sds((count, D), low), sds((count, D), low), sds((count, D)), sds(STATES)]
+        + [sds((NDIM * SUB, LANES))] * 2
+        + [sds((8, D))]
         + [sds((count, units), low)] * 4
         + [sds((count, D), low)] * 2
         + [sds((count, D)), sds((count, z))]
+        + [sds((mp,) + first.shape, low), sds((count, D), low)]
         + [sds((mp,) + pack.shape, low), sds((count, D), low)],
         scratch_shapes=[
-            pltpu.VMEM((count, D), low), ROWS, ROWS,
+            pltpu.VMEM((mp,) + first.shape, low), pltpu.VMEM((count, D), low),
+            pltpu.VMEM((mp * lines, width), jnp.float32), pltpu.VMEM((count, D), low), ROWS, ROWS,
             pltpu.VMEM(STATES, jnp.float32), pltpu.VMEM(STATES, jnp.float32),
-            pltpu.VMEM(STATE, jnp.float32), dma((1,)), dma((1,)),
+            pltpu.VMEM(STATE, jnp.float32), dma((1,)), dma((1,)), dma((2,)),
         ]
-        + swap_sems(mp)
-        + gather_sems(dp, mp),
+        + swap_scratch(mp, count, cotangent.shape[1])
+        + gather_scratch(dp, mp, pack)
+        + swap_scratch(mp, count, tokens.shape[1])
+        + swap_scratch(mp, lines, width, small.dtype)
+        + gather_scratch(dp, mp, first)[1:],
         compiler_params=pltpu.CompilerParams(
-            collective_id=1, has_side_effects=True, vmem_limit_bytes=60 << 20
+            collective_id=1, has_side_effects=True, vmem_limit_bytes=61 << 20
         ),
         name="forward",
-    )(x, gain, keep, weight, omega, one, shared, *vectors, pack, cotangent)
+    )(small, first, tokens, shared, *vectors, pack, cotangent)
 
 
 def add_rows(acc, first, other, count):
@@ -1048,6 +1078,7 @@
 
 
 FEATURES = 40
+LAG = 2
 
 
 def closing_kernel(
@@ -1082,8 +1113,8 @@
         Reduce(dp, mp, src, out, stage, recvs[i], lines[i], last[i], (load_sem,) + take(9), waits)
         for i, (src, out) in enumerate(((two_ref, two_out), (one_ref, one_out)))
     ]
-    layer = Swap(mp, layer_ref, layer_out, take(3), back=True)
-    token = Swap(mp, tokens, token_out, take(3), back=True)
+    layer = Swap(mp, layer_ref, layer_out, take(4), back=True)
+    token = Swap(mp, tokens, token_out, take(4), back=True)
     quarter = shared.shape[0] // mp
     columns = feat.shape[1] // mp
     tiny_shared = Tiny(
@@ -1279,9 +1310,10 @@
     }
     jobs = [(pack, i) for pack in packs for i in range(mp)]
     finals = {}
-    for wave in range(len(jobs) + bits + bits + 2):
-        for stage_number in range(bits - 1, -1, -1):
-            number = wave - stage_number - 1
+    lags = [1 + LAG * stage_number for stage_number in range(bits)]
+    for wave in range(len(jobs) + lags[-1] + bits + 2):
+        for stage_number in range(bits):
+            number = wave - lags[stage_number]
             if 0 <= number < len(jobs):
                 pack, i = jobs[number]
                 pack.fold(i, stage_number, number % 2)
@@ -1295,6 +1327,7 @@
         for item in work.get(wave, []):
             item()
         if wave == 1:
+            layer.turn()
             loads[5].wait()
             loads[6].wait()
             tiny_shared.start()
@@ -1311,6 +1344,7 @@
     for step in range(1, mp):
         source = lax.rem(part + step, mp)
         arrived(shared_out.at[span_of(source, quarter), :], spread_recv.at[source])
+    token.turn()
     for item in (layer, token):
         item.receive()
         item.close()
@@ -1346,7 +1380,7 @@
     scratch += [vmem(mp, FEATURES, columns), vmem(bits + 1, FEATURES, columns), vmem(bits, FEATURES, columns)]
     scratch += [vmem(8, z), vmem(mp, 8, z), vmem(bits + 1, 8, z), vmem(bits, 8, z)]
     scratch += [dma((2, 2)), dma((7,)), dma((1,)), dma((1,)), dma((mp,)), dma((mp,)), dma((1,))]
-    scratch += reduce_sems(dp, mp) * 2 + swap_sems(mp) * 2 + tiny_sems(dp, mp) * 3
+    scratch += reduce_sems(dp, mp) * 2 + swap_scratch(mp, count, D // mp) * 2 + tiny_sems(dp, mp) * 3
     scratch += [ROWS]
     near = pl.BlockSpec(memory_space=pltpu.VMEM)
     return pl.pallas_call(
@@ -1405,25 +1439,17 @@
     folded = jnp.concatenate([output_proj[:, : D // 2], output_proj[:, D // 2 :]], axis=0)
     pack_one = jnp.concatenate([value_proj, gate_proj, mixer_proj, update_proj, folded], axis=1)
     pack_two = jnp.concatenate([up_proj, down_proj], axis=1)
-    small, one, x_low = opening(dp, mp, jnp.tile(small, (1, mp)), pack_one, tokens)
-    small = small.reshape(mp, -1, width).transpose(1, 0, 2).reshape(-1, D)
-    delta, alpha, beta, eta = (small[NDIM * i : NDIM * (i + 1)] for i in range(4))
-    gain = small[4 * NDIM : 4 * NDIM + 1]
-    omega = small[4 * NDIM + 1 : 4 * NDIM + 2]
-    gain_two = small[4 * NDIM + 2 : 4 * NDIM + 3]
-    rate = jax.nn.sigmoid(delta)
-    damp = jax.nn.sigmoid(alpha)
-    keep = (1.0 - rate * damp).reshape(STATE)
-    weight = (rate * beta * eta).reshape(STATE)
-
     vectors = (query_gain[None], query_bias[None], key_gain[None])
     wide, narrow = value_proj.shape[1], mixer_proj.shape[1]
     (
-        xn, xp, mix_pre, starts, vpre, gpre, att, hidden, act_pre, upd_pre, middle, spre, two, grad_out,
+        xn, xp, mix_pre, starts, keep, weight, gains,
+        vpre, gpre, att, hidden, act_pre, upd_pre, middle, spre, one, x_low, two, grad_out,
     ) = forward(
-        dp, mp, span, mp * wide, x_low, gain, keep, weight, omega, one, shared_proj, vectors,
+        dp, mp, span, mp * wide, jnp.tile(small, (1, mp)), pack_one, tokens, shared_proj, vectors,
         pack_two, cotangent,
     )
+    keep, weight = keep.reshape(STATE), weight.reshape(STATE)
+    gain, omega, gain_two = gains[0:1], gains[1:2], gains[2:3]
     layer_rows, ffn_in, upper, d_up, d_act, d_upd, d_inputs, ffn_part = ffn(
         middle, grad_out, x_low, act_pre, upd_pre, two, gain_two
     )

time: 709 us -> 632 us (0.89)
  Pallas kernels: 659 us -> 585 us
    pallas_call x1 -> x0, Pallas kernels: 107 us -> none  [opening(): pl.pallas_call(functools.partial(opening_kernel, dp, mp), in_specs=[HBM]...]
    pallas_call x1, Pallas kernels: 159 us -> 222 us  [forward(): pl.pallas_call(functools.partial(forward_kernel, dp, mp, span), grid=(2 *...]
    pallas_call x1, Pallas kernels: 248 us -> 219 us  [closing(): pl.pallas_call(functools.partial(closing_kernel, dp, mp, span), in_specs=...]
    unnamed x43 -> x33, local copies, waits for them, and re-layouts: 14.9 us -> 9.59 us
where the time goes in v4:
time: 632 us; the launch traced here: 623 us
  Pallas kernels  585 us (93%)
  local copies, waits for them, and re-layouts  20.1 us (3%)
  other arithmetic  16.8 us (3%)
    pallas_call x1, Pallas kernels, forward(): pl.pallas_call(functools.partial(forward_kernel, dp, mp, span), grid=(2 *...  222 us
    pallas_call x1, Pallas kernels, closing(): pl.pallas_call(functools.partial(closing_kernel, dp, mp, span), in_specs=...  219 us
    pallas_call x1, Pallas kernels, ffn(): pl.pallas_call(ffn_kernel, grid=(count // ROWS_C,), in_specs=[rows_block(...  56.9 us
    pallas_call x1, Pallas kernels, mixer_backward(): pl.pallas_call(mixer_backward_kernel, grid=(count // ROWS_C,), in_specs=[...  36.6 us
    pallas_call x1, Pallas kernels, mixer_weights(): pl.pallas_call(mixer_weights_kernel, grid=(mp,), in_specs=[held(count, D)...  26.3 us
    pallas_call x1, Pallas kernels, ffn_weights(): pl.pallas_call(ffn_weights_kernel, grid=(mp,), in_specs=[held(count, D),...  24.2 us

profile of v4, /device:TPU:0, one launch (start us, length us, event | category | flops | bytes accessed | tf_op | source)
XLA Modules:
  0.0 622.7 jit_solution(10382086037325229184)
XLA Ops:
  0.7 0.0 copy-start.7
  0.7 0.0 copy-start.6
  0.7 3.7 concatenate.15
  4.4 0.0 copy-start.8
  4.4 0.1 tile.4
  4.5 0.8 copy.40
  5.2 1.3 fusion.11
  6.5 0.0 copy-start.4
  6.5 0.0 copy-start.5
  6.5 2.4 constant_dynamic-update-slice_fusion.3
  9.0 0.0 copy-done.6
  9.0 1.0 constant_dynamic-update-slice_fusion.2
  10.0 0.0 copy-done.7
  10.0 0.8 constant_dynamic-update-slice_fusion.1
  10.8 0.0 copy-done.8
  10.8 0.8 constant_dynamic-update-slice_fusion
  11.7 1.0 maximum_dynamic-update-slice_fusion.first_ref
  12.7 0.0 copy-done.4
  12.7 0.0 copy-done.5
  12.7 2.5 pad_maximum_fusion.pack_ref
  15.1 221.7 %forward.1 = (bf16[1024,1024]{1,0:T(8,128)(2,1)}, bf16[1024,1024]{1,0:T(8,128)(2,1)}, f32[1024,1024]{1,0:T(8,128)}, f32[32,8,128]{2,1,0:T(8,128)}, f32[128,128]{...) custom-call(f32[72,1024]{1,0:T(8,128)} %bitcast.92, ...), custom_call_target="tpu_custom_call" | custom-call | tf_op jit(solution)/shard_map/forward/pallas_call | solution.py:845
  236.9 1.5 fusion.13
  238.3 56.9 %ffn.1 = (bf16[1024,1024]{1,0:T(8,128)(2,1)}, bf16[1024,1024]{1,0:T(8,128)(2,1)}, bf16[1024,4096]{1,0:T(8,128)(2,1)}, bf16[1024,4096]{1,0:T(8,128)(2,1)}, bf16[1...) custom-call(f32[1024,1024]{1,0:T(8,128)} %get-tuple-element.65.mid_ref, ...), custom_call_target="tpu_custom_call" | custom-call | flops 34359738368 | bytes 62914560 | tf_op jit(solution)/shard_map/ffn/pallas_call | solution.py:333
  295.3 36.6 %mixer_backward.1 = (bf16[1024,2048]{1,0:T(8,128)(2,1)}, bf16[1024,2048]{1,0:T(8,128)(2,1)}, bf16[1024,128]{1,0:T(8,128)(2,1)}, f32[1024,1024]{1,0:T(8,128)}, bf...) custom-call(bf16[1024,1024]{1,0:T(8,128)(2,1)} %get-tuple-element.72.dact_ref.dact_all_ref, ...), custom_call_target="tpu_custom_call" | custom-call | flops 17448304640 | bytes 62914560 | tf_op jit(solution)/shard_map/mixer_backward/pallas_call | solution.py:353
  331.9 24.2 %ffn_weights.1.two_ref = bf16[4,1024,2048]{2,1,0:T(8,128)(2,1)} custom-call(bf16[1024,1024]{1,0:T(8,128)(2,1)} %get-tuple-element.84.ffn_ref, bf16[1024,1024]{1,0:T(8,128)(2,1)} %get-tuple-element.66.grad_ref, bf16[1024,4096]{1,0:T(8,128)(2,1)} %get-tuple-element.85.upper_ref, bf16[1024,4096]{1,0:T(8,128)(2,1)} %get-tuple-element.86.dup_ref), custom_call_target="tpu_custom_call" | custom-call | flops 17179869184 | bytes 41943040 | tf_op jit(solution)/shard_map/ffn_weights/pallas_call | solution.py:404
  356.0 26.3 %mixer_weights.1 = (bf16[4,1024,2048]{2,1,0:T(8,128)(2,1)}, bf16[1024,128]{1,0:T(8,128)(2,1)}) custom-call(bf16[1024,1024]{1,0:T(8,128)(2,1)} %get-tuple-element.62.xn_ref, bf16[1024,1024]{1,0:T(8,128)(2,1)} %get-tuple-element.63.xp_ref, bf16[1024,2048]{1,0:T(8,128)(2,1)} %get-tuple-element.64.hid_ref, ...), custom_call_target="tpu_custom_call" | custom-call | flops 17179869184 | bytes 41943040 | tf_op jit(solution)/shard_map/mixer_weights/pallas_call | solution.py:379
  382.3 0.0 copy-start.9
  382.3 0.0 copy-start.10
  382.3 0.0 copy-start.11
  382.3 0.0 copy-start.12
  382.3 218.9 %closing.1 = (bf16[1024,2048]{1,0:T(8,128)(2,1)}, bf16[1024,2048]{1,0:T(8,128)(2,1)}, bf16[4096,256]{1,0:T(8,128)(2,1)}, bf16[4096,256]{1,0:T(8,128)(2,1)}, f32[...) custom-call(bf16[4,1024,2048]{2,1,0:T(8,128)(2,1)} %get-tuple-element.83.one_ref, ...), custom_call_target="tpu_custom_call" | custom-call | tf_op jit(solution)/shard_map/closing/pallas_call | solution.py:1386
  601.3 0.0 copy-start.1
  601.3 1.4 slice_bitcast_fusion
  602.6 1.4 fusion.12
  604.0 0.0 copy-done.9
  604.0 0.0 copy-done.10
  604.0 0.0 copy-done.11
  604.0 0.0 copy-done.12
  604.0 1.4 fusion.5
  605.4 1.8 convert_element_type.26
  607.2 1.3 fusion.10
  608.5 1.6 maximum_convert_fusion
  610.1 0.0 copy-done.1
  610.1 0.0 copy-start
  610.1 1.5 slice_convert_fusion.4
  611.6 2.6 slice_convert_fusion.2
  614.2 0.0 copy-done
  614.2 0.0 copy-start.3
  614.2 4.4 slice_convert_fusion
  618.6 0.0 copy-start.2
  618.6 0.0 copy-done.3
  618.6 1.3 copy.47
  620.0 1.0 copy-done.2
  621.0 1.3 copy.48
  (1 shorter events, 0.0 us)
Async XLA Ops:
  0.7 9.3 %copy-start.7 = (bf16[1024,256]{1,0:T(8,128)(2,1)S(1)}, bf16[1024,256]{1,0:T(8,128)(2,1)}, u32[]{:S(2)}) copy-start(bf16[1024,256]{1,0:T(8,128)(2,1)} %param.34) | copy-start | bytes 1572868
  0.7 8.3 %copy-start.6 = (bf16[1024,512]{1,0:T(8,128)(2,1)S(1)}, bf16[1024,512]{1,0:T(8,128)(2,1)}, u32[]{:S(2)}) copy-start(bf16[1024,512]{1,0:T(8,128)(2,1)} %param.33) | copy-start | bytes 3145732
  4.4 6.4 %copy-start.8 = (bf16[1024,256]{1,0:T(8,128)(2,1)S(1)}, bf16[1024,256]{1,0:T(8,128)(2,1)}, u32[]{:S(2)}) copy-start(bf16[1024,256]{1,0:T(8,128)(2,1)} %param.35) | copy-start | bytes 1572868
  6.5 6.2 copy-start.4
  6.5 6.2 copy-start.5
  382.3 221.7 %copy-start.9 = (f32[256,16]{0,1:T(8,128)S(1)}, f32[256,16]{0,1:T(8,128)}, u32[]{:S(2)}) copy-start(f32[256,16]{0,1:T(8,128)} %param.23) | copy-start | bytes 49156
  382.3 221.7 %copy-start.10 = (f32[256,16]{0,1:T(8,128)S(1)}, f32[256,16]{0,1:T(8,128)}, u32[]{:S(2)}) copy-start(f32[256,16]{0,1:T(8,128)} %param.24) | copy-start | bytes 49156
  382.3 221.7 %copy-start.11 = (f32[256,16]{0,1:T(8,128)S(1)}, f32[256,16]{0,1:T(8,128)}, u32[]{:S(2)}) copy-start(f32[256,16]{0,1:T(8,128)} %param.25) | copy-start | bytes 49156
  382.3 221.7 %copy-start.12 = (f32[256,16]{0,1:T(8,128)S(1)}, f32[256,16]{0,1:T(8,128)}, u32[]{:S(2)}) copy-start(f32[256,16]{0,1:T(8,128)} %param.26) | copy-start | bytes 49156
  601.3 8.8 %copy-start.1 = (bf16[1024,2048]{1,0:T(8,128)(2,1)S(1)}, bf16[1024,2048]{1,0:T(8,128)(2,1)}, u32[]{:S(2)}) copy-start(bf16[1024,2048]{1,0:T(8,128)(2,1)} %get-tuple-element.102) | copy-start | bytes 12582916
  610.1 4.1 copy-start
  614.2 4.4 copy-start.3
  618.6 2.3 copy-start.2

commit v5 on v4

--- a/solution.py
+++ b/solution.py
@@ -69,6 +69,10 @@
 
 
 ROWS_C = 256
+ROWS_E = 128
+LEAD = 8
+LAG = 2
+SPLIT = 2
 
 
 def sigmoid(value):
@@ -193,6 +197,41 @@
     dx_ref[...] = (d_middle - d_update).astype(jnp.bfloat16)
 
 
+def backward_kernel(dp, mp, pack_ref, layer_ref, *refs):
+    ins, outs, refs = refs[:12], refs[12:18], refs[18:]
+    sums_out, layer_out = refs[:2]
+    layer = Swap(mp, layer_ref, layer_out, refs[2:6], back=True)
+    _, total, width = pack_ref.shape
+    plan, refs = reduce_plan(dp, mp, pack_ref, total, width, refs[6:], 0, SPLIT)
+    plan.sums, plan.sums_sem = sums_out, refs[0]
+    index = pl.program_id(0)
+    steps = pl.num_programs(0)
+
+    @pl.when(index == 0)
+    def _():
+        greet(dp, mp)
+        plan.wave(0)
+        layer.start()
+
+    for number in range(1, LEAD):
+
+        @pl.when(index == number)
+        def _(number=number):
+            plan.wave(number)
+            if number == 1:
+                layer.turn()
+
+    mixer_backward_kernel(*ins, *outs)
+
+    @pl.when(index == steps - 1)
+    def _():
+        for number in range(LEAD, plan.waves()):
+            plan.wave(number)
+        layer.receive()
+        layer.close()
+        plan.close()
+
+
 def mixer_backward_kernel(
     dact_ref, dupd_ref, vpre_ref, gpre_ref, att_ref, spre_ref, mix_ref, one_ref, shared_ref,
     qgain_ref, qbias_ref, kgain_ref,
@@ -202,7 +241,7 @@
     narrow = D // mp
     wide = vpre_ref.shape[1] // mp
     base = 2 * (wide + narrow)
-    groups = ROWS_C // GROUP
+    groups = dact_ref.shape[0] // GROUP
     shared_pre = spre_ref[...]
     logistic = sigmoid(shared_pre)
     shared = shared_pre * logistic
@@ -345,27 +384,38 @@
     )(middle, grad, x, act, upd, two, gain)
 
 
-def mixer_backward(d_act, d_upd, vpre, gpre, att, spre, mix, one, shared, qgain, qbias, kgain):
+def mixer_backward(
+    dp, mp, d_act, d_upd, vpre, gpre, att, spre, mix, one, shared, qgain, qbias, kgain, pack, layer
+):
     count = d_act.shape[0]
     units = vpre.shape[1]
     z = shared.shape[1]
     low = jnp.bfloat16
+
+    def part(width):
+        return pl.BlockSpec((ROWS_E, width), lambda i: (i, 0))
+
     return pl.pallas_call(
-        mixer_backward_kernel,
-        grid=(count // ROWS_C,),
-        in_specs=[rows_block(D)] * 2
-        + [rows_block(units)] * 3
-        + [rows_block(z), rows_block(D)]
+        functools.partial(backward_kernel, dp, mp),
+        grid=(count // ROWS_E,),
+        in_specs=[HBM, HBM]
+        + [part(D)] * 2
+        + [part(units)] * 3
+        + [part(z), part(D)]
         + [held(*one.shape), held(*shared.shape)]
         + [held(1, z)] * 3,
-        out_specs=[rows_block(units)] * 2
-        + [rows_block(z), rows_block(D), rows_block(D), whole(8, z)],
+        out_specs=[part(units)] * 2 + [part(z), part(D), part(D), whole(8, z)] + [HBM] * 2,
         out_shape=[sds((count, units), low)] * 2
-        + [sds((count, z), low), sds((count, D)), sds((count, D), low), sds((8, z))],
-        compiler_params=BIG,
-        cost_estimate=cost(2 * count * (one.size + shared.size), 60 << 20),
+        + [sds((count, z), low), sds((count, D)), sds((count, D), low), sds((8, z))]
+        + [sds((mp, 2, pack.shape[1] >> SPLIT, pack.shape[2] // 2), low), sds((count * mp, D // mp), low)],
+        scratch_shapes=swap_scratch(mp, count, D // mp)
+        + reduce_scratch(dp, mp, pack.shape[1], pack.shape[2], 0, SPLIT)
+        + [pltpu.SemaphoreType.DMA((mp, 2))],
+        compiler_params=pltpu.CompilerParams(
+            collective_id=3, has_side_effects=True, vmem_limit_bytes=61 << 20
+        ),
         name="mixer_backward",
-    )(d_act, d_upd, vpre, gpre, att, spre, mix, one, shared, qgain, qbias, kgain)
+    )(pack, layer, d_act, d_upd, vpre, gpre, att, spre, mix, one, shared, qgain, qbias, kgain)
 
 
 def mixer_weights(mp, xn, xp, hidden, d_act, d_value, d_gate, d_upd, d_shared):
@@ -519,8 +569,8 @@
 
 
 class Gather:
-    def __init__(self, dp, mp, src, dst, sems):
-        self.dp, self.mp, self.src, self.dst = dp, mp, src, dst
+    def __init__(self, dp, mp, srcs, dst, sems):
+        self.dp, self.mp, self.srcs, self.dst = dp, mp, srcs, dst
         self.hold, self.line_send, self.pass_send, self.line_recv, self.send, self.recv, self.own = sems
         self.me, self.part = lax.axis_index("dp"), lax.axis_index("mp")
         self.bits = dp.bit_length() - 1
@@ -532,26 +582,54 @@
         first = lax.div(rank_of(index, self.orders[half]), 1 << held) * (share << held)
         return ref.at[pl.ds(pl.multiple_of(half * total + first, share), share << held), :]
 
-    def load(self):
+    def spans(self):
+        first = 0
+        for ref in self.srcs:
+            folded = ref.shape[0] < self.dst.shape[1]
+            width = ref.shape[1] // 2 if folded else ref.shape[1]
+            yield ref, slice(first, first + width), width, folded
+            first += width
+
+    def loads(self):
         there = self.dst.at[self.part] if self.hold is None else self.hold
-        return pltpu.make_async_copy(self.src, there, self.own.at[0])
+        total = self.dst.shape[1] // 2
+        for place, (ref, columns, width, folded) in enumerate(self.spans()):
+            if not folded:
+                yield pltpu.make_async_copy(ref, there.at[:, columns], self.own.at[place])
+                continue
+            for half in range(2):
+                yield pltpu.make_async_copy(
+                    ref.at[:, half * width : (half + 1) * width],
+                    there.at[half * total : (half + 1) * total, columns],
+                    self.own.at[place + half],
+                )
 
     def store(self):
-        return pltpu.make_async_copy(self.hold, self.dst.at[self.part], self.own.at[1])
+        return pltpu.make_async_copy(self.hold, self.dst.at[self.part], self.own.at[7])
 
     def turn(self):
-        self.load().wait()
+        for copy in self.loads():
+            copy.wait()
         if self.hold is not None:
             self.store().start()
 
     def first(self, up):
         to = self.part + 1 if up else self.part - 1
+        total = self.dst.shape[1] // 2
+        share = total // self.dp
         for half in range(2):
-            yield remote(
-                self.region(self.src, half, self.me, 0),
-                self.region(self.dst.at[self.part], half, self.me, 0),
-                self.line_send.at[int(up), half], self.line_recv.at[self.part, half], "mp", to,
-            )
+            first = pl.multiple_of(rank_of(self.me, self.orders[half]) * share, share)
+            whole_rows = pl.ds(pl.multiple_of(half * total + first, share), share)
+            for place, (ref, columns, width, folded) in enumerate(self.spans()):
+                if folded:
+                    piece = ref.at[pl.ds(first, share), half * width : (half + 1) * width]
+                else:
+                    piece = ref.at[whole_rows, :]
+                yield remote(
+                    piece, self.dst.at[self.part].at[whole_rows, columns],
+                    self.line_send.at[place, int(up), half], self.line_recv.at[self.part, half],
+                    "mp", to,
+                )
 
     def passed(self, source):
         to = jnp.where(source < self.part, self.part + 1, self.part - 1)
@@ -590,7 +668,8 @@
                 for copy in self.first(up):
                     copy.start()
 
-        self.load().start()
+        for copy in self.loads():
+            copy.start()
 
     def advance(self, step, stage):
         source = self.source(step)
@@ -653,8 +732,8 @@
     dma = pltpu.SemaphoreType.DMA
     bits = dp.bit_length() - 1
     return [
-        pltpu.VMEM(pack.shape, pack.dtype), dma((2, 2)), dma((mp, 2)), dma((mp, 2)),
-        dma((bits, mp, 2)), dma((bits, mp, 2)), dma((2,)),
+        pltpu.VMEM(pack.shape, pack.dtype), dma((5, 2, 2)), dma((mp, 2)), dma((mp, 2)),
+        dma((bits, mp, 2)), dma((bits, mp, 2)), dma((8,)),
     ]
 
 
@@ -663,7 +742,8 @@
 
 def forward_kernel(
     dp, mp, span,
-    small_ref, first_ref, tok_ref, shared_ref, qgain_ref, qbias_ref, kgain_ref, pack_ref, cot_ref,
+    small_ref, v_ref, g_ref, m_ref, u_ref, o_ref, tok_ref, shared_ref, qgain_ref, qbias_ref, kgain_ref,
+    up_ref, down_ref, cot_ref,
     xn_ref, xp_ref, mix_ref, starts_ref, keep_ref, weight_ref, gains_ref,
     vpre_ref, gpre_ref, att_ref, hid_ref, act_ref, upd_ref, mid_ref, spre_ref,
     one_out, x_out, full_ref, grad_ref,
@@ -674,10 +754,11 @@
     steps = pl.num_programs(0) // 2
     part = lax.axis_index("mp")
     swap = Swap(mp, cot_ref, grad_ref, sems[0:4])
-    plan = Gather(dp, mp, pack_ref, full_ref, sems[4:11])
+    plan = Gather(dp, mp, (up_ref, down_ref), full_ref, sems[4:11])
     tokens = Swap(mp, tok_ref, x_all, sems[11:15])
     tiny = Swap(mp, small_ref, small_all, sems[15:19], back=True)
-    opening = Gather(dp, mp, first_ref, one_ref, (None,) + tuple(sems[19:25]))
+    firsts = (v_ref, g_ref, m_ref, u_ref, o_ref)
+    opening = Gather(dp, mp, firsts, one_ref, (None,) + tuple(sems[19:25]))
     gives = lax.rem(part + 1, span) != 0
     takes = lax.rem(part, span) != 0
     gain_ref, omega_ref = gains_ref.at[0:1, :], gains_ref.at[1:2, :]
@@ -700,9 +781,12 @@
         opening.turn()
         for number in range(opening.waves()):
             opening.wave(number)
-            if number == mp - 2:
+            if number == 0:
                 tokens.start()
-        plan.start()
+            if number == 2:
+                plan.start()
+            if number == 4:
+                swap.start()
         tokens.turn()
         tiny.receive()
         lines = small_all.shape[0] // mp
@@ -817,8 +901,6 @@
         @pl.when(index == jnp.minimum(number + 2, 2 * steps - 1))
         def _(number=number):
             plan.wave(number)
-            if number == 0:
-                swap.start()
 
     @pl.when(index == 2 * steps - 1)
     def _():
@@ -830,7 +912,7 @@
         x_copy().wait()
 
 
-def forward(dp, mp, span, units, small, first, tokens, shared, vectors, pack, cotangent):
+def forward(dp, mp, span, units, small, firsts, tokens, shared, vectors, packs, cotangent):
     count = tokens.shape[0] // mp
     steps = count // ROWS_C
     z = shared.shape[1]
@@ -842,10 +924,12 @@
 
     dma = pltpu.SemaphoreType.DMA
     lines, width = small.shape[0], small.shape[1] // mp
+    first = sds((D, sum(item.size for item in firsts) // D), low)
+    pack = sds((D, sum(item.size for item in packs) // D), low)
     return pl.pallas_call(
         functools.partial(forward_kernel, dp, mp, span),
         grid=(2 * steps,),
-        in_specs=[HBM] * 3 + [held(*shared.shape)] + [held(1, z)] * 3 + [HBM] * 2,
+        in_specs=[HBM] * 7 + [held(*shared.shape)] + [held(1, z)] * 3 + [HBM] * 3,
         out_specs=[early, late(D), late(D), whole(*STATES)]
         + [whole(NDIM * SUB, LANES)] * 2
         + [whole(8, D)]
@@ -876,7 +960,7 @@
             collective_id=1, has_side_effects=True, vmem_limit_bytes=61 << 20
         ),
         name="forward",
-    )(small, first, tokens, shared, *vectors, pack, cotangent)
+    )(small, *firsts, tokens, shared, *vectors, *packs, cotangent)
 
 
 def add_rows(acc, first, other, count):
@@ -892,140 +976,234 @@
     lax.fori_loop(0, count // chunk, step, 0)
 
 
-class Reduce:
-    def __init__(self, dp, mp, src, out, stage, recvs, lines, last, sems, waits):
-        self.dp, self.mp, self.src, self.out, self.stage = dp, mp, src, out, stage
-        self.recvs, self.lines, self.last, self.waits = recvs, lines, last, waits
+class Across:
+    def __init__(self, dp, mp, mine, out, refs, sums=None):
+        self.dp, self.mp, self.mine, self.out, self.sums = dp, mp, mine, out, sums
         (
-            self.load, self.send, self.recv, self.line_send, self.line_recv,
+            self.lines, self.last, self.line_send, self.line_recv,
             self.last_send, self.last_recv, self.ring_send, self.ring_recv, self.own,
-        ) = sems
+        ) = refs
         self.me, self.part = lax.axis_index("dp"), lax.axis_index("mp")
         self.bits = dp.bit_length() - 1
         self.orders = orders_of(dp)
-        self.share = src.shape[1] // dp
-        self.width = src.shape[2] // 2
+        if sums is None:
+            self.share = out.shape[0] // dp
+            self.width = out.shape[1] // 2
+        else:
+            self.share, self.width = sums.shape[1], sums.shape[2]
 
     def shard(self, i):
         near, far = flip(self.part, 0), flip(self.part, 1)
-        return (near, flip(far, 0), far, self.part)[i]
-
-    def rank(self, half, index):
-        return rank_of(index, self.orders[half])
-
-    def push(self, copy):
-        copy.start()
-        self.waits.append(copy.wait_send)
-
-    def begin(self, i, slot):
-        m = self.shard(i)
-        count = self.share << (self.bits - 1)
-        for half in range(2):
-            columns = slice(half * self.width, (half + 1) * self.width)
-            other = flip(self.me, self.orders[half][self.bits - 1])
-
-            def rows(index):
-                return span_of(lax.div(self.rank(half, index), 1 << (self.bits - 1)), count)
-
-            self.push(
-                remote(
-                    self.src.at[m, rows(other), columns], self.recvs[0].at[m, half],
-                    self.send.at[0, i, half], self.recv.at[0, m, half], "dp", other,
-                )
+        return (flip(far, 0), far, near, self.part)[i]
+
+    def kept(self, half, src=None):
+        src = self.mine(self.mp - 1, half) if src is None else src
+        dst = self.rows_at(half, self.me, 0) if self.sums is None else self.sums.at[half]
+        return pltpu.make_async_copy(src, dst, self.own.at[half])
+
+    def across(self, i, half):
+        if i % 2 == 0:
+            return remote(
+                self.mine(i, half), self.lines.at[self.shard(i), half],
+                self.line_send.at[i // 2, half], self.line_recv.at[self.shard(i), half],
+                "mp", flip(self.part, 0),
             )
-            pltpu.make_async_copy(
-                self.src.at[m, rows(self.me), columns], self.stage.at[slot, half],
-                self.load.at[slot, half],
-            ).start()
-
-    def offset(self, half, index, stage):
-        low = lax.rem(self.rank(half, index), 1 << (self.bits - 1))
-        left = self.bits - 1 - stage
-        return lax.div(low, 1 << left) * (self.share << left)
-
-    def fold(self, i, stage, slot):
-        m = self.shard(i)
-        count = self.share << (self.bits - 1 - stage)
-        for half in range(2):
-            acc = self.recvs[0].at[m, half]
-            came = self.recvs[stage].at[m, half]
-            arrived(came, self.recv.at[stage, m, half])
-            if stage == 0:
-                own = self.stage.at[slot, half]
-                arrived(own, self.load.at[slot, half])
-                add_rows(acc, 0, own, count)
-            else:
-                add_rows(acc, self.offset(half, self.me, stage), came, count)
-            if stage < self.bits - 1:
-                other = flip(self.me, self.orders[half][self.bits - 2 - stage])
-                give = self.offset(half, other, stage + 1)
-                self.push(
-                    remote(
-                        acc.at[pl.ds(pl.multiple_of(give, self.share), count // 2), :],
-                        self.recvs[stage + 1].at[m, half],
-                        self.send.at[stage + 1, i, half], self.recv.at[stage + 1, m, half],
-                        "dp", other,
-                    )
-                )
-                continue
-            first = self.offset(half, self.me, stage)
-            mine = acc.at[pl.ds(pl.multiple_of(first, self.share), self.share), :]
-            if i >= 2:
-                came = self.lines.at[m, half]
-                arrived(came, self.line_recv.at[m, half])
-                add_rows(acc, first, came, self.share)
-            if i < 2:
-                self.push(
-                    remote(
-                        mine, self.lines.at[m, half],
-                        self.line_send.at[i, half], self.line_recv.at[m, half],
-                        "mp", flip(self.part, 0),
-                    )
-                )
-            elif i == 2:
-                self.push(
-                    remote(
-                        mine, self.last.at[half], self.last_send.at[half], self.last_recv.at[half],
-                        "mp", flip(self.part, 1),
-                    )
-                )
-            else:
-                came = self.last.at[half]
-                arrived(came, self.last_recv.at[half])
-                add_rows(acc, first, came, self.share)
-                pltpu.make_async_copy(mine, self.rows_at(half, self.me, 0), self.own.at[half]).start()
+        return remote(
+            self.mine(i, half), self.last.at[half],
+            self.last_send.at[half], self.last_recv.at[half], "mp", flip(self.part, 1),
+        )
+
+    def ring(self, half, stage):
+        rows = self.rows_at(half, self.me, stage)
+        return remote(
+            rows, rows, self.ring_send.at[stage, half], self.ring_recv.at[stage, half],
+            "dp", flip(self.me, self.orders[half][stage]),
+        )
 
     def rows_at(self, half, index, stage):
-        first = lax.div(self.rank(half, index), 1 << stage) * (self.share << stage)
+        rank = rank_of(index, self.orders[half])
+        first = lax.div(rank, 1 << stage) * (self.share << stage)
         return self.out.at[
             pl.ds(pl.multiple_of(first, self.share), self.share << stage),
             half * self.width : (half + 1) * self.width,
         ]
 
+    def fold(self, i):
+        for half in range(2):
+            mine = self.mine(i, half)
+            if i % 2:
+                came = self.lines.at[self.shard(i), half]
+                arrived(came, self.line_recv.at[self.shard(i), half])
+                add_rows(mine, 0, came, self.share)
+            if i < self.mp - 1:
+                self.across(i, half).start()
+            else:
+                came = self.last.at[half]
+                arrived(came, self.last_recv.at[half])
+                add_rows(mine, 0, came, self.share)
+                self.kept(half).start()
+
     def spread(self, stage):
         for half in range(2):
-            mine = self.rows_at(half, self.me, stage)
             if stage == 0:
-                arrived(mine, self.own.at[half])
+                arrived(self.rows_at(half, self.me, 0), self.own.at[half])
             else:
                 other = flip(self.me, self.orders[half][stage - 1])
                 arrived(self.rows_at(half, other, stage - 1), self.ring_recv.at[stage - 1, half])
             if stage < self.bits:
-                self.push(
-                    remote(
-                        mine, mine, self.ring_send.at[stage, half], self.ring_recv.at[stage, half],
-                        "dp", flip(self.me, self.orders[half][stage]),
-                    )
-                )
-
-
-def reduce_sems(dp, mp):
+                self.ring(half, stage).start()
+
+    def close(self, summed=True):
+        for half in range(2):
+            for i in range(self.mp - 1):
+                if summed:
+                    self.across(i, half).wait_send()
+            if self.sums is not None:
+                self.kept(half).wait()
+                continue
+            for stage in range(self.bits):
+                self.ring(half, stage).wait_send()
+
+
+class Reduce:
+    def __init__(self, dp, mp, src, share, width, stage, load, recvs, send, recv, first, stop):
+        self.dp, self.mp, self.src, self.stage, self.load = dp, mp, src, stage, load
+        self.share, self.width, self.first, self.stop = share, width, first, stop
+        self.recvs, self.send, self.recv = recvs, send, recv
+        self.acc = recvs[0] if first == 0 else stage
+        self.base = max(first, 1)
+        self.tail = self.sums = self.sums_sem = None
+        self.me, self.part = lax.axis_index("dp"), lax.axis_index("mp")
+        self.bits = dp.bit_length() - 1
+        self.orders = orders_of(dp)
+
+    def shard(self, i):
+        near, far = flip(self.part, 0), flip(self.part, 1)
+        return (flip(far, 0), far, near, self.part)[i]
+
+    def rank(self, half, index):
+        return rank_of(index, self.orders[half])
+
+    def top(self, half, index):
+        count = self.share << (self.bits - 1)
+        return span_of(lax.div(self.rank(half, index), 1 << (self.bits - 1)), count)
+
+    def offset(self, half, index, stage):
+        low = lax.rem(self.rank(half, index), 1 << (self.bits - self.base))
+        left = self.bits - 1 - stage
+        return pl.multiple_of(lax.div(low, 1 << left) * (self.share << left), self.share)
+
+    def columns(self, half):
+        return slice(half * self.width, (half + 1) * self.width)
+
+    def rows(self, i, half, index, stage):
+        first = self.offset(half, index, stage)
+        count = self.share << (self.bits - 1 - stage)
+        return self.acc.at[self.shard(i), half].at[pl.ds(first, count), :]
+
+    def give(self, i, half, stage):
+        m = self.shard(i)
+        place = stage - self.first
+        other = flip(self.me, self.orders[half][self.bits - 1 - stage])
+        if stage == 0:
+            rows = self.src.at[m, self.top(half, other), self.columns(half)]
+        else:
+            rows = self.rows(i, half, other, stage)
+        return remote(
+            rows, self.recvs[place].at[m, half],
+            self.send.at[place, i, half], self.recv.at[place, m, half], "dp", other,
+        )
+
+    def mine(self, i, half):
+        return self.rows(i, half, self.me, self.bits - 1)
+
+    def saved(self, i, half):
+        return pltpu.make_async_copy(
+            self.rows(i, half, self.me, self.stop - 1),
+            self.sums.at[self.shard(i), half],
+            self.sums_sem.at[i, half],
+        )
+
+    def begin(self, i):
+        for half in range(2):
+            self.give(i, half, self.first).start()
+            if self.first == 0:
+                pltpu.make_async_copy(
+                    self.src.at[self.shard(i), self.top(half, self.me), self.columns(half)],
+                    self.stage.at[i, half], self.load.at[i, half],
+                ).start()
+
+    def fold(self, i, stage):
+        m = self.shard(i)
+        place = stage - self.first
+        count = self.share << (self.bits - 1 - stage)
+        for half in range(2):
+            acc = self.acc.at[m, half]
+            came = self.recvs[place].at[m, half]
+            arrived(came, self.recv.at[place, m, half])
+            if stage == 0:
+                own = self.stage.at[i, half]
+                arrived(own, self.load.at[i, half])
+                add_rows(acc, 0, own, count)
+            else:
+                add_rows(acc, self.offset(half, self.me, stage), came, count)
+            if stage < self.stop - 1:
+                self.give(i, half, stage + 1).start()
+            elif self.sums is not None:
+                self.saved(i, half).start()
+        if stage == self.bits - 1:
+            self.tail.fold(i)
+
+    def waves(self):
+        return self.mp + LAG * (self.stop - 1) + 1
+
+    def wave(self, number):
+        for stage in range(self.stop):
+            i = number - 1 - LAG * stage
+            if 0 <= i < self.mp:
+                self.fold(i, stage)
+        if number == 0:
+            for i in range(self.mp):
+                self.begin(i)
+
+    def close(self):
+        for half in range(2):
+            for i in range(self.mp):
+                for stage in range(self.first, self.stop):
+                    self.give(i, half, stage).wait_send()
+                if self.sums is not None:
+                    self.saved(i, half).wait()
+        if self.tail is not None:
+            self.tail.close()
+
+
+def across_scratch(dp, mp, total, width):
+    low = jnp.bfloat16
     dma = pltpu.SemaphoreType.DMA
     bits = dp.bit_length() - 1
     return [
-        dma((bits, mp, 2)), dma((bits, mp, 2)), dma((2, 2)), dma((mp, 2)),
-        dma((2,)), dma((2,)), dma((bits, 2)), dma((bits, 2)), dma((2,)),
+        pltpu.VMEM((mp, 2, total // dp, width // 2), low), pltpu.VMEM((2, total // dp, width // 2), low),
+        dma((2, 2)), dma((mp, 2)), dma((2,)), dma((2,)), dma((bits, 2)), dma((bits, 2)), dma((2,)),
     ]
+
+
+def reduce_scratch(dp, mp, total, width, first, stop):
+    low = jnp.bfloat16
+    dma = pltpu.SemaphoreType.DMA
+    half = width // 2
+    held = total // 2 if first == 0 else total >> first
+    stages = [pltpu.VMEM((mp, 2, held, half), low), dma((mp, 2))]
+    stages += [pltpu.VMEM((mp, 2, total >> (i + 1), half), low) for i in range(first, stop)]
+    return stages + [dma((stop - first, mp, 2)), dma((stop - first, mp, 2))]
+
+
+def reduce_plan(dp, mp, src, total, width, refs, first, stop):
+    count = stop - first
+    plan = Reduce(
+        dp, mp, src, total // dp, width // 2, refs[0], refs[1], refs[2 : 2 + count],
+        refs[2 + count], refs[3 + count], first, stop,
+    )
+    return plan, refs[4 + count :]
 
 
 class Tiny:
@@ -1078,42 +1256,38 @@
 
 
 FEATURES = 40
-LAG = 2
 
 
 def closing_kernel(
     dp, mp, span,
-    one_ref, two_ref, layer_ref, grad_ref, xn_ref, x_ref, normed_ref, direct_ref, shared_ref, vector_ref,
+    one_ref, two_ref, grad_ref, xn_ref, x_ref, normed_ref, direct_ref, shared_ref, vector_ref,
     keep_ref, weight_ref, gain_ref, omega_ref, ffn_ref, starts_ref,
-    one_out, two_out, layer_out, token_out, feat_out, shared_out, vector_out,
-    stage, *refs,
+    one_out, two_out, token_out, feat_out, shared_out, vector_out,
+    *refs,
 ):
     bits = dp.bit_length() - 1
     me, part = lax.axis_index("dp"), lax.axis_index("mp")
     waits = []
     taken = 0
+    _, total, width = one_ref.shape
+    pack, refs = reduce_plan(dp, mp, one_ref, total, width, refs, 0, bits)
+    pack.tail = Across(dp, mp, pack.mine, one_out, refs[:9])
+    other, refs = reduce_plan(dp, mp, None, total, width, refs[9:], SPLIT, bits)
+    other.tail = Across(dp, mp, other.mine, two_out, refs[:9])
+    refs = refs[9:]
 
     def take(count):
         nonlocal taken
         taken += count
         return refs[taken - count : taken]
 
-    recvs = [take(bits), take(bits)]
-    lines = take(2)
-    last = take(2)
     grad, xn, x, normed_part, direct, tokens, rows, outs, states, ahead, sums, feat = take(12)
     shared, shared_line, shared_ring, shared_came, shared_low = take(5)
     feat_line, feat_ring, feat_came = take(3)
     vector, vector_line, vector_ring, vector_came = take(4)
-    (load_sem,) = take(1)
     (in_sem,) = take(1)
     carry_send, carry_recv = take(2)
     spread_send, spread_recv, spread_own = take(3)
-    packs = [
-        Reduce(dp, mp, src, out, stage, recvs[i], lines[i], last[i], (load_sem,) + take(9), waits)
-        for i, (src, out) in enumerate(((two_ref, two_out), (one_ref, one_out)))
-    ]
-    layer = Swap(mp, layer_ref, layer_out, take(4), back=True)
     token = Swap(mp, tokens, token_out, take(4), back=True)
     quarter = shared.shape[0] // mp
     columns = feat.shape[1] // mp
@@ -1300,64 +1474,80 @@
     greet(dp, mp)
     for copy in loads:
         copy.start()
-    layer.start()
-    work = {
-        0: [adjoint],
-        1: [lambda: params(0, blocks // 2)],
-        2: [lambda: params(blocks // 2, blocks)],
-        3: [meet, lambda: token_rows(0, blocks // 2)],
-        4: [lambda: token_rows(blocks // 2, blocks), gathered],
-    }
-    jobs = [(pack, i) for pack in packs for i in range(mp)]
-    finals = {}
-    lags = [1 + LAG * stage_number for stage_number in range(bits)]
-    for wave in range(len(jobs) + lags[-1] + bits + 2):
-        for stage_number in range(bits):
-            number = wave - lags[stage_number]
-            if 0 <= number < len(jobs):
-                pack, i = jobs[number]
-                pack.fold(i, stage_number, number % 2)
-                if stage_number == bits - 1 and i == mp - 1:
-                    for step in range(bits + 1):
-                        finals.setdefault(wave + step, []).append((pack, step))
-        if wave < len(jobs):
-            jobs[wave][0].begin(jobs[wave][1], wave % 2)
-        for pack, step in finals.get(wave, []):
-            pack.spread(step)
-        for item in work.get(wave, []):
-            item()
-        if wave == 1:
-            layer.turn()
-            loads[5].wait()
-            loads[6].wait()
-            tiny_shared.start()
-            tiny_vector.start()
-        for item, first in ((tiny_shared, 3), (tiny_vector, 3), (tiny_feat, 7)):
-            if 0 <= wave - first <= bits:
-                item.fold(wave - first)
-        if wave == 3 + bits:
-            shared_back()
-            vector_out[...] = vector_ring[bits]
-        if wave == 7 + bits:
-            feat_out[...] = feat_ring[bits]
+    def parts():
+        return pltpu.make_async_copy(two_ref, other.stage, other.load.at[0, 0])
+
+    def sums_ready():
+        parts().wait()
+        for i in range(mp):
+            other.begin(i)
+
+    def tiny_ready():
+        loads[5].wait()
+        loads[6].wait()
+        tiny_shared.start()
+        tiny_vector.start()
+
+    def vector_ready():
+        shared_back()
+        vector_out[...] = vector_ring[bits]
+
+    def feat_ready():
+        feat_out[...] = feat_ring[bits]
+
+    parts().start()
+    for i in range(mp):
+        pack.begin(i)
+    pace = max(blocks // 4, 1)
+    late = [
+        lambda i=i, stage=stage: other.fold(i, stage)
+        for stage in range(SPLIT, bits)
+        for i in range(mp)
+    ]
+    work = [sums_ready, adjoint, lambda: pack.fold(0, 0), lambda: params(0, pace)]
+    work += [lambda: pack.fold(1, 0), late[0], tiny_ready, lambda: params(pace, 2 * pace)]
+    work += [lambda: pack.fold(2, 0), lambda: pack.fold(3, 0), late[1], lambda: params(2 * pace, 3 * pace)]
+    work += [late[2], lambda: pack.fold(0, 1), lambda: params(3 * pace, blocks)]
+    work += [meet, lambda: pack.fold(1, 1), lambda: token_rows(0, blocks // 2)]
+    work += [lambda: pack.fold(2, 1), lambda: token_rows(blocks // 2, blocks), gathered]
+    work += [lambda: pack.fold(3, 1)] + late[3:] + [lambda: other.tail.spread(0)]
+    for stage in range(2, bits):
+        for i in range(mp):
+            work.append(lambda i=i, stage=stage: pack.fold(i, stage))
+            if stage == 2 and i < 3:
+                work.append(lambda i=i: other.tail.spread(1 + i))
+            if stage == 2 and i <= bits:
+                work.append(lambda i=i: tiny_shared.fold(i))
+                work.append(lambda i=i: tiny_vector.fold(i))
+    for i in range(mp, bits + 1):
+        work.append(lambda i=i: other.tail.spread(i))
+        work.append(lambda i=i: tiny_shared.fold(i))
+        work.append(lambda i=i: tiny_vector.fold(i))
+    work.append(vector_ready)
+    for step in range(bits + 1):
+        work.append(lambda step=step: pack.tail.spread(step))
+        work.append(lambda step=step: tiny_feat.fold(step))
+    work.append(feat_ready)
+    for item in work:
+        item()
     arrived(shared_low, spread_own.at[0])
     for step in range(1, mp):
         source = lax.rem(part + step, mp)
         arrived(shared_out.at[span_of(source, quarter), :], spread_recv.at[source])
     token.turn()
-    for item in (layer, token):
-        item.receive()
-        item.close()
+    token.receive()
+    token.close()
+    pack.close()
+    other.close()
     for wait in waits:
         wait()
 
 
-def closing(dp, mp, span, packs, layer_rows, inputs, shared, vector, params, starts):
-    one, two = packs
+def closing(dp, mp, span, one, two, inputs, shared, vector, params, starts):
     low, full = jnp.bfloat16, jnp.float32
     bits = dp.bit_length() - 1
     dma = pltpu.SemaphoreType.DMA
-    count = layer_rows.shape[0]
+    count = inputs[0].shape[0]
     _, total, width = one.shape
     z = shared.shape[1]
     quarter, columns = D // mp, D // mp
@@ -1365,11 +1555,8 @@
     def vmem(*shape, dtype=full):
         return pltpu.VMEM(shape, dtype)
 
-    scratch = [vmem(2, 2, total // 2, width // 2, dtype=low)]
-    for _ in range(2):
-        scratch += [vmem(mp, 2, total >> (i + 1), width // 2, dtype=low) for i in range(bits)]
-    scratch += [vmem(mp, 2, total // dp, width // 2, dtype=low)] * 2
-    scratch += [vmem(2, total // dp, width // 2, dtype=low)] * 2
+    scratch = reduce_scratch(dp, mp, total, width, 0, bits) + across_scratch(dp, mp, total, width)
+    scratch += reduce_scratch(dp, mp, total, width, SPLIT, bits) + across_scratch(dp, mp, total, width)
     scratch += [vmem(count, D)] + [vmem(count, D, dtype=low)] * 5
     scratch += [ROWS, ROWS, pltpu.VMEM(STATES, full), vmem(NDIM * SUB, LANES)]
     scratch += [vmem(2 * NDIM * SUB, LANES), vmem(FEATURES, D)]
@@ -1379,17 +1566,16 @@
     ]
     scratch += [vmem(mp, FEATURES, columns), vmem(bits + 1, FEATURES, columns), vmem(bits, FEATURES, columns)]
     scratch += [vmem(8, z), vmem(mp, 8, z), vmem(bits + 1, 8, z), vmem(bits, 8, z)]
-    scratch += [dma((2, 2)), dma((7,)), dma((1,)), dma((1,)), dma((mp,)), dma((mp,)), dma((1,))]
-    scratch += reduce_sems(dp, mp) * 2 + swap_scratch(mp, count, D // mp) * 2 + tiny_sems(dp, mp) * 3
+    scratch += [dma((7,)), dma((1,)), dma((1,)), dma((mp,)), dma((mp,)), dma((1,))]
+    scratch += swap_scratch(mp, count, D // mp) + tiny_sems(dp, mp) * 3
     scratch += [ROWS]
     near = pl.BlockSpec(memory_space=pltpu.VMEM)
     return pl.pallas_call(
         functools.partial(closing_kernel, dp, mp, span),
-        in_specs=[HBM] * 10 + [near] * 6,
-        out_specs=[HBM] * 4 + [near, HBM, near],
+        in_specs=[HBM] * 9 + [near] * 6,
+        out_specs=[HBM] * 3 + [near, HBM, near],
         out_shape=[
-            sds((total, width), low), sds((total, width), low),
-            sds((count * mp, D // mp), low), sds((count * mp, D // mp), low),
+            sds((total, width), low), sds((total, width), low), sds((count * mp, D // mp), low),
             sds((FEATURES, columns)), sds((D, z), low), sds((8, z)),
         ],
         scratch_shapes=scratch,
@@ -1397,7 +1583,7 @@
             collective_id=2, has_side_effects=True, vmem_limit_bytes=61 << 20
         ),
         name="closing",
-    )(one, two, layer_rows, *inputs, shared, vector, *params, starts)
+    )(one, two, *inputs, shared, vector, *params, starts)
 
 
 def local(
@@ -1436,17 +1622,15 @@
     ).T
     lines = small.shape[0]
     small = jnp.pad(small, ((0, -lines % 8), (0, 0)))
-    folded = jnp.concatenate([output_proj[:, : D // 2], output_proj[:, D // 2 :]], axis=0)
-    pack_one = jnp.concatenate([value_proj, gate_proj, mixer_proj, update_proj, folded], axis=1)
-    pack_two = jnp.concatenate([up_proj, down_proj], axis=1)
+    firsts = (value_proj, gate_proj, mixer_proj, update_proj, output_proj)
     vectors = (query_gain[None], query_bias[None], key_gain[None])
     wide, narrow = value_proj.shape[1], mixer_proj.shape[1]
     (
         xn, xp, mix_pre, starts, keep, weight, gains,
         vpre, gpre, att, hidden, act_pre, upd_pre, middle, spre, one, x_low, two, grad_out,
     ) = forward(
-        dp, mp, span, mp * wide, jnp.tile(small, (1, mp)), pack_one, tokens, shared_proj, vectors,
-        pack_two, cotangent,
+        dp, mp, span, mp * wide, jnp.tile(small, (1, mp)), firsts, tokens, shared_proj, vectors,
+        (up_proj, down_proj), cotangent,
     )
     keep, weight = keep.reshape(STATE), weight.reshape(STATE)
     gain, omega, gain_two = gains[0:1], gains[1:2], gains[2:3]
@@ -1454,15 +1638,18 @@
         middle, grad_out, x_low, act_pre, upd_pre, two, gain_two
     )
     two_grad = ffn_weights(mp, ffn_in, grad_out, upper, d_up)
-    d_value, d_gate, d_shared, d_mix_pre, normed_part, vector_sums = mixer_backward(
-        d_act, d_upd, vpre, gpre, att, spre, mix_pre, one, shared_proj, *vectors
+    (
+        d_value, d_gate, d_shared, d_mix_pre, normed_part, vector_sums, two_sums, layer_out,
+    ) = mixer_backward(
+        dp, mp, d_act, d_upd, vpre, gpre, att, spre, mix_pre, one, shared_proj, *vectors,
+        two_grad, layer_rows,
     )
     one_grad, shared_part = mixer_weights(
         mp, xn, xp, hidden, d_act, d_value, d_gate, d_upd, d_shared
     )
 
-    one_grad, two_grad, layer_out, token_grad, feature, shared_grad, vector_sums = closing(
-        dp, mp, span, (one_grad, two_grad), layer_rows,
+    one_grad, two_grad, token_grad, feature, shared_grad, vector_sums = closing(
+        dp, mp, span, one_grad, two_sums,
         (d_mix_pre, xn, x_low, normed_part, d_inputs), shared_part, vector_sums,
         (keep, weight, gain, omega, ffn_part), starts,
     )

time: 632 us -> 592 us (0.937)
  Pallas kernels: 585 us -> 555 us
    pallas_call x1, Pallas kernels: 219 us -> 173 us  [closing(): pl.pallas_call(functools.partial(closing_kernel, dp, mp, span), in_specs=...]
    pallas_call x1, Pallas kernels: 36.6 us -> 74.7 us  [mixer_backward(): pl.pallas_call(functools.partial(backward_kernel, dp, mp), grid=(count //...]
    pallas_call x1, Pallas kernels: 222 us -> 200 us  [forward(): pl.pallas_call(functools.partial(forward_kernel, dp, mp, span), grid=(2 *...]
where the time goes in v5:
time: 592 us; the launch traced here: 584 us
  Pallas kernels  555 us (94%)
  local copies, waits for them, and re-layouts  14.7 us (2%)
  other arithmetic  13.4 us (2%)
    pallas_call x1, Pallas kernels, forward(): pl.pallas_call(functools.partial(forward_kernel, dp, mp, span), grid=(2 *...  200 us
    pallas_call x1, Pallas kernels, closing(): pl.pallas_call(functools.partial(closing_kernel, dp, mp, span), in_specs=...  173 us
    pallas_call x1, Pallas kernels, mixer_backward(): pl.pallas_call(functools.partial(backward_kernel, dp, mp), grid=(count //...  74.7 us
    pallas_call x1, Pallas kernels, ffn(): pl.pallas_call(ffn_kernel, grid=(count // ROWS_C,), in_specs=[rows_block(...  57 us
    pallas_call x1, Pallas kernels, mixer_weights(): pl.pallas_call(mixer_weights_kernel, grid=(mp,), in_specs=[held(count, D)...  26.2 us
    pallas_call x1, Pallas kernels, ffn_weights(): pl.pallas_call(ffn_weights_kernel, grid=(mp,), in_specs=[held(count, D),...  24.4 us

profile of v5, /device:TPU:0, one launch (start us, length us, event | category | flops | bytes accessed | tf_op | source)
XLA Modules:
  0.0 584.3 jit_solution(11869994204052871970)
XLA Ops:
  0.7 3.6 concatenate.6
  4.3 0.1 tile.4
  4.3 0.8 copy.40
  5.1 199.6 %forward.1 = (bf16[1024,1024]{1,0:T(8,128)(2,1)}, bf16[1024,1024]{1,0:T(8,128)(2,1)}, f32[1024,1024]{1,0:T(8,128)}, f32[32,8,128]{2,1,0:T(8,128)}, f32[128,128]{...) custom-call(f32[72,1024]{1,0:T(8,128)} %bitcast.92, ...), custom_call_target="tpu_custom_call" | custom-call | tf_op jit(solution)/shard_map/forward/pallas_call | solution.py:929
  204.7 1.5 fusion.12
  206.2 57.0 %ffn.1 = (bf16[1024,1024]{1,0:T(8,128)(2,1)}, bf16[1024,1024]{1,0:T(8,128)(2,1)}, bf16[1024,4096]{1,0:T(8,128)(2,1)}, bf16[1024,4096]{1,0:T(8,128)(2,1)}, bf16[1...) custom-call(f32[1024,1024]{1,0:T(8,128)} %get-tuple-element.63.mid_ref, ...), custom_call_target="tpu_custom_call" | custom-call | flops 34359738368 | bytes 62914560 | tf_op jit(solution)/shard_map/ffn/pallas_call | solution.py:372
  263.1 24.4 %ffn_weights.1.pack_ref = bf16[4,1024,2048]{2,1,0:T(8,128)(2,1)} custom-call(bf16[1024,1024]{1,0:T(8,128)(2,1)} %get-tuple-element.70.ffn_ref, bf16[1024,1024]{1,0:T(8,128)(2,1)} %get-tuple-element.64.grad_ref, bf16[1024,4096]{1,0:T(8,128)(2,1)} %get-tuple-element.71.upper_ref, bf16[1024,4096]{1,0:T(8,128)(2,1)} %get-tuple-element.72.dup_ref), custom_call_target="tpu_custom_call" | custom-call | flops 17179869184 | bytes 41943040 | tf_op jit(solution)/shard_map/ffn_weights/pallas_call | solution.py:454
  287.5 74.7 %mixer_backward.1 = (bf16[1024,2048]{1,0:T(8,128)(2,1)}, bf16[1024,2048]{1,0:T(8,128)(2,1)}, bf16[1024,128]{1,0:T(8,128)(2,1)}, f32[1024,1024]{1,0:T(8,128)}, bf...) custom-call(bf16[4,1024,2048]{2,1,0:T(8,128)(2,1)} %ffn_weights.1.pa, ...), custom_call_target="tpu_custom_call" | custom-call | tf_op jit(solution)/shard_map/mixer_backward/pallas_call | solution.py:398
  362.2 26.2 %mixer_weights.1 = (bf16[4,1024,2048]{2,1,0:T(8,128)(2,1)}, bf16[1024,128]{1,0:T(8,128)(2,1)}) custom-call(bf16[1024,1024]{1,0:T(8,128)(2,1)} %get-tuple-element.83.xn_ref, bf16[1024,1024]{1,0:T(8,128)(2,1)} %get-tuple-element.84.xp_ref, bf16[1024,2048]{1,0:T(8,128)(2,1)} %get-tuple-element.85.hid_ref, ...), custom_call_target="tpu_custom_call" | custom-call | flops 17179869184 | bytes 41943040 | tf_op jit(solution)/shard_map/mixer_weights/pallas_call | solution.py:429
  388.5 0.0 copy-start.4
  388.5 0.0 copy-start.5
  388.5 0.0 copy-start.6
  388.5 0.0 copy-start.7
  388.5 173.0 %closing.1 = (bf16[1024,2048]{1,0:T(8,128)(2,1)}, bf16[1024,2048]{1,0:T(8,128)(2,1)}, bf16[4096,256]{1,0:T(8,128)(2,1)}, f32[40,256]{1,0:T(8,128)}, bf16[1024,128]{1,0:T(8,128)(2,1)}, /*index=5*/f32[8,128]{1,0:T(8,128)}) custom-call(bf16[4,1024,2048]{2,1,0:T(8,128)(2,1)} %get-tuple-element.89.one_ref, bf16[4,2,256,1024]{3,2,1,0:T(8,128)(2,1)} %get-tuple-element.90.two_ref, ...), custom_call_target="tpu_custom_call" | custom-call | tf_op jit(solution)/shard_map/closing/pallas_call | solution.py:1573
  561.6 1.3 slice_bitcast_fusion
  562.9 1.4 fusion.11
  564.3 0.0 copy-done.4
  564.3 0.0 copy-done.5
  564.3 0.0 copy-done.6
  564.3 0.0 copy-done.7
  564.3 1.4 fusion.5
  565.7 1.8 convert_element_type.26
  567.5 0.0 copy-start.1
  567.5 1.4 fusion.10
  568.9 1.6 maximum_convert_fusion
  570.5 0.0 copy-done.1
  570.5 1.5 slice_convert_fusion.4
  572.0 0.0 copy-start
  572.0 2.7 slice_convert_fusion.2
  574.8 1.0 copy-done
  575.7 0.0 copy-start.2
  575.7 4.4 slice_convert_fusion
  580.2 0.0 copy-done.2
  580.2 0.0 copy-start.3
  580.2 1.3 copy.43
  581.5 1.0 copy-done.3
  582.5 1.3 copy.44
  (1 shorter events, 0.0 us)
Async XLA Ops:
  388.5 175.8 %copy-start.4 = (f32[256,16]{0,1:T(8,128)S(1)}, f32[256,16]{0,1:T(8,128)}, u32[]{:S(2)}) copy-start(f32[256,16]{0,1:T(8,128)} %param.23) | copy-start | bytes 49156
  388.5 175.8 %copy-start.5 = (f32[256,16]{0,1:T(8,128)S(1)}, f32[256,16]{0,1:T(8,128)}, u32[]{:S(2)}) copy-start(f32[256,16]{0,1:T(8,128)} %param.24) | copy-start | bytes 49156
  388.5 175.8 %copy-start.6 = (f32[256,16]{0,1:T(8,128)S(1)}, f32[256,16]{0,1:T(8,128)}, u32[]{:S(2)}) copy-start(f32[256,16]{0,1:T(8,128)} %param.25) | copy-start | bytes 49156
  388.5 175.8 %copy-start.7 = (f32[256,16]{0,1:T(8,128)S(1)}, f32[256,16]{0,1:T(8,128)}, u32[]{:S(2)}) copy-start(f32[256,16]{0,1:T(8,128)} %param.26) | copy-start | bytes 49156
  567.5 3.0 copy-start.1
  572.0 3.7 copy-start
  575.7 4.4 copy-start.2
  580.2 2.3 copy-start.3

commit v6 on v5

--- a/solution.py
+++ b/solution.py
@@ -71,7 +71,7 @@
 ROWS_C = 256
 ROWS_E = 128
 LEAD = 8
-LAG = 2
+LAG = 1
 SPLIT = 2
 
 

time: 592 us -> 598 us (1.010)
  Pallas kernels: 555 us -> 561 us
where the time goes in v6:
time: 598 us; the launch traced here: 590 us
  Pallas kernels  561 us (94%)
  local copies, waits for them, and re-layouts  14.7 us (2%)
  other arithmetic  13.4 us (2%)
    pallas_call x1, Pallas kernels, forward(): pl.pallas_call(functools.partial(forward_kernel, dp, mp, span), grid=(2 *...  200 us
    pallas_call x1, Pallas kernels, closing(): pl.pallas_call(functools.partial(closing_kernel, dp, mp, span), in_specs=...  173 us
    pallas_call x1, Pallas kernels, mixer_backward(): pl.pallas_call(functools.partial(backward_kernel, dp, mp), grid=(count //...  80.6 us
    pallas_call x1, Pallas kernels, ffn(): pl.pallas_call(ffn_kernel, grid=(count // ROWS_C,), in_specs=[rows_block(...  57 us
    pallas_call x1, Pallas kernels, mixer_weights(): pl.pallas_call(mixer_weights_kernel, grid=(mp,), in_specs=[held(count, D)...  26.2 us
    pallas_call x1, Pallas kernels, ffn_weights(): pl.pallas_call(ffn_weights_kernel, grid=(mp,), in_specs=[held(count, D),...  24.4 us

profile of v6, /device:TPU:0, one launch (start us, length us, event | category | flops | bytes accessed | tf_op | source)
XLA Modules:
  0.0 590.2 jit_solution(9052111226552224677)
XLA Ops:
  0.7 3.6 concatenate.6
  4.3 0.1 tile.4
  4.3 0.8 copy.40
  5.1 199.6 %forward.1 = (bf16[1024,1024]{1,0:T(8,128)(2,1)}, bf16[1024,1024]{1,0:T(8,128)(2,1)}, f32[1024,1024]{1,0:T(8,128)}, f32[32,8,128]{2,1,0:T(8,128)}, f32[128,128]{...) custom-call(f32[72,1024]{1,0:T(8,128)} %bitcast.92, ...), custom_call_target="tpu_custom_call" | custom-call | tf_op jit(solution)/shard_map/forward/pallas_call | solution.py:929
  204.7 1.5 fusion.12
  206.2 57.0 %ffn.1 = (bf16[1024,1024]{1,0:T(8,128)(2,1)}, bf16[1024,1024]{1,0:T(8,128)(2,1)}, bf16[1024,4096]{1,0:T(8,128)(2,1)}, bf16[1024,4096]{1,0:T(8,128)(2,1)}, bf16[1...) custom-call(f32[1024,1024]{1,0:T(8,128)} %get-tuple-element.63.mid_ref, ...), custom_call_target="tpu_custom_call" | custom-call | flops 34359738368 | bytes 62914560 | tf_op jit(solution)/shard_map/ffn/pallas_call | solution.py:372
  263.1 24.4 %ffn_weights.1.pack_ref = bf16[4,1024,2048]{2,1,0:T(8,128)(2,1)} custom-call(bf16[1024,1024]{1,0:T(8,128)(2,1)} %get-tuple-element.70.ffn_ref, bf16[1024,1024]{1,0:T(8,128)(2,1)} %get-tuple-element.64.grad_ref, bf16[1024,4096]{1,0:T(8,128)(2,1)} %get-tuple-element.71.upper_ref, bf16[1024,4096]{1,0:T(8,128)(2,1)} %get-tuple-element.72.dup_ref), custom_call_target="tpu_custom_call" | custom-call | flops 17179869184 | bytes 41943040 | tf_op jit(solution)/shard_map/ffn_weights/pallas_call | solution.py:454
  287.5 80.6 %mixer_backward.1 = (bf16[1024,2048]{1,0:T(8,128)(2,1)}, bf16[1024,2048]{1,0:T(8,128)(2,1)}, bf16[1024,128]{1,0:T(8,128)(2,1)}, f32[1024,1024]{1,0:T(8,128)}, bf...) custom-call(bf16[4,1024,2048]{2,1,0:T(8,128)(2,1)} %ffn_weights.1.pa, ...), custom_call_target="tpu_custom_call" | custom-call | tf_op jit(solution)/shard_map/mixer_backward/pallas_call | solution.py:398
  368.1 26.2 %mixer_weights.1 = (bf16[4,1024,2048]{2,1,0:T(8,128)(2,1)}, bf16[1024,128]{1,0:T(8,128)(2,1)}) custom-call(bf16[1024,1024]{1,0:T(8,128)(2,1)} %get-tuple-element.83.xn_ref, bf16[1024,1024]{1,0:T(8,128)(2,1)} %get-tuple-element.84.xp_ref, bf16[1024,2048]{1,0:T(8,128)(2,1)} %get-tuple-element.85.hid_ref, ...), custom_call_target="tpu_custom_call" | custom-call | flops 17179869184 | bytes 41943040 | tf_op jit(solution)/shard_map/mixer_weights/pallas_call | solution.py:429
  394.4 0.0 copy-start.4
  394.4 0.0 copy-start.5
  394.4 0.0 copy-start.6
  394.4 0.0 copy-start.7
  394.4 173.0 %closing.1 = (bf16[1024,2048]{1,0:T(8,128)(2,1)}, bf16[1024,2048]{1,0:T(8,128)(2,1)}, bf16[4096,256]{1,0:T(8,128)(2,1)}, f32[40,256]{1,0:T(8,128)}, bf16[1024,128]{1,0:T(8,128)(2,1)}, /*index=5*/f32[8,128]{1,0:T(8,128)}) custom-call(bf16[4,1024,2048]{2,1,0:T(8,128)(2,1)} %get-tuple-element.89.one_ref, bf16[4,2,256,1024]{3,2,1,0:T(8,128)(2,1)} %get-tuple-element.90.two_ref, ...), custom_call_target="tpu_custom_call" | custom-call | tf_op jit(solution)/shard_map/closing/pallas_call | solution.py:1573
  567.5 1.3 slice_bitcast_fusion
  568.8 1.4 fusion.11
  570.2 0.0 copy-done.4
  570.2 0.0 copy-done.5
  570.2 0.0 copy-done.6
  570.2 0.0 copy-done.7
  570.2 1.4 fusion.5
  571.6 1.8 convert_element_type.26
  573.4 0.0 copy-start.1
  573.4 1.4 fusion.10
  574.8 1.6 maximum_convert_fusion
  576.4 0.0 copy-done.1
  576.4 1.5 slice_convert_fusion.4
  577.9 0.0 copy-start
  577.9 2.7 slice_convert_fusion.2
  580.6 1.0 copy-done
  581.6 0.0 copy-start.2
  581.6 4.4 slice_convert_fusion
  586.0 0.0 copy-done.2
  586.0 0.0 copy-start.3
  586.0 1.3 copy.43
  587.4 1.0 copy-done.3
  588.4 1.3 copy.44
  (1 shorter events, 0.0 us)
Async XLA Ops:
  394.4 175.8 %copy-start.4 = (f32[256,16]{0,1:T(8,128)S(1)}, f32[256,16]{0,1:T(8,128)}, u32[]{:S(2)}) copy-start(f32[256,16]{0,1:T(8,128)} %param.23) | copy-start | bytes 49156
  394.4 175.8 %copy-start.5 = (f32[256,16]{0,1:T(8,128)S(1)}, f32[256,16]{0,1:T(8,128)}, u32[]{:S(2)}) copy-start(f32[256,16]{0,1:T(8,128)} %param.24) | copy-start | bytes 49156
  394.4 175.8 %copy-start.6 = (f32[256,16]{0,1:T(8,128)S(1)}, f32[256,16]{0,1:T(8,128)}, u32[]{:S(2)}) copy-start(f32[256,16]{0,1:T(8,128)} %param.25) | copy-start | bytes 49156
  394.4 175.8 %copy-start.7 = (f32[256,16]{0,1:T(8,128)S(1)}, f32[256,16]{0,1:T(8,128)}, u32[]{:S(2)}) copy-start(f32[256,16]{0,1:T(8,128)} %param.26) | copy-start | bytes 49156
  573.4 3.0 copy-start.1
  577.9 3.7 copy-start
  581.6 4.4 copy-start.2
  586.0 2.3 copy-start.3
